TPU v7x, 32 devices: a whole 2x2x4 slice. The times are simulated.
32 devices in a mesh: gx: 4 (over y, core), gy: 8 (over z, x).
Axes of the slice: x: 2, y: 2, z: 4, core: 2. Of those that a mesh axis runs over, the one named last changes fastest.
Arguments:
- macro_state: float32 [4, 512, 512], P(None, 'gx', 'gy'), may hold values from -6 to 6
- face_list: int32 [4, 8, 256], P('gx', 'gy'), may hold values from -1 to 16383
- owner: int32 [4, 8, 256, 1], P('gx', 'gy'), may hold values from 0 to 31; in each aligned block of 256 rows (0 to 255, 256 to 511, ..., all dimensions but the last counted through in order) at most 8 rows name the same one
- face_states: bfloat16 [4, 8, 256, 192, 128], P('gx', 'gy'), may hold values from -6 to 6
- micro_weight: bfloat16 [128, 128], replicated, may hold values from -0.5 to 0.5
- lift_weight: float32 [8, 128], replicated, may hold values from -2 to 2
- readout: float32 [128, 4], replicated, may hold values from -0.5 to 0.5
Outputs:
- macro_next: float32 [4, 512, 512], P(None, 'gx', 'gy')
- micro_states: bfloat16 [4, 8, 32, 8, 192, 128], P('gx', 'gy')
Inputs may be any that keep to these rules, and one draw needn't show every extreme that they name: `owner`: among the 256 slots of one tile, live or empty, no ensemble device is named more than 8 times.
All inputs are finite; a program needn't handle non-finite values.
Results may differ from a plain program's by a relative error of at most 0.007.
Values may be sent and summed in bfloat16 or wider, within the bound.
No kernel may reach another device: no remote copies, remote signals or barrier semaphores. Data moves between devices by JAX's collectives and lax.ppermute only.
A program may use at most 128 MiB of HBM per device.

v0:
```python
import math

import jax
import jax.numpy as jnp
from jax import lax
from jax.sharding import PartitionSpec as P

STEPS = 3


diffusion = 0.2
relax_rate = 0.5
time_step = 0.5


def passed_along(value, axis, steps):
    count = lax.axis_size(axis)
    pairs = [(source, (source + steps) % count) for source in range(count)]
    return lax.ppermute(value, axis, pairs)


def relax_faces(states, inputs, micro_weight, lift_weight, readout):
    leading = states.shape[:-2]
    members = states.shape[-2]
    state_width = states.shape[-1]
    slot_count = math.prod(leading)
    forcing = jnp.dot(inputs[:, :8], lift_weight, precision=lax.Precision.HIGHEST)
    live_mask = inputs[:, 8]
    group_size = math.gcd(slot_count, 32)
    groups = slot_count // group_size

    def advance(block_data):
        block_states, block_force, block_live = block_data
        for repeat in range(STEPS):
            flat_rows = block_states.reshape(group_size * members, state_width)
            activation = jnp.dot(flat_rows, micro_weight, preferred_element_type=jnp.float32)
            activation = activation.reshape(group_size, members, state_width)
            block_states = (
                (1.0 - relax_rate) * block_states.astype(jnp.float32)
                + relax_rate * jnp.tanh(activation + block_force[:, None, :])
            ).astype(jnp.bfloat16)
        block_states = block_states * block_live[:, None, None].astype(jnp.bfloat16)
        ensemble_mean = jnp.sum(block_states, axis=1, dtype=jnp.float32) / members
        face_flux = jnp.dot(ensemble_mean, readout, precision=lax.Precision.HIGHEST)
        return (block_states, face_flux)

    relaxed, face_flux = lax.map(
        advance,
        (
            states.reshape(groups, group_size, members, state_width),
            forcing.reshape(groups, group_size, state_width),
            live_mask.reshape(groups, group_size),
        ),
    )
    return (relaxed.reshape(states.shape), face_flux.reshape(leading + (readout.shape[1],)))


def per_device(macro_state, face_list, owner, face_states, micro_weight, lift_weight, readout):
    channels, tile_rows, tile_cols = macro_state.shape
    slot_total = face_list.shape[2]
    members = face_states.shape[3]
    state_width = face_states.shape[4]
    devices = lax.axis_size("gx") * lax.axis_size("gy")
    capacity = max(2, slot_total // devices)
    next_row = passed_along(macro_state[:, :1, :], "gx", -1)
    next_col = passed_along(macro_state[:, :, :1], "gy", -1)
    extended_rows = jnp.concatenate([macro_state, next_row], axis=1)
    extended_cols = jnp.concatenate([macro_state, next_col], axis=2)
    face_ids = face_list.reshape(slot_total)
    live = face_ids >= 0
    safe_index = jnp.where(live, face_ids, 0)
    direction = safe_index // (tile_rows * tile_cols)
    cell_index = safe_index % (tile_rows * tile_cols)
    row_of = cell_index // tile_cols
    col_of = cell_index % tile_cols
    left_vals = macro_state.reshape(channels, -1)[:, cell_index]
    column_vals = extended_cols.reshape(channels, -1)[:, row_of * (tile_cols + 1) + col_of + 1]
    rowwise_vals = extended_rows.reshape(channels, -1)[:, (row_of + 1) * tile_cols + col_of]
    right_vals = jnp.where(direction[None, :] == 0, column_vals, rowwise_vals)
    inputs = jnp.concatenate([left_vals.T, right_vals.T, live[:, None].astype(jnp.float32)], axis=1)
    destination = owner.reshape(slot_total)
    onehot = (destination[:, None] == jnp.arange(devices, dtype=jnp.int32)).astype(jnp.int32)
    slot_rank = jnp.sum((jnp.cumsum(onehot, axis=0) - onehot) * onehot, axis=-1)
    position = destination * capacity + slot_rank
    buffer_slots = jnp.arange(devices * capacity, dtype=jnp.int32)
    matches = (position[None, :] == buffer_slots[:, None]).astype(jnp.int32)
    found = jnp.sum(matches, axis=1) > 0
    source_slot = jnp.sum(matches * jnp.arange(slot_total, dtype=jnp.int32)[None, :], axis=1)
    source_slot = jnp.where(found, source_slot, slot_total)
    states = face_states.reshape(slot_total, members, state_width)
    relaxed, face_flux = relax_faces(states, inputs, micro_weight, lift_weight, readout)
    picked = jnp.take(relaxed, source_slot, axis=0, mode="fill", fill_value=0)
    micro_out = lax.all_to_all(
        picked.reshape((devices, capacity) + relaxed.shape[1:]),
        ("gx", "gy"),
        split_axis=0,
        concat_axis=0,
        tiled=True,
    )
    east_flux = diffusion * (macro_state - extended_cols[:, :, 1:])
    south_flux = diffusion * (macro_state - extended_rows[:, 1:, :])
    face_total = 2 * tile_rows * tile_cols
    face_values = jnp.stack([east_flux, south_flux], axis=1).reshape(channels, face_total)
    target = jnp.where(live, safe_index, face_total)
    face_values = face_values.at[:, target].set(face_flux.T, mode="drop")
    face_values = face_values.reshape(channels, 2, tile_rows, tile_cols)
    east_flux = face_values[:, 0]
    south_flux = face_values[:, 1]
    west_flux = passed_along(east_flux[:, :, -1:], "gy", 1)
    north_flux = passed_along(south_flux[:, -1:, :], "gx", 1)
    macro_next = macro_state - time_step * (
        east_flux
        - jnp.concatenate([west_flux, east_flux[:, :, :-1]], axis=2)
        + south_flux
        - jnp.concatenate([north_flux, south_flux[:, :-1, :]], axis=1)
    )
    micro_states = micro_out.reshape(1, 1, devices, capacity, members, state_width)
    return (macro_next, micro_states)


def solution(mesh):
    return jax.shard_map(
        per_device,
        mesh=mesh,
        in_specs=(
            P(None, "gx", "gy"),
            P("gx", "gy", None),
            P("gx", "gy", None, None),
            P("gx", "gy", None, None, None),
            P(),
            P(),
            P(),
        ),
        out_specs=(P(None, "gx", "gy"), P("gx", "gy", None, None, None, None)),
        check_vma=False,
    )
```

profile of v0, /device:TPU:20, one launch (start us, length us, event | category | flops | bytes accessed | tf_op | source)
XLA Modules:
  0.0 411.6 jit_solution(7415527831016843450)
XLA Ops:
  9.2 5.3 %copy.38 = f32[4,128,64]{0,2,1:T(8,128)} copy(f32[4,128,64]{1,2,0:T(8,128)} %param.9) | data formatting | bytes 262144 | tf_op args[0]
  14.4 2.9 gather_fusion
  17.5 5.8 %copy.41 = f32[4,129,64]{0,2,1:T(8,128)} copy(f32[4,129,64]{1,2,0:T(8,128)S(1)} %constant_dynamic-update-slice_fusion.1) | data formatting | bytes 264192 | tf_op jit(solution)/shard_map/concatenate | solution.py:67
  23.4 2.9 gather_fusion.2
  26.7 2.9 copy.40
  29.6 2.9 gather_fusion.1
  33.2 48.6 %while.12 = (s32[]{:T(128)}, bf16[8,32,192,128]{3,2,1,0:T(8,128)(2,1)}, f32[8,32,4]{1,2,0:T(4,128)S(1)}, bf16[8,32,192,128]{3,2,1,0:T(8,128)(2,1)}, bf16[128,128...) while((s32[]{:T(128)}, ...), condition=%wide.region_2.3_spmd, body=%wide.region_0.2_spmd.sunk | while | flops 620691456 | bytes 15948009 | solution.py:47
  33.2 2.7 multiply_convert_fusion.5
  36.7 2.1 bitcast_dynamic-update-slice_fusion.2
  39.2 2.7 multiply_convert_fusion.5
  42.8 2.1 bitcast_dynamic-update-slice_fusion.2
  45.3 2.7 multiply_convert_fusion.5
  48.8 2.1 bitcast_dynamic-update-slice_fusion.2
  51.3 2.7 multiply_convert_fusion.5
  57.4 2.7 multiply_convert_fusion.5
  61.0 2.1 bitcast_dynamic-update-slice_fusion.2
  63.5 2.7 multiply_convert_fusion.5
  67.0 2.1 bitcast_dynamic-update-slice_fusion.2
  69.5 2.7 multiply_convert_fusion.5
  73.1 2.1 bitcast_dynamic-update-slice_fusion.2
  75.6 2.7 multiply_convert_fusion.5
  81.7 15.2 %gather_fusion.3 = bf16[256,192,128]{2,1,0:T(8,128)(2,1)} fusion(bf16[256,192,128]{2,1,0:T(8,128)(2,1)} %bitcast.108, s32[1024]{0:T(1024)S(1)} %get-tuple-element.79), kind=kCustom, calls=%fused_computation.3 | custom fusion | bytes 25166848 | tf_op jit(solution)/shard_map/jit(_take)/gather | solution.py:92
  97.0 10.7 %broadcast_select_fusion = bf16[32,8,192,128]{3,2,1,0:T(8,128)(2,1)} fusion(bf16[32,8,192,128]{3,2,1,0:T(8,128)(2,1)} %bitcast.105, pred[32,8]{1,0:T(8,128)(4,1)S(1)} %compare_and_fusion), kind=kLoop, calls=%fused_computation.26 | loop fusion | flops 6291456 | bytes 25166080 | tf_op jit(solution)/shard_map/jit(_take)/select_n | solution.py:92
  107.7 8.0 %all-to-all-start = ((bf16[32,8,192,128]{3,2,1,0:T(8,128)(2,1)}), bf16[32,8,192,128]{3,2,1,0:T(8,128)(2,1)}, u32[]{:S(2)}, u32[]{:S(2)}) async-start(bf16[32,8,192,128]{3,2,1,0:T(8,128)(2,1)} %broadcast_select_fusion), calls=%async_computation | async-start | bytes 25165824 | tf_op jit(solution)/shard_map/all_to_all | solution.py:93
  116.0 7.6 %copy.37 = f32[4,2,128,64]{0,3,2,1:T(8,128)} copy(f32[4,2,128,64]{2,3,0,1:T(8,128)S(1)} %pad_maximum_fusion) | data formatting | bytes 524288 | tf_op jit(solution)/shard_map/stack | solution.py:103
  123.5 7.7 %scatter_fusion = f32[4,16384]{0,1:T(8,128)} fusion(f32[4,16384]{0,1:T(8,128)} %bitcast.106, s32[256]{0:T(256)S(1)} %bitcast.122, f32[256,4]{1,0:T(8,128)S(1)} %bitcast.116), kind=kCustom, calls=%fused_computation.4 | custom fusion | bytes 13312 | tf_op jit(solution)/shard_map/scatter | solution.py:105
  131.2 8.4 %fusion.33 = (f32[4,1,128,64]{0,3,2,1:T(8,128)}, f32[4,1,128,64]{0,3,2,1:T(8,128)}) fusion(f32[4,2,128,64]{0,3,2,1:T(8,128)} %bitcast.107), kind=kLoop, calls=%fused_computation.92 | loop fusion | bytes 524288 | tf_op jit(solution)/shard_map/slice | solution.py:108
  139.6 3.7 copy.51
  144.9 3.7 copy.52
  148.8 36.1 %collective-permute-done.3 = f32[4,1,64]{1,2,0:T(8,128)S(1)} collective-permute-done((f32[4,1,64]{1,2,0:T(8,128)S(1)}, f32[4,1,64]{1,2,0:T(8,128)S(1)}, u32[]{:S(2)}, u32[]{:S(2)}) %collective-permute-start.3) | collective-permute-done | bytes 1056 | tf_op jit(solution)/shard_map/ppermute | solution.py:19
  185.0 214.2 %collective-permute-done.2 = f32[4,128,1]{1,2,0:T(1,128)S(1)} collective-permute-done((f32[4,128,1]{1,2,0:T(1,128)S(1)}, f32[4,128,1]{1,2,0:T(1,128)S(1)}, u32[]{:S(2)}, u32[]{:S(2)}) %collective-permute-start.2) | collective-permute-done | bytes 2080 | tf_op jit(solution)/shard_map/ppermute | solution.py:19
  400.0 11.6 %copy.72 = bf16[1,1,32,8,192,128]{5,4,3,2,1,0:T(8,128)(2,1)} copy(bf16[1,1,32,8,192,128]{5,4,3,2,1,0:T(8,128)(2,1)} %bitcast.30) | data formatting | bytes 25165824
  (97 shorter events, 26.3 us)
Async XLA Ops:
  0.6 32.1 %copy-start = (f32[8,128]{1,0:T(8,128)S(1)}, f32[8,128]{1,0:T(8,128)}, u32[]{:S(2)}) copy-start(f32[8,128]{1,0:T(8,128)} %param.14) | copy-start | bytes 12292
  0.6 16.9 %collective-permute-start.1 = (f32[4,1,64]{1,2,0:T(8,128)}, f32[4,1,64]{1,2,0:T(8,128)S(1)}, u32[]{:S(2)}, u32[]{:S(2)}) collective-permute-start(f32[4,1,64]{1,2,0:T(8,128)} %bitcast.111), channel_id=1, source_target_pairs={{0,24},{8,0},{16,8},{24,16},{1,25},{9,1},{17,9},{25,17},{2,26},{10... | collective-permute-start | bytes 3080 | tf_op jit(solution)/shard_map/ppermute | solution.py:19
  1.5 24.9 %collective-permute-start = (f32[4,128,1]{1,2,0:T(1,128)S(1)}, f32[4,128,1]{1,2,0:T(1,128)S(1)}, u32[]{:S(2)}, u32[]{:S(2)}) collective-permute-start(f32[4,128,1]{1,2,0:T(1,128)S(1)} %slice.36), channel_id=1, source_target_pairs={{0,7},{1,0},{2,1},{3,2},{4,3},{5,4},{6,5},{7,6},{8,15},{9,8},{10,9... | collective-permute-start | bytes 6152 | tf_op jit(solution)/shard_map/ppermute | solution.py:19
  23.4 9.8 %copy-start.3 = (f32[128,4]{0,1:T(4,128)S(1)}, f32[128,4]{0,1:T(4,128)}, u32[]{:S(2)}) copy-start(f32[128,4]{0,1:T(4,128)} %param.15) | copy-start | bytes 6148
  23.4 9.8 %copy-start.4 = (bf16[128,128]{1,0:T(8,128)(2,1)S(1)}, bf16[128,128]{1,0:T(8,128)(2,1)}, u32[]{:S(2)}) copy-start(bf16[128,128]{1,0:T(8,128)(2,1)} %param.13) | copy-start | bytes 98308
  107.7 8.1 %copy-start.2 = (f32[4,128,64]{1,2,0:T(8,128)S(1)}, f32[4,128,64]{1,2,0:T(8,128)}, u32[]{:S(2)}) copy-start(f32[4,128,64]{1,2,0:T(8,128)} %param.9) | copy-start | bytes 393220
  107.7 292.3 %all-to-all-start = ((bf16[32,8,192,128]{3,2,1,0:T(8,128)(2,1)}), bf16[32,8,192,128]{3,2,1,0:T(8,128)(2,1)}, u32[]{:S(2)}, u32[]{:S(2)}) async-start(bf16[32,8,192,128]{3,2,1,0:T(8,128)(2,1)} %broadcast_select_fusion), calls=%async_computation | async-start | bytes 25165824 | tf_op jit(solution)/shard_map/all_to_all | solution.py:93
  143.4 255.8 %collective-permute-start.2 = (f32[4,128,1]{1,2,0:T(1,128)S(1)}, f32[4,128,1]{1,2,0:T(1,128)S(1)}, u32[]{:S(2)}, u32[]{:S(2)}) collective-permute-start(f32[4,128,1]{1,2,0:T(1,128)S(1)} %slice.59), channel_id=1, source_target_pairs={{0,1},{1,2},{2,3},{3,4},{4,5},{5,6},{6,7},{7,0},{8,9},{9,10},{10,1... | collective-permute-start | bytes 6152 | tf_op jit(solution)/shard_map/ppermute | solution.py:19
  148.8 36.2 %collective-permute-start.3 = (f32[4,1,64]{1,2,0:T(8,128)S(1)}, f32[4,1,64]{1,2,0:T(8,128)S(1)}, u32[]{:S(2)}, u32[]{:S(2)}) collective-permute-start(f32[4,1,64]{1,2,0:T(8,128)S(1)} %slice.62), channel_id=1, source_target_pairs={{0,8},{8,16},{16,24},{24,0},{1,9},{9,17},{17,25},{25,1},{2,10},{10... | collective-permute-start | bytes 3080 | tf_op jit(solution)/shard_map/ppermute | solution.py:19
  400.0 11.7 %copy-start.1 = (f32[8,128]{1,0:T(8,128)S(1)}, f32[8,128]{1,0:T(8,128)}, u32[]{:S(2)}) copy-start(f32[8,128]{1,0:T(8,128)} %param.14) | copy-start | bytes 12292
where the time goes:
time: 412 us
  waiting for transfers between devices  250 us (61%)
  local copies, waits for them, and re-layouts  83.7 us (20%)
  matrix products  46.5 us (11%)
  other arithmetic  18.9 us (5%)
  starting transfers between devices  11 us (3%)
    ppermute x4, waiting for transfers between devices, passed_along(): return lax.ppermute(value, axis, pairs)  250 us
    dot_general x24, matrix products, advance(): jnp.dot(flat_rows, micro_weight, preferred_element_type=jnp.float32)  45 us
    unnamed x15, local copies, waits for them, and re-layouts  25.4 us
    gather x1, local copies, waits for them, and re-layouts, per_device(): picked = jnp.take(relaxed, source_slot, axis=0, mode='fill', fill_value=0)  15.2 us
    select_n x2, other arithmetic, per_device(): picked = jnp.take(relaxed, source_slot, axis=0, mode='fill', fill_value=0)  10.7 us
    slice x1, local copies, waits for them, and re-layouts, per_device(): south_flux = face_values[:, 1]  8.41 us
  transfers between devices with their start and end apart: 5, of which 2 were waited for; matrix products, arithmetic and copies ran while one was open for 14% of the time, Pallas kernels for 0%

commit v1 on v0

v1 whole, which is shorter than its diff:
```python
import functools

import jax
import jax.numpy as jnp
from jax import lax
from jax.experimental import pallas as pl
from jax.experimental.pallas import tpu as pltpu
from jax.sharding import PartitionSpec as P


STEPS = 3
RAW = 2
GROUP = 4


diffusion = 0.2
relax_rate = 0.5
time_step = 0.5
HIGHEST = lax.Precision.HIGHEST


def passed_along(value, axis, steps):
    count = lax.axis_size(axis)
    pairs = [(source, (source + steps) % count) for source in range(count)]
    return lax.ppermute(value, axis, pairs)


def partner_order(gx_count, gy_count):
    devices = gx_count * gy_count
    far = [k for k in range(1, devices) if k & (gy_count // 2)]
    near = [k for k in range(1, devices) if not k & (gy_count // 2)]
    order, taken = list(far[:2]), 0
    for place, k in enumerate(far[2:]):
        order.append(k)
        want = (place + 1) * len(near) // max(1, len(far) - 4)
        while taken < min(want, len(near)):
            order.append(near[taken])
            taken += 1
    return order + near[taken:]


def partner_groups(order):
    todo = order[RAW:] + order[:RAW] + [0]
    return [todo[:2]] + [todo[i : i + GROUP] for i in range(2, len(todo), GROUP)]


def route_kernel(capacity, raw, me_ref, owner_ref, face_ref, states_ref, table_ref, ids_ref, *rest):
    out_refs, (count_ref, buffer, in_sem, out_sem) = rest[: len(raw)], rest[len(raw) :]
    slot_total = owner_ref.shape[0]
    me = me_ref[0]

    def clear(number, carry):
        count_ref[number] = 0
        return carry

    lax.fori_loop(0, count_ref.shape[0], clear, 0)

    def place(slot, carry):
        code = jnp.bitwise_xor(owner_ref[slot], me)
        rank = count_ref[code]
        count_ref[code] = rank + 1
        position = code * capacity + rank
        table_ref[position] = slot
        ids_ref[position] = face_ref[slot]
        return carry

    lax.fori_loop(0, slot_total, place, 0, unroll=8)

    def fetch(turn, i):
        slot = table_ref[raw[turn] * capacity + i]
        return pltpu.make_async_copy(states_ref.at[slot], buffer.at[turn, i], in_sem.at[turn, i])

    def send(turn, i):
        return pltpu.make_async_copy(buffer.at[turn, i], out_refs[turn].at[i], out_sem.at[turn, i])

    steps = [(turn, i) for turn in range(len(raw)) for i in range(capacity)]
    for step in steps:
        fetch(*step).start()
    for step in steps:
        fetch(*step).wait()
        send(*step).start()
    for step in steps:
        send(*step).wait()


def forcing_kernel(capacity, raw, macro_ref, row_ref, col_ref, place_ref, lift_ref, force_ref, live_ref, *out_refs):
    channels, tile_rows, tile_cols = macro_ref.shape
    slot_total = place_ref.shape[0]
    place = place_ref[...]
    left_row, left_col, right_row, right_col, live = [place[:, i : i + 1] for i in range(5)]
    row_iota = lax.broadcasted_iota(jnp.int32, (slot_total, tile_rows), 1)
    col_iota = lax.broadcasted_iota(jnp.int32, (slot_total, tile_cols), 1)
    left_pick = (row_iota == left_row).astype(jnp.float32)
    right_pick = (row_iota == right_row).astype(jnp.float32)
    left_mask = col_iota == left_col
    right_mask = col_iota == right_col
    edge_row = right_mask & (right_row == tile_rows)
    edge_col = (row_iota == right_row) & (right_col == tile_cols)
    total = jnp.zeros((slot_total, lift_ref.shape[1]), jnp.float32)
    for channel in range(channels):
        block = macro_ref[channel]
        left = jnp.dot(left_pick, block, precision=HIGHEST, preferred_element_type=jnp.float32)
        left = jnp.sum(jnp.where(left_mask, left, 0.0), axis=1, keepdims=True)
        right = jnp.dot(right_pick, block, precision=HIGHEST, preferred_element_type=jnp.float32)
        right = jnp.where(right_mask, right, 0.0) + jnp.where(edge_row, row_ref[channel : channel + 1, :], 0.0)
        right = jnp.sum(right, axis=1, keepdims=True)
        beyond = jnp.where(edge_col, col_ref[channel : channel + 1, :], 0.0)
        right = right + jnp.sum(beyond, axis=1, keepdims=True)
        total = total + left * lift_ref[channel : channel + 1, :]
        total = total + right * lift_ref[channels + channel : channels + channel + 1, :]
    force_ref[...] = total
    alive = jnp.broadcast_to((live > 0).astype(jnp.float32), total.shape)
    live_ref[...] = alive
    for turn, k in enumerate(raw):
        out_refs[turn][0:capacity, :] = total[k * capacity : (k + 1) * capacity, :]
        out_refs[turn][capacity:, :] = alive[k * capacity : (k + 1) * capacity, :]


def relaxed_states(current, force, weight, live):
    slots, members, width = current.shape
    force = force.reshape(slots, 1, width)
    for _ in range(STEPS):
        activation = jnp.dot(current.reshape(slots * members, width), weight, preferred_element_type=jnp.float32)
        activation = activation.reshape(slots, members, width) + force
        current = (
            (1.0 - relax_rate) * current.astype(jnp.float32) + relax_rate * jnp.tanh(activation)
        ).astype(jnp.bfloat16)
    return current * live.astype(jnp.bfloat16).reshape(slots, 1, width)


def relax_kernel(
    capacity, partners, kept, own, me_ref, table_ref, states_ref, force_ref, live_ref, weight_ref, *rest
):
    out_refs, (sums_ref, in_buffer, out_buffer, in_sem, out_sem) = rest[: len(kept)], rest[len(kept) :]
    target = {k: ref for k, ref in zip(kept, out_refs)}

    def fetch(turn, i):
        slot = table_ref[partners[turn] * capacity + i]
        return pltpu.make_async_copy(states_ref.at[slot], in_buffer.at[turn % 2, i], in_sem.at[turn % 2, i])

    def send(turn):
        k = partners[turn]
        ref = target[k].at[me_ref[0]] if k == own else target[k]
        return pltpu.make_async_copy(out_buffer.at[turn % 2], ref, out_sem.at[turn % 2])

    for i in range(capacity):
        fetch(0, i).start()
    weight = weight_ref[...]
    waiting = {}
    for turn, k in enumerate(partners):
        if turn + 1 < len(partners):
            for i in range(capacity):
                fetch(turn + 1, i).start()
        if turn % 2 in waiting:
            send(waiting.pop(turn % 2)).wait()
        for i in range(capacity):
            fetch(turn, i).wait()

        rows = slice(k * capacity, (k + 1) * capacity)
        block = relaxed_states(in_buffer[turn % 2], force_ref[rows, :], weight, live_ref[rows, :])
        out_buffer[turn % 2] = block
        sums_ref[turn * capacity : (turn + 1) * capacity, :] = jnp.sum(block.astype(jnp.float32), axis=1)
        if k in target:
            send(turn).start()
            waiting[turn % 2] = turn
    for turn in waiting.values():
        send(turn).wait()


def land_kernel(capacity, source_ref, raw_ref, force_ref, weight_ref, whole_ref, out_ref, buffer, out_sem):
    buffer[...] = relaxed_states(
        raw_ref[...], force_ref[0:capacity, :], weight_ref[...], force_ref[capacity:, :]
    )
    copy = pltpu.make_async_copy(buffer, out_ref.at[source_ref[0]], out_sem)
    copy.start()
    copy.wait()


def flux_kernel(members, sums_ref, readout_ref, place_ref, place_row_ref, flux_ref, hit_ref):
    _, channels, tile_rows, tile_cols = flux_ref.shape
    slot_total = place_ref.shape[0]
    mean = sums_ref[...] / members
    flux = jnp.dot(mean, readout_ref[...], precision=HIGHEST, preferred_element_type=jnp.float32)
    col_iota = lax.broadcasted_iota(jnp.int32, (slot_total, tile_cols), 1)
    col_pick = (col_iota == place_ref[:, 1:2]).astype(jnp.float32)
    row_iota = lax.broadcasted_iota(jnp.int32, (tile_rows, slot_total), 0)
    row_pick = (row_iota == place_row_ref[0:1, :]) & (place_row_ref[4:5, :] > 0)
    for direction in range(2):
        pick = (row_pick & (place_row_ref[5:6, :] == direction)).astype(jnp.float32)
        hit_ref[direction] = jnp.dot(pick, col_pick, precision=HIGHEST, preferred_element_type=jnp.float32)
        for channel in range(channels):
            spread = col_pick * flux[:, channel : channel + 1]
            flux_ref[direction, channel] = jnp.dot(
                pick, spread, precision=HIGHEST, preferred_element_type=jnp.float32
            )


ANY = pl.BlockSpec(memory_space=pl.ANY)
VMEM = pl.BlockSpec(memory_space=pltpu.VMEM)
SMEM = pl.BlockSpec(memory_space=pltpu.SMEM)


def per_device(macro_state, face_list, owner, face_states, micro_weight, lift_weight, readout):
    channels, tile_rows, tile_cols = macro_state.shape
    slot_total = face_list.shape[2]
    members, state_width = face_states.shape[3:]
    gx_count, gy_count = lax.axis_size("gx"), lax.axis_size("gy")
    devices = gx_count * gy_count
    capacity = max(2, slot_total // devices)
    assert capacity * devices == slot_total and devices & (devices - 1) == 0
    order = partner_order(gx_count, gy_count)
    raw = order[:RAW]
    block = jax.ShapeDtypeStruct((capacity, members, state_width), jnp.bfloat16)
    whole = jax.ShapeDtypeStruct((devices, capacity, members, state_width), jnp.bfloat16)
    me = lax.axis_index("gx") * gy_count + lax.axis_index("gy")
    me_ref = me.astype(jnp.int32).reshape(1)
    states = face_states.reshape(slot_total, members, state_width)
    faces = face_list.reshape(slot_total)

    def exchanged(value, k):
        return lax.ppermute(value, ("gx", "gy"), [(source, source ^ k) for source in range(devices)])

    slots_smem = jax.ShapeDtypeStruct((slot_total,), jnp.int32)
    table, ids, *raw_sent = pl.pallas_call(
        functools.partial(route_kernel, capacity, raw),
        out_shape=[slots_smem, slots_smem] + [block] * len(raw),
        in_specs=[SMEM, SMEM, SMEM, ANY],
        out_specs=[SMEM, SMEM] + [ANY] * len(raw),
        scratch_shapes=[
            pltpu.SMEM((devices,), jnp.int32),
            pltpu.VMEM((len(raw), capacity, members, state_width), jnp.bfloat16),
            pltpu.SemaphoreType.DMA((len(raw), capacity)),
            pltpu.SemaphoreType.DMA((len(raw), capacity)),
        ],
        name="route",
    )(me_ref, owner.reshape(slot_total), faces, states)

    raw_got = []
    for turn, k in enumerate(raw):
        raw_got.append(exchanged(raw_sent[turn], k))

    first_row, first_col, table = lax.optimization_barrier((macro_state[:, 0, :], macro_state[:, :, 0], table))
    next_row = passed_along(first_row, "gx", -1)
    next_col = passed_along(first_col, "gy", -1)

    live = ids >= 0
    safe = jnp.where(live, ids, 0)
    direction = safe // (tile_rows * tile_cols)
    cell = safe % (tile_rows * tile_cols)
    left_row, left_col = cell // tile_cols, cell % tile_cols
    right_row, right_col = left_row + direction, left_col + 1 - direction
    place = [left_row, left_col, right_row, right_col, live.astype(jnp.int32), direction, cell, safe]
    place_rows = jnp.stack(place, axis=0)
    place_cols = jnp.stack(place, axis=1)

    force, alive, *raw_force = pl.pallas_call(
        functools.partial(forcing_kernel, capacity, raw),
        out_shape=[jax.ShapeDtypeStruct((slot_total, state_width), jnp.float32)] * 2
        + [jax.ShapeDtypeStruct((2 * capacity, state_width), jnp.float32)] * len(raw),
        in_specs=[VMEM] * 5,
        out_specs=[VMEM] * (2 + len(raw)),
        name="forcing",
    )(macro_state, next_row, next_col, place_cols, lift_weight)

    force_got = []
    for turn, k in enumerate(raw):
        force_got.append(exchanged(raw_force[turn], k))

    groups = partner_groups(order)
    sums, relaxed = {}, {}
    for partners in groups:
        kept = [k for k in partners if k not in raw]
        *blocks, part = pl.pallas_call(
            functools.partial(relax_kernel, capacity, partners, kept, 0),
            out_shape=[whole if k == 0 else block for k in kept]
            + [jax.ShapeDtypeStruct((len(partners) * capacity, state_width), jnp.float32)],
            in_specs=[SMEM, SMEM, ANY, VMEM, VMEM, VMEM],
            out_specs=[ANY] * len(kept) + [VMEM],
            scratch_shapes=[
                pltpu.VMEM((2, capacity, members, state_width), jnp.bfloat16),
                pltpu.VMEM((2, capacity, members, state_width), jnp.bfloat16),
                pltpu.SemaphoreType.DMA((2, capacity)),
                pltpu.SemaphoreType.DMA((2,)),
            ],
        )(me_ref, table, states, force, alive, micro_weight)
        table, part = lax.optimization_barrier((table, part))
        for k, value in zip(kept, blocks):
            relaxed[k] = value
        for turn, k in enumerate(partners):
            sums[k] = part[turn * capacity : (turn + 1) * capacity]
    all_sums = jnp.concatenate([sums[k] for k in range(devices)], axis=0)

    got = {}
    for k in order[RAW:]:
        got[k] = exchanged(relaxed[k], k)

    face_flux, hit = pl.pallas_call(
        functools.partial(flux_kernel, members),
        out_shape=[
            jax.ShapeDtypeStruct((2, channels, tile_rows, tile_cols), jnp.float32),
            jax.ShapeDtypeStruct((2, tile_rows, tile_cols), jnp.float32),
        ],
        in_specs=[VMEM] * 4,
        out_specs=[VMEM] * 2,
        name="flux",
    )(all_sums, readout, place_cols, place_rows)
    beyond_row = jnp.concatenate([macro_state[:, 1:, :], next_row[:, None, :]], axis=1)
    beyond_col = jnp.concatenate([macro_state[:, :, 1:], next_col[:, :, None]], axis=2)
    east_flux = jnp.where(hit[0] > 0.5, face_flux[0], diffusion * (macro_state - beyond_col))
    south_flux = jnp.where(hit[1] > 0.5, face_flux[1], diffusion * (macro_state - beyond_row))
    west_flux = passed_along(east_flux[:, :, -1], "gy", 1)
    north_flux = passed_along(south_flux[:, -1, :], "gx", 1)
    macro_next = macro_state - time_step * (
        east_flux
        - jnp.concatenate([west_flux[:, :, None], east_flux[:, :, :-1]], axis=2)
        + south_flux
        - jnp.concatenate([north_flux[:, None, :], south_flux[:, :-1, :]], axis=1)
    )

    out = relaxed[0]
    for turn, k in enumerate(raw):
        out = pl.pallas_call(
            functools.partial(land_kernel, capacity),
            out_shape=whole,
            in_specs=[SMEM, VMEM, VMEM, VMEM, ANY],
            out_specs=ANY,
            scratch_shapes=[
                pltpu.VMEM((capacity, members, state_width), jnp.bfloat16),
                pltpu.SemaphoreType.DMA,
            ],
            input_output_aliases={4: 0},
        )(jnp.bitwise_xor(me_ref, k), raw_got[turn], force_got[turn], micro_weight, out)
    for k in order[RAW:]:
        out = lax.dynamic_update_slice(out, got[k][None], (jnp.bitwise_xor(me, k), 0, 0, 0))
    return macro_next, out.reshape(1, 1, devices, capacity, members, state_width)


def solution(mesh):
    return jax.shard_map(
        per_device,
        mesh=mesh,
        in_specs=(
            P(None, "gx", "gy"),
            P("gx", "gy", None),
            P("gx", "gy", None, None),
            P("gx", "gy", None, None, None),
            P(),
            P(),
            P(),
        ),
        out_specs=(P(None, "gx", "gy"), P("gx", "gy", None, None, None, None)),
        check_vma=False,
    )
```

time: 412 us -> 348 us (0.84)
  waiting for transfers between devices: 250 us -> 174 us
  Pallas kernels: 0 us -> 70.9 us
  starting transfers between devices: 11 us -> 62.3 us
  local copies, waits for them, and re-layouts: 83.7 us -> 32.6 us
  matrix products: 46.5 us -> 0 us
  other arithmetic: 18.9 us -> 3.63 us
    ppermute x4, waiting for transfers between devices: 250 us -> 19.1 us  [passed_along(): return lax.ppermute(value, axis, pairs)]
    ppermute x0 -> x33, waiting for transfers between devices: none -> 155 us  [exchanged(): lax.ppermute(value, ('gx', 'gy'), [(source, source ^ k) for source in ran...]
    pallas_call x0 -> x14, Pallas kernels: none -> 70.9 us  [the longest x9 54.7 us: per_device(): pl.pallas_call(functools.partial(relax_kernel, capacity, partners, kept,...]
    ppermute x0 -> x33, starting transfers between devices: none -> 59 us  [exchanged(): lax.ppermute(value, ('gx', 'gy'), [(source, source ^ k) for source in ran...]
    dot_general x33 -> x0, matrix products: 46.5 us -> none  [the longest x24 45 us: advance(): jnp.dot(flat_rows, micro_weight, preferred_element_type=jnp.float32)]
    gather x5 -> x0, local copies, waits for them, and re-layouts: 24 us -> none  [the longest x1 15.2 us: per_device(): picked = jnp.take(relaxed, source_slot, axis=0, mode='fill', fill_value=0)]
    dynamic_update_slice x0 -> x29, local copies, waits for them, and re-layouts: none -> 22.4 us  [per_device(): lax.dynamic_update_slice(out, got[k][None], (jnp.bitwise_xor(me, k), 0, 0...]
    unnamed x15 -> x93, local copies, waits for them, and re-layouts: 25.4 us -> 7.28 us
  transfers between devices with their start and end apart: 5 -> 37, of which waited for: 2 -> 20; matrix products, arithmetic and copies ran while one was open for 14% -> 9% of each run, Pallas kernels for 0% -> 19%
where the time goes in v1:
time: 348 us; the launch traced here: 345 us
  waiting for transfers between devices  174 us (50%)
  Pallas kernels  70.9 us (20%)
  starting transfers between devices  62.3 us (18%)
  local copies, waits for them, and re-layouts  32.6 us (9%)
  other arithmetic  3.63 us (1%)
    ppermute x33, waiting for transfers between devices, exchanged(): lax.ppermute(value, ('gx', 'gy'), [(source, source ^ k) for source in ran...  155 us
    ppermute x33, starting transfers between devices, exchanged(): lax.ppermute(value, ('gx', 'gy'), [(source, source ^ k) for source in ran...  59 us
    pallas_call x9, Pallas kernels, per_device(): pl.pallas_call(functools.partial(relax_kernel, capacity, partners, kept,...  54.7 us
    dynamic_update_slice x29, local copies, waits for them, and re-layouts, per_device(): lax.dynamic_update_slice(out, got[k][None], (jnp.bitwise_xor(me, k), 0, 0...  22.4 us
    ppermute x4, waiting for transfers between devices, passed_along(): return lax.ppermute(value, axis, pairs)  19.1 us
    unnamed x93, local copies, waits for them, and re-layouts  7.28 us
  transfers between devices with their start and end apart: 37, of which 20 were waited for; matrix products, arithmetic and copies ran while one was open for 9% of the time, Pallas kernels for 19%

profile of v1, /device:TPU:20, one launch (start us, length us, event | category | flops | bytes accessed | tf_op | source)
XLA Modules:
  0.0 345.2 jit_solution(1971436659281319823)
XLA Ops:
  2.4 5.0 %route.1 = (s32[256]{0:T(256)}, s32[256]{0:T(256)}, bf16[8,192,128]{2,1,0:T(8,128)(2,1)}, bf16[8,192,128]{2,1,0:T(8,128)(2,1)}) custom-call(s32[1]{0:T(128)} %bitcast.2.me_ref, s32[256]{0:T(256)} %bitcast.138, s32[256]{0:T(256)} %bitcast.139, bf16[256,192,128]{2,1,0:T(8,128)(2,1)} %bitcast.101), custom_call_target="tpu_custom_call" | custom-call | tf_op jit(solution)/shard_map/route/pallas_call | solution.py:224
  20.5 4.9 %shard_map.86 = (bf16[8,192,128]{2,1,0:T(8,128)(2,1)}, bf16[8,192,128]{2,1,0:T(8,128)(2,1)}, f32[16,128]{1,0:T(8,128)}) custom-call(s32[1]{0:T(128)} %bitcast.2.me_ref, s32[256]{0:T(256)} %get-tuple-element.93.table_ref, bf16[256,192,128]{2,1,0:T(8,128)(2,1)} %bitcast.102, f32[256,128]{1,0:T(8,128)} %get-tuple-element.76.force_ref, ...), custom_call_target="tpu_custom_call" | custom-call | tf_op jit(solution)/shard_map/pallas_call | solution.py:273
  25.5 6.4 %shard_map.87 = (bf16[8,192,128]{2,1,0:T(8,128)(2,1)}, bf16[8,192,128]{2,1,0:T(8,128)(2,1)}, bf16[8,192,128]{2,1,0:T(8,128)(2,1)}, bf16[8,192,128]{2,1,0:T(8,128)(2,1)}, f32[32,128]{1,0:T(8,128)}) custom-call(s32[1]{0:T(128)} %bitcast.2.me_ref, s32[256]{0:T(256)} %get-tuple-element.93.table_ref, bf16[256,192,128]{2,1,0:T(8,128)(2,1)} %bitcast.103, ...), custom_call_target="tpu_custom_call" | custom-call | tf_op jit(solution)/shard_map/pallas_call | solution.py:273
  31.9 6.5 %shard_map.88 = (bf16[8,192,128]{2,1,0:T(8,128)(2,1)}, bf16[8,192,128]{2,1,0:T(8,128)(2,1)}, bf16[8,192,128]{2,1,0:T(8,128)(2,1)}, bf16[8,192,128]{2,1,0:T(8,128)(2,1)}, f32[32,128]{1,0:T(8,128)}) custom-call(s32[1]{0:T(128)} %bitcast.2.me_ref, s32[256]{0:T(256)} %get-tuple-element.93.table_ref, bf16[256,192,128]{2,1,0:T(8,128)(2,1)} %bitcast.104, ...), custom_call_target="tpu_custom_call" | custom-call | tf_op jit(solution)/shard_map/pallas_call | solution.py:273
  38.4 6.7 %shard_map.89 = (bf16[8,192,128]{2,1,0:T(8,128)(2,1)}, bf16[8,192,128]{2,1,0:T(8,128)(2,1)}, bf16[8,192,128]{2,1,0:T(8,128)(2,1)}, bf16[8,192,128]{2,1,0:T(8,128)(2,1)}, f32[32,128]{1,0:T(8,128)}) custom-call(s32[1]{0:T(128)} %bitcast.2.me_ref, s32[256]{0:T(256)} %get-tuple-element.93.table_ref, bf16[256,192,128]{2,1,0:T(8,128)(2,1)} %bitcast.105, ...), custom_call_target="tpu_custom_call" | custom-call | tf_op jit(solution)/shard_map/pallas_call | solution.py:273
  45.1 6.5 %shard_map.90 = (bf16[8,192,128]{2,1,0:T(8,128)(2,1)}, bf16[8,192,128]{2,1,0:T(8,128)(2,1)}, bf16[8,192,128]{2,1,0:T(8,128)(2,1)}, bf16[8,192,128]{2,1,0:T(8,128)(2,1)}, f32[32,128]{1,0:T(8,128)}) custom-call(s32[1]{0:T(128)} %bitcast.2.me_ref, s32[256]{0:T(256)} %get-tuple-element.93.table_ref, bf16[256,192,128]{2,1,0:T(8,128)(2,1)} %bitcast.106, ...), custom_call_target="tpu_custom_call" | custom-call | tf_op jit(solution)/shard_map/pallas_call | solution.py:273
  51.5 6.5 %shard_map.91 = (bf16[8,192,128]{2,1,0:T(8,128)(2,1)}, bf16[8,192,128]{2,1,0:T(8,128)(2,1)}, bf16[8,192,128]{2,1,0:T(8,128)(2,1)}, bf16[8,192,128]{2,1,0:T(8,128)(2,1)}, f32[32,128]{1,0:T(8,128)}) custom-call(s32[1]{0:T(128)} %bitcast.2.me_ref, s32[256]{0:T(256)} %get-tuple-element.93.table_ref, bf16[256,192,128]{2,1,0:T(8,128)(2,1)} %bitcast.107, ...), custom_call_target="tpu_custom_call" | custom-call | tf_op jit(solution)/shard_map/pallas_call | solution.py:273
  58.0 6.4 %shard_map.92 = (bf16[8,192,128]{2,1,0:T(8,128)(2,1)}, bf16[8,192,128]{2,1,0:T(8,128)(2,1)}, bf16[8,192,128]{2,1,0:T(8,128)(2,1)}, bf16[8,192,128]{2,1,0:T(8,128)(2,1)}, f32[32,128]{1,0:T(8,128)}) custom-call(s32[1]{0:T(128)} %bitcast.2.me_ref, s32[256]{0:T(256)} %get-tuple-element.93.table_ref, bf16[256,192,128]{2,1,0:T(8,128)(2,1)} %bitcast.108, ...), custom_call_target="tpu_custom_call" | custom-call | tf_op jit(solution)/shard_map/pallas_call | solution.py:273
  64.6 5.8 %shard_map.93 = (bf16[8,192,128]{2,1,0:T(8,128)(2,1)}, bf16[8,192,128]{2,1,0:T(8,128)(2,1)}, bf16[8,192,128]{2,1,0:T(8,128)(2,1)}, f32[32,128]{1,0:T(8,128)}) custom-call(s32[1]{0:T(128)} %bitcast.2.me_ref, s32[256]{0:T(256)} %get-tuple-element.93.table_ref, bf16[256,192,128]{2,1,0:T(8,128)(2,1)} %bitcast.109, f32[256,128]{1,0:T(8,128)} %get-tuple-element.76.force_ref, ...), custom_call_target="tpu_custom_call" | custom-call | tf_op jit(solution)/shard_map/pallas_call | solution.py:273
  70.4 5.0 %shard_map.94 = (bf16[32,8,192,128]{3,2,1,0:T(8,128)(2,1)}, f32[16,128]{1,0:T(8,128)}) custom-call(s32[1]{0:T(128)} %bitcast.2.me_ref, s32[256]{0:T(256)} %get-tuple-element.93.table_ref, bf16[256,192,128]{2,1,0:T(8,128)(2,1)} %bitcast.110, f32[256,128]{1,0:T(8,128)} %get-tuple-element.76.force_ref, f32[256,128]{1,0:T(8,128)} %get-tuple-element.77.live_ref, ...), custom_call_target="tpu_custom_call" | custom-call | tf_op jit(solution)/shard_map/pallas_call | solution.py:273
  77.7 3.3 flux.1
  87.9 16.2 %collective-permute-done.2 = f32[4,128]{1,0:T(4,128)S(1)} collective-permute-done((f32[4,128]{1,0:T(4,128)S(1)}, f32[4,128]{1,0:T(4,128)S(1)}, u32[]{:S(2)}, u32[]{:S(2)}) %collective-permute-start.2) | collective-permute-done | bytes 2080 | tf_op jit(solution)/shard_map/ppermute | solution.py:25
  121.5 3.6 %collective-permute-start.14 = (bf16[8,192,128]{2,1,0:T(8,128)(2,1)}, bf16[8,192,128]{2,1,0:T(8,128)(2,1)S(1)}, u32[]{:S(2)}, u32[]{:S(2)}) collective-permute-start(bf16[8,192,128]{2,1,0:T(8,128)(2,1)} %get-tuple-element.117), channel_id=1, source_target_pairs={{0,13},{1,12},{2,15},{3,14},{4,9},{5,8},{6,11},{7,10},{8,5},{9,4},... | collective-permute-start | bytes 1179656 | tf_op jit(solution)/shard_map/ppermute | solution.py:221
  125.8 5.2 %collective-permute-done.10 = bf16[8,192,128]{2,1,0:T(8,128)(2,1)S(1)} collective-permute-done((bf16[8,192,128]{2,1,0:T(8,128)(2,1)}, bf16[8,192,128]{2,1,0:T(8,128)(2,1)S(1)}, u32[]{:S(2)}, u32[]{:S(2)}) %collective-permute-start.10) | collective-permute-done | bytes 393248 | tf_op jit(solution)/shard_map/ppermute | solution.py:221
  134.7 8.9 %collective-permute-done.12 = bf16[8,192,128]{2,1,0:T(8,128)(2,1)S(1)} collective-permute-done((bf16[8,192,128]{2,1,0:T(8,128)(2,1)}, bf16[8,192,128]{2,1,0:T(8,128)(2,1)S(1)}, u32[]{:S(2)}, u32[]{:S(2)}) %collective-permute-start.12) | collective-permute-done | bytes 393248 | tf_op jit(solution)/shard_map/ppermute | solution.py:221
  144.4 7.5 %collective-permute-done.13 = bf16[8,192,128]{2,1,0:T(8,128)(2,1)S(1)} collective-permute-done((bf16[8,192,128]{2,1,0:T(8,128)(2,1)}, bf16[8,192,128]{2,1,0:T(8,128)(2,1)S(1)}, u32[]{:S(2)}, u32[]{:S(2)}) %collective-permute-start.13) | collective-permute-done | bytes 393248 | tf_op jit(solution)/shard_map/ppermute | solution.py:221
  152.7 15.9 %collective-permute-done.14 = bf16[8,192,128]{2,1,0:T(8,128)(2,1)S(1)} collective-permute-done((bf16[8,192,128]{2,1,0:T(8,128)(2,1)}, bf16[8,192,128]{2,1,0:T(8,128)(2,1)S(1)}, u32[]{:S(2)}, u32[]{:S(2)}) %collective-permute-start.14) | collective-permute-done | bytes 393248 | tf_op jit(solution)/shard_map/ppermute | solution.py:221
  169.4 4.0 %collective-permute-start.20 = (bf16[8,192,128]{2,1,0:T(8,128)(2,1)}, bf16[8,192,128]{2,1,0:T(8,128)(2,1)S(1)}, u32[]{:S(2)}, u32[]{:S(2)}) collective-permute-start(bf16[8,192,128]{2,1,0:T(8,128)(2,1)} %get-tuple-element.123), channel_id=1, source_target_pairs={{0,11},{1,10},{2,9},{3,8},{4,15},{5,14},{6,13},{7,12},{8,3},{9,2},... | collective-permute-start | bytes 1179656 | tf_op jit(solution)/shard_map/ppermute | solution.py:221
  174.1 3.2 collective-permute-start.21
  178.1 7.3 %collective-permute-done.17 = bf16[8,192,128]{2,1,0:T(8,128)(2,1)S(1)} collective-permute-done((bf16[8,192,128]{2,1,0:T(8,128)(2,1)}, bf16[8,192,128]{2,1,0:T(8,128)(2,1)S(1)}, u32[]{:S(2)}, u32[]{:S(2)}) %collective-permute-start.17) | collective-permute-done | bytes 393248 | tf_op jit(solution)/shard_map/ppermute | solution.py:221
  188.4 24.5 %collective-permute-done.19 = bf16[8,192,128]{2,1,0:T(8,128)(2,1)S(1)} collective-permute-done((bf16[8,192,128]{2,1,0:T(8,128)(2,1)}, bf16[8,192,128]{2,1,0:T(8,128)(2,1)S(1)}, u32[]{:S(2)}, u32[]{:S(2)}) %collective-permute-start.19) | collective-permute-done | bytes 393248 | tf_op jit(solution)/shard_map/ppermute | solution.py:221
  216.6 4.1 %collective-permute-done.21 = bf16[8,192,128]{2,1,0:T(8,128)(2,1)S(1)} collective-permute-done((bf16[8,192,128]{2,1,0:T(8,128)(2,1)}, bf16[8,192,128]{2,1,0:T(8,128)(2,1)S(1)}, u32[]{:S(2)}, u32[]{:S(2)}) %collective-permute-start.21) | collective-permute-done | bytes 393248 | tf_op jit(solution)/shard_map/ppermute | solution.py:221
  220.7 3.3 collective-permute-start.26
  224.7 4.4 %collective-permute-start.27 = (bf16[8,192,128]{2,1,0:T(8,128)(2,1)}, bf16[8,192,128]{2,1,0:T(8,128)(2,1)S(1)}, u32[]{:S(2)}, u32[]{:S(2)}) collective-permute-start(bf16[8,192,128]{2,1,0:T(8,128)(2,1)} %get-tuple-element.130), channel_id=1, source_target_pairs={{0,19},{1,18},{2,17},{3,16},{4,23},{5,22},{6,21},{7,20},{8,27},{9,... | collective-permute-start | bytes 1179656 | tf_op jit(solution)/shard_map/ppermute | solution.py:221
  235.7 10.8 %collective-permute-done.25 = bf16[8,192,128]{2,1,0:T(8,128)(2,1)S(1)} collective-permute-done((bf16[8,192,128]{2,1,0:T(8,128)(2,1)}, bf16[8,192,128]{2,1,0:T(8,128)(2,1)S(1)}, u32[]{:S(2)}, u32[]{:S(2)}) %collective-permute-start.25) | collective-permute-done | bytes 393248 | tf_op jit(solution)/shard_map/ppermute | solution.py:221
  248.9 7.6 %collective-permute-done.26 = bf16[8,192,128]{2,1,0:T(8,128)(2,1)S(1)} collective-permute-done((bf16[8,192,128]{2,1,0:T(8,128)(2,1)}, bf16[8,192,128]{2,1,0:T(8,128)(2,1)S(1)}, u32[]{:S(2)}, u32[]{:S(2)}) %collective-permute-start.26) | collective-permute-done | bytes 393248 | tf_op jit(solution)/shard_map/ppermute | solution.py:221
  262.5 32.1 %collective-permute-done.28 = bf16[8,192,128]{2,1,0:T(8,128)(2,1)S(1)} collective-permute-done((bf16[8,192,128]{2,1,0:T(8,128)(2,1)S(1)}, bf16[8,192,128]{2,1,0:T(8,128)(2,1)S(1)}, u32[]{:S(2)}, u32[]{:S(2)}) %collective-permute-start.28) | collective-permute-done | bytes 393248 | tf_op jit(solution)/shard_map/ppermute | solution.py:221
  299.2 7.1 %collective-permute-start.35 = (bf16[8,192,128]{2,1,0:T(8,128)(2,1)S(1)}, bf16[8,192,128]{2,1,0:T(8,128)(2,1)S(1)}, u32[]{:S(2)}, u32[]{:S(2)}) collective-permute-start(bf16[8,192,128]{2,1,0:T(8,128)(2,1)S(1)} %copy-done.21), channel_id=1, source_target_pairs={{0,30},{1,31},{2,28},{3,29},{4,26},{5,27},{6,24},{7,25},{8,22},{9,... | collective-permute-start | bytes 1179656 | tf_op jit(solution)/shard_map/ppermute | solution.py:221
  307.1 7.2 %collective-permute-start.36 = (bf16[8,192,128]{2,1,0:T(8,128)(2,1)S(1)}, bf16[8,192,128]{2,1,0:T(8,128)(2,1)S(1)}, u32[]{:S(2)}, u32[]{:S(2)}) collective-permute-start(bf16[8,192,128]{2,1,0:T(8,128)(2,1)S(1)} %copy-done.20), channel_id=1, source_target_pairs={{0,31},{1,30},{2,29},{3,28},{4,27},{5,26},{6,25},{7,24},{8,23},{9,... | collective-permute-start | bytes 1179656 | tf_op jit(solution)/shard_map/ppermute | solution.py:221
  316.7 4.0 %collective-permute-done.34 = bf16[8,192,128]{2,1,0:T(8,128)(2,1)S(1)} collective-permute-done((bf16[8,192,128]{2,1,0:T(8,128)(2,1)S(1)}, bf16[8,192,128]{2,1,0:T(8,128)(2,1)S(1)}, u32[]{:S(2)}, u32[]{:S(2)}) %collective-permute-start.34) | collective-permute-done | bytes 393248 | tf_op jit(solution)/shard_map/ppermute | solution.py:221
  321.4 12.6 %collective-permute-done.35 = bf16[8,192,128]{2,1,0:T(8,128)(2,1)S(1)} collective-permute-done((bf16[8,192,128]{2,1,0:T(8,128)(2,1)S(1)}, bf16[8,192,128]{2,1,0:T(8,128)(2,1)S(1)}, u32[]{:S(2)}, u32[]{:S(2)}) %collective-permute-start.35) | collective-permute-done | bytes 393248 | tf_op jit(solution)/shard_map/ppermute | solution.py:221
  334.8 9.7 %collective-permute-done.36 = bf16[8,192,128]{2,1,0:T(8,128)(2,1)S(1)} collective-permute-done((bf16[8,192,128]{2,1,0:T(8,128)(2,1)S(1)}, bf16[8,192,128]{2,1,0:T(8,128)(2,1)S(1)}, u32[]{:S(2)}, u32[]{:S(2)}) %collective-permute-start.36) | collective-permute-done | bytes 393248 | tf_op jit(solution)/shard_map/ppermute | solution.py:221
  (195 shorter events, 81.6 us)
Async XLA Ops:
  8.9 107.0 %collective-permute-start.4 = (bf16[8,192,128]{2,1,0:T(8,128)(2,1)}, bf16[8,192,128]{2,1,0:T(8,128)(2,1)S(1)}, u32[]{:S(2)}, u32[]{:S(2)}) collective-permute-start(bf16[8,192,128]{2,1,0:T(8,128)(2,1)} %get-tuple-element.106), channel_id=1, source_target_pairs={{0,5},{1,4},{2,7},{3,6},{4,1},{5,0},{6,3},{7,2},{8,13},{9,12},{10,... | collective-permute-start | bytes 1179656 | tf_op jit(solution)/shard_map/ppermute | solution.py:221
  9.3 98.8 %collective-permute-start.6 = (bf16[8,192,128]{2,1,0:T(8,128)(2,1)}, bf16[8,192,128]{2,1,0:T(8,128)(2,1)S(1)}, u32[]{:S(2)}, u32[]{:S(2)}) collective-permute-start(bf16[8,192,128]{2,1,0:T(8,128)(2,1)} %get-tuple-element.108), channel_id=1, source_target_pairs={{0,4},{1,5},{2,6},{3,7},{4,0},{5,1},{6,2},{7,3},{8,12},{9,13},{10,... | collective-permute-start | bytes 1179656 | tf_op jit(solution)/shard_map/ppermute | solution.py:221
  81.9 25.1 %collective-permute-start.7 = (f32[16,128]{1,0:T(8,128)S(1)}, f32[16,128]{1,0:T(8,128)S(1)}, u32[]{:S(2)}, u32[]{:S(2)}) collective-permute-start(f32[16,128]{1,0:T(8,128)S(1)} %copy-done.30), channel_id=1, source_target_pairs={{0,4},{1,5},{2,6},{3,7},{4,0},{5,1},{6,2},{7,3},{8,12},{9,13},{10,... | collective-permute-start | bytes 24584 | tf_op jit(solution)/shard_map/ppermute | solution.py:221
  82.0 37.1 %collective-permute-start.8 = (bf16[8,192,128]{2,1,0:T(8,128)(2,1)}, bf16[8,192,128]{2,1,0:T(8,128)(2,1)S(1)}, u32[]{:S(2)}, u32[]{:S(2)}) collective-permute-start(bf16[8,192,128]{2,1,0:T(8,128)(2,1)} %get-tuple-element.111), channel_id=1, source_target_pairs={{0,6},{1,7},{2,4},{3,5},{4,2},{5,3},{6,0},{7,1},{8,14},{9,15},{10,... | collective-permute-start | bytes 1179656 | tf_op jit(solution)/shard_map/ppermute | solution.py:221
  86.0 18.1 %collective-permute-start.2 = (f32[4,128]{1,0:T(4,128)S(1)}, f32[4,128]{1,0:T(4,128)S(1)}, u32[]{:S(2)}, u32[]{:S(2)}) collective-permute-start(f32[4,128]{1,0:T(4,128)S(1)} %slice_reduce_fusion), channel_id=1, source_target_pairs={{0,1},{1,2},{2,3},{3,4},{4,5},{5,6},{6,7},{7,0},{8,9},{9,10},{10,1... | collective-permute-start | bytes 6152 | tf_op jit(solution)/shard_map/ppermute | solution.py:25
  108.1 22.9 %collective-permute-start.10 = (bf16[8,192,128]{2,1,0:T(8,128)(2,1)}, bf16[8,192,128]{2,1,0:T(8,128)(2,1)S(1)}, u32[]{:S(2)}, u32[]{:S(2)}) collective-permute-start(bf16[8,192,128]{2,1,0:T(8,128)(2,1)} %get-tuple-element.113), channel_id=1, source_target_pairs={{0,7},{1,6},{2,5},{3,4},{4,3},{5,2},{6,1},{7,0},{8,15},{9,14},{10,... | collective-permute-start | bytes 1179656 | tf_op jit(solution)/shard_map/ppermute | solution.py:221
  112.7 19.3 %collective-permute-start.11 = (bf16[8,192,128]{2,1,0:T(8,128)(2,1)}, bf16[8,192,128]{2,1,0:T(8,128)(2,1)S(1)}, u32[]{:S(2)}, u32[]{:S(2)}) collective-permute-start(bf16[8,192,128]{2,1,0:T(8,128)(2,1)} %get-tuple-element.114), channel_id=1, source_target_pairs={{0,2},{1,3},{2,0},{3,1},{4,6},{5,7},{6,4},{7,5},{8,10},{9,11},{10,... | collective-permute-start | bytes 1179656 | tf_op jit(solution)/shard_map/ppermute | solution.py:221
  115.8 27.7 %collective-permute-start.12 = (bf16[8,192,128]{2,1,0:T(8,128)(2,1)}, bf16[8,192,128]{2,1,0:T(8,128)(2,1)S(1)}, u32[]{:S(2)}, u32[]{:S(2)}) collective-permute-start(bf16[8,192,128]{2,1,0:T(8,128)(2,1)} %get-tuple-element.115), channel_id=1, source_target_pairs={{0,12},{1,13},{2,14},{3,15},{4,8},{5,9},{6,10},{7,11},{8,4},{9,5},... | collective-permute-start | bytes 1179656 | tf_op jit(solution)/shard_map/ppermute | solution.py:221
  119.1 32.8 %collective-permute-start.13 = (bf16[8,192,128]{2,1,0:T(8,128)(2,1)}, bf16[8,192,128]{2,1,0:T(8,128)(2,1)S(1)}, u32[]{:S(2)}, u32[]{:S(2)}) collective-permute-start(bf16[8,192,128]{2,1,0:T(8,128)(2,1)} %get-tuple-element.116), channel_id=1, source_target_pairs={{0,3},{1,2},{2,1},{3,0},{4,7},{5,6},{6,5},{7,4},{8,11},{9,10},{10,... | collective-permute-start | bytes 1179656 | tf_op jit(solution)/shard_map/ppermute | solution.py:221
  121.5 47.1 %collective-permute-start.14 = (bf16[8,192,128]{2,1,0:T(8,128)(2,1)}, bf16[8,192,128]{2,1,0:T(8,128)(2,1)S(1)}, u32[]{:S(2)}, u32[]{:S(2)}) collective-permute-start(bf16[8,192,128]{2,1,0:T(8,128)(2,1)} %get-tuple-element.117), channel_id=1, source_target_pairs={{0,13},{1,12},{2,15},{3,14},{4,9},{5,8},{6,11},{7,10},{8,5},{9,4},... | collective-permute-start | bytes 1179656 | tf_op jit(solution)/shard_map/ppermute | solution.py:221
  131.0 38.3 %collective-permute-start.15 = (bf16[8,192,128]{2,1,0:T(8,128)(2,1)}, bf16[8,192,128]{2,1,0:T(8,128)(2,1)S(1)}, u32[]{:S(2)}, u32[]{:S(2)}) collective-permute-start(bf16[8,192,128]{2,1,0:T(8,128)(2,1)} %get-tuple-element.118), channel_id=1, source_target_pairs={{0,8},{1,9},{2,10},{3,11},{4,12},{5,13},{6,14},{7,15},{8,0},{9,1},... | collective-permute-start | bytes 1179656 | tf_op jit(solution)/shard_map/ppermute | solution.py:221
  132.0 42.1 %collective-permute-start.16 = (bf16[8,192,128]{2,1,0:T(8,128)(2,1)}, bf16[8,192,128]{2,1,0:T(8,128)(2,1)S(1)}, u32[]{:S(2)}, u32[]{:S(2)}) collective-permute-start(bf16[8,192,128]{2,1,0:T(8,128)(2,1)} %get-tuple-element.119), channel_id=1, source_target_pairs={{0,9},{1,8},{2,11},{3,10},{4,13},{5,12},{6,15},{7,14},{8,1},{9,0},... | collective-permute-start | bytes 1179656 | tf_op jit(solution)/shard_map/ppermute | solution.py:221
  143.6 41.9 %collective-permute-start.17 = (bf16[8,192,128]{2,1,0:T(8,128)(2,1)}, bf16[8,192,128]{2,1,0:T(8,128)(2,1)S(1)}, u32[]{:S(2)}, u32[]{:S(2)}) collective-permute-start(bf16[8,192,128]{2,1,0:T(8,128)(2,1)} %get-tuple-element.120), channel_id=1, source_target_pairs={{0,14},{1,15},{2,12},{3,13},{4,10},{5,11},{6,8},{7,9},{8,6},{9,7},... | collective-permute-start | bytes 1179656 | tf_op jit(solution)/shard_map/ppermute | solution.py:221
  151.9 35.7 %collective-permute-start.18 = (bf16[8,192,128]{2,1,0:T(8,128)(2,1)}, bf16[8,192,128]{2,1,0:T(8,128)(2,1)S(1)}, u32[]{:S(2)}, u32[]{:S(2)}) collective-permute-start(bf16[8,192,128]{2,1,0:T(8,128)(2,1)} %get-tuple-element.121), channel_id=1, source_target_pairs={{0,10},{1,11},{2,8},{3,9},{4,14},{5,15},{6,12},{7,13},{8,2},{9,3},... | collective-permute-start | bytes 1179656 | tf_op jit(solution)/shard_map/ppermute | solution.py:221
  168.6 44.2 %collective-permute-start.19 = (bf16[8,192,128]{2,1,0:T(8,128)(2,1)}, bf16[8,192,128]{2,1,0:T(8,128)(2,1)S(1)}, u32[]{:S(2)}, u32[]{:S(2)}) collective-permute-start(bf16[8,192,128]{2,1,0:T(8,128)(2,1)} %get-tuple-element.122), channel_id=1, source_target_pairs={{0,15},{1,14},{2,13},{3,12},{4,11},{5,10},{6,9},{7,8},{8,7},{9,6},... | collective-permute-start | bytes 1179656 | tf_op jit(solution)/shard_map/ppermute | solution.py:221
  169.4 46.4 %collective-permute-start.20 = (bf16[8,192,128]{2,1,0:T(8,128)(2,1)}, bf16[8,192,128]{2,1,0:T(8,128)(2,1)S(1)}, u32[]{:S(2)}, u32[]{:S(2)}) collective-permute-start(bf16[8,192,128]{2,1,0:T(8,128)(2,1)} %get-tuple-element.123), channel_id=1, source_target_pairs={{0,11},{1,10},{2,9},{3,8},{4,15},{5,14},{6,13},{7,12},{8,3},{9,2},... | collective-permute-start | bytes 1179656 | tf_op jit(solution)/shard_map/ppermute | solution.py:221
  174.1 46.6 %collective-permute-start.21 = (bf16[8,192,128]{2,1,0:T(8,128)(2,1)}, bf16[8,192,128]{2,1,0:T(8,128)(2,1)S(1)}, u32[]{:S(2)}, u32[]{:S(2)}) collective-permute-start(bf16[8,192,128]{2,1,0:T(8,128)(2,1)} %get-tuple-element.124), channel_id=1, source_target_pairs={{0,20},{1,21},{2,22},{3,23},{4,16},{5,17},{6,18},{7,19},{8,28},{9,... | collective-permute-start | bytes 1179656 | tf_op jit(solution)/shard_map/ppermute | solution.py:221
  185.4 39.3 %collective-permute-start.22 = (bf16[8,192,128]{2,1,0:T(8,128)(2,1)}, bf16[8,192,128]{2,1,0:T(8,128)(2,1)S(1)}, u32[]{:S(2)}, u32[]{:S(2)}) collective-permute-start(bf16[8,192,128]{2,1,0:T(8,128)(2,1)} %get-tuple-element.125), channel_id=1, source_target_pairs={{0,16},{1,17},{2,18},{3,19},{4,20},{5,21},{6,22},{7,23},{8,24},{9,... | collective-permute-start | bytes 1179656 | tf_op jit(solution)/shard_map/ppermute | solution.py:221
  187.6 42.6 %collective-permute-start.23 = (bf16[8,192,128]{2,1,0:T(8,128)(2,1)}, bf16[8,192,128]{2,1,0:T(8,128)(2,1)S(1)}, u32[]{:S(2)}, u32[]{:S(2)}) collective-permute-start(bf16[8,192,128]{2,1,0:T(8,128)(2,1)} %get-tuple-element.126), channel_id=1, source_target_pairs={{0,21},{1,20},{2,23},{3,22},{4,17},{5,16},{6,19},{7,18},{8,29},{9,... | collective-permute-start | bytes 1179656 | tf_op jit(solution)/shard_map/ppermute | solution.py:221
  212.8 20.8 %collective-permute-start.24 = (bf16[8,192,128]{2,1,0:T(8,128)(2,1)}, bf16[8,192,128]{2,1,0:T(8,128)(2,1)S(1)}, u32[]{:S(2)}, u32[]{:S(2)}) collective-permute-start(bf16[8,192,128]{2,1,0:T(8,128)(2,1)} %get-tuple-element.127), channel_id=1, source_target_pairs={{0,17},{1,16},{2,19},{3,18},{4,21},{5,20},{6,23},{7,22},{8,25},{9,... | collective-permute-start | bytes 1179656 | tf_op jit(solution)/shard_map/ppermute | solution.py:221
  215.8 30.7 %collective-permute-start.25 = (bf16[8,192,128]{2,1,0:T(8,128)(2,1)}, bf16[8,192,128]{2,1,0:T(8,128)(2,1)S(1)}, u32[]{:S(2)}, u32[]{:S(2)}) collective-permute-start(bf16[8,192,128]{2,1,0:T(8,128)(2,1)} %get-tuple-element.128), channel_id=1, source_target_pairs={{0,18},{1,19},{2,16},{3,17},{4,22},{5,23},{6,20},{7,21},{8,26},{9,... | collective-permute-start | bytes 1179656 | tf_op jit(solution)/shard_map/ppermute | solution.py:221
  220.7 35.9 %collective-permute-start.26 = (bf16[8,192,128]{2,1,0:T(8,128)(2,1)}, bf16[8,192,128]{2,1,0:T(8,128)(2,1)S(1)}, u32[]{:S(2)}, u32[]{:S(2)}) collective-permute-start(bf16[8,192,128]{2,1,0:T(8,128)(2,1)} %get-tuple-element.129), channel_id=1, source_target_pairs={{0,22},{1,23},{2,20},{3,21},{4,18},{5,19},{6,16},{7,17},{8,30},{9,... | collective-permute-start | bytes 1179656 | tf_op jit(solution)/shard_map/ppermute | solution.py:221
  224.7 33.8 %collective-permute-start.27 = (bf16[8,192,128]{2,1,0:T(8,128)(2,1)}, bf16[8,192,128]{2,1,0:T(8,128)(2,1)S(1)}, u32[]{:S(2)}, u32[]{:S(2)}) collective-permute-start(bf16[8,192,128]{2,1,0:T(8,128)(2,1)} %get-tuple-element.130), channel_id=1, source_target_pairs={{0,19},{1,18},{2,17},{3,16},{4,23},{5,22},{6,21},{7,20},{8,27},{9,... | collective-permute-start | bytes 1179656 | tf_op jit(solution)/shard_map/ppermute | solution.py:221
  230.2 64.4 %collective-permute-start.28 = (bf16[8,192,128]{2,1,0:T(8,128)(2,1)S(1)}, bf16[8,192,128]{2,1,0:T(8,128)(2,1)S(1)}, u32[]{:S(2)}, u32[]{:S(2)}) collective-permute-start(bf16[8,192,128]{2,1,0:T(8,128)(2,1)S(1)} %copy-done.28), channel_id=1, source_target_pairs={{0,23},{1,22},{2,21},{3,20},{4,19},{5,18},{6,17},{7,16},{8,31},{9,... | collective-permute-start | bytes 1179656 | tf_op jit(solution)/shard_map/ppermute | solution.py:221
  233.7 63.9 %collective-permute-start.29 = (bf16[8,192,128]{2,1,0:T(8,128)(2,1)S(1)}, bf16[8,192,128]{2,1,0:T(8,128)(2,1)S(1)}, u32[]{:S(2)}, u32[]{:S(2)}) collective-permute-start(bf16[8,192,128]{2,1,0:T(8,128)(2,1)S(1)} %copy-done.27), channel_id=1, source_target_pairs={{0,24},{1,25},{2,26},{3,27},{4,28},{5,29},{6,30},{7,31},{8,16},{9,... | collective-permute-start | bytes 1179656 | tf_op jit(solution)/shard_map/ppermute | solution.py:221
  246.5 52.7 %collective-permute-start.30 = (bf16[8,192,128]{2,1,0:T(8,128)(2,1)S(1)}, bf16[8,192,128]{2,1,0:T(8,128)(2,1)S(1)}, u32[]{:S(2)}, u32[]{:S(2)}) collective-permute-start(bf16[8,192,128]{2,1,0:T(8,128)(2,1)S(1)} %copy-done.26), channel_id=1, source_target_pairs={{0,28},{1,29},{2,30},{3,31},{4,24},{5,25},{6,26},{7,27},{8,20},{9,... | collective-permute-start | bytes 1179656 | tf_op jit(solution)/shard_map/ppermute | solution.py:221
  256.5 50.6 %collective-permute-start.31 = (bf16[8,192,128]{2,1,0:T(8,128)(2,1)S(1)}, bf16[8,192,128]{2,1,0:T(8,128)(2,1)S(1)}, u32[]{:S(2)}, u32[]{:S(2)}) collective-permute-start(bf16[8,192,128]{2,1,0:T(8,128)(2,1)S(1)} %copy-done.25), channel_id=1, source_target_pairs={{0,25},{1,24},{2,27},{3,26},{4,29},{5,28},{6,31},{7,30},{8,17},{9,... | collective-permute-start | bytes 1179656 | tf_op jit(solution)/shard_map/ppermute | solution.py:221
  258.5 56.6 %collective-permute-start.32 = (bf16[8,192,128]{2,1,0:T(8,128)(2,1)S(1)}, bf16[8,192,128]{2,1,0:T(8,128)(2,1)S(1)}, u32[]{:S(2)}, u32[]{:S(2)}) collective-permute-start(bf16[8,192,128]{2,1,0:T(8,128)(2,1)S(1)} %copy-done.24), channel_id=1, source_target_pairs={{0,29},{1,28},{2,31},{3,30},{4,25},{5,24},{6,27},{7,26},{8,21},{9,... | collective-permute-start | bytes 1179656 | tf_op jit(solution)/shard_map/ppermute | solution.py:221
  294.6 21.3 %collective-permute-start.33 = (bf16[8,192,128]{2,1,0:T(8,128)(2,1)S(1)}, bf16[8,192,128]{2,1,0:T(8,128)(2,1)S(1)}, u32[]{:S(2)}, u32[]{:S(2)}) collective-permute-start(bf16[8,192,128]{2,1,0:T(8,128)(2,1)S(1)} %copy-done.23), channel_id=1, source_target_pairs={{0,26},{1,27},{2,24},{3,25},{4,30},{5,31},{6,28},{7,29},{8,18},{9,... | collective-permute-start | bytes 1179656 | tf_op jit(solution)/shard_map/ppermute | solution.py:221
  297.6 23.1 %collective-permute-start.34 = (bf16[8,192,128]{2,1,0:T(8,128)(2,1)S(1)}, bf16[8,192,128]{2,1,0:T(8,128)(2,1)S(1)}, u32[]{:S(2)}, u32[]{:S(2)}) collective-permute-start(bf16[8,192,128]{2,1,0:T(8,128)(2,1)S(1)} %copy-done.22), channel_id=1, source_target_pairs={{0,27},{1,26},{2,25},{3,24},{4,31},{5,30},{6,29},{7,28},{8,19},{9,... | collective-permute-start | bytes 1179656 | tf_op jit(solution)/shard_map/ppermute | solution.py:221
  299.2 34.8 %collective-permute-start.35 = (bf16[8,192,128]{2,1,0:T(8,128)(2,1)S(1)}, bf16[8,192,128]{2,1,0:T(8,128)(2,1)S(1)}, u32[]{:S(2)}, u32[]{:S(2)}) collective-permute-start(bf16[8,192,128]{2,1,0:T(8,128)(2,1)S(1)} %copy-done.21), channel_id=1, source_target_pairs={{0,30},{1,31},{2,28},{3,29},{4,26},{5,27},{6,24},{7,25},{8,22},{9,... | collective-permute-start | bytes 1179656 | tf_op jit(solution)/shard_map/ppermute | solution.py:221
  307.1 37.4 %collective-permute-start.36 = (bf16[8,192,128]{2,1,0:T(8,128)(2,1)S(1)}, bf16[8,192,128]{2,1,0:T(8,128)(2,1)S(1)}, u32[]{:S(2)}, u32[]{:S(2)}) collective-permute-start(bf16[8,192,128]{2,1,0:T(8,128)(2,1)S(1)} %copy-done.20), channel_id=1, source_target_pairs={{0,31},{1,30},{2,29},{3,28},{4,27},{5,26},{6,25},{7,24},{8,23},{9,... | collective-permute-start | bytes 1179656 | tf_op jit(solution)/shard_map/ppermute | solution.py:221
  (36 other events, 1622.8 us)

commit v2 on v1

--- a/solution.py
+++ b/solution.py
@@ -27,16 +27,17 @@
 
 def partner_order(gx_count, gy_count):
     devices = gx_count * gy_count
-    far = [k for k in range(1, devices) if k & (gy_count // 2)]
-    near = [k for k in range(1, devices) if not k & (gy_count // 2)]
-    order, taken = list(far[:2]), 0
-    for place, k in enumerate(far[2:]):
-        order.append(k)
-        want = (place + 1) * len(near) // max(1, len(far) - 4)
-        while taken < min(want, len(near)):
-            order.append(near[taken])
-            taken += 1
-    return order + near[taken:]
+    far_bit, row_bit, col_bit = gy_count // 2, 1, devices // 2
+    turns = lambda k: (bool(k & (far_bit // 2)), bool(k & row_bit), bool(k & col_bit), k)
+    far = sorted([k for k in range(1, devices) if k & far_bit], key=turns)
+    near = [k for k in range(1, devices) if not k & far_bit]
+    near.sort(key=lambda k: (not k & row_bit, not k & col_bit, k))
+    order, spare = far[:RAW], max(0, len(near) - len(far) + RAW)
+    for place, k in enumerate(far[RAW:]):
+        take = 2 if place < spare else 1
+        order += [k] + near[:take]
+        near = near[take:]
+    return order + near
 
 
 def partner_groups(order):
@@ -44,8 +45,55 @@
     return [todo[:2]] + [todo[i : i + GROUP] for i in range(2, len(todo), GROUP)]
 
 
-def route_kernel(capacity, raw, me_ref, owner_ref, face_ref, states_ref, table_ref, ids_ref, *rest):
-    out_refs, (count_ref, buffer, in_sem, out_sem) = rest[: len(raw)], rest[len(raw) :]
+def block_copies(turns, capacity, slot_of, states_ref, out_refs, buffer, in_sem, out_sem, between=None):
+    def fetch(turn, i):
+        return pltpu.make_async_copy(states_ref.at[slot_of(turn, i)], buffer.at[turn, i], in_sem.at[turn, i])
+
+    def send(turn, i):
+        return pltpu.make_async_copy(buffer.at[turn, i], out_refs[turn].at[i], out_sem.at[turn, i])
+
+    steps = [(turn, i) for turn in range(turns) for i in range(capacity)]
+    for step in steps:
+        fetch(*step).start()
+    if between is not None:
+        between()
+    for step in steps:
+        fetch(*step).wait()
+        send(*step).start()
+    for step in steps:
+        send(*step).wait()
+
+
+def first_kernel(capacity, partner, me_ref, owner_ref, macro_ref, states_ref, out_ref, row_ref, col_ref, *scratch):
+    slot_ref, macro_buffer, macro_sem, *gather = scratch
+    slot_total = owner_ref.shape[0]
+    owner = jnp.bitwise_xor(me_ref[0], partner)
+    fields = pltpu.make_async_copy(macro_ref, macro_buffer, macro_sem)
+    fields.start()
+
+    def look(slot, found):
+        slot_ref[found] = slot
+        return found + (owner_ref[slot] == owner).astype(jnp.int32)
+
+    lax.fori_loop(0, slot_total, look, jnp.int32(0), unroll=8)
+
+    def edges():
+        fields.wait()
+        channels, _, tile_rows = macro_buffer.shape
+        pick = (lax.broadcasted_iota(jnp.int32, (8, tile_rows), 1) == 0).astype(jnp.float32)
+        for channel in range(channels):
+            field = macro_buffer[channel]
+            col_ref[channel : channel + 1, :] = field[0:1, :]
+            rows = lax.dot_general(
+                pick, field, (((1,), (1,)), ((), ())), precision=HIGHEST, preferred_element_type=jnp.float32
+            )
+            row_ref[channel : channel + 1, :] = rows[0:1, :]
+
+    block_copies(1, capacity, lambda turn, i: slot_ref[i], states_ref, [out_ref], *gather, between=edges)
+
+
+def route_kernel(capacity, partners, me_ref, owner_ref, face_ref, states_ref, table_ref, ids_ref, *rest):
+    out_refs, (count_ref, buffer, in_sem, out_sem) = rest[: len(partners)], rest[len(partners) :]
     slot_total = owner_ref.shape[0]
     me = me_ref[0]
 
@@ -65,46 +113,34 @@
         return carry
 
     lax.fori_loop(0, slot_total, place, 0, unroll=8)
-
-    def fetch(turn, i):
-        slot = table_ref[raw[turn] * capacity + i]
-        return pltpu.make_async_copy(states_ref.at[slot], buffer.at[turn, i], in_sem.at[turn, i])
-
-    def send(turn, i):
-        return pltpu.make_async_copy(buffer.at[turn, i], out_refs[turn].at[i], out_sem.at[turn, i])
-
-    steps = [(turn, i) for turn in range(len(raw)) for i in range(capacity)]
-    for step in steps:
-        fetch(*step).start()
-    for step in steps:
-        fetch(*step).wait()
-        send(*step).start()
-    for step in steps:
-        send(*step).wait()
-
-
-def forcing_kernel(capacity, raw, macro_ref, row_ref, col_ref, place_ref, lift_ref, force_ref, live_ref, *out_refs):
-    channels, tile_rows, tile_cols = macro_ref.shape
+    slot_of = lambda turn, i: table_ref[partners[turn] * capacity + i]
+    block_copies(len(partners), capacity, slot_of, states_ref, out_refs, buffer, in_sem, out_sem)
+
+
+def forcing_kernel(
+    capacity, raw, macro_ref, row_ref, col_ref, place_ref, lift_ref, force_ref, live_ref, *out_refs
+):
+    channels, tile_cols, tile_rows = macro_ref.shape
     slot_total = place_ref.shape[0]
     place = place_ref[...]
     left_row, left_col, right_row, right_col, live = [place[:, i : i + 1] for i in range(5)]
     row_iota = lax.broadcasted_iota(jnp.int32, (slot_total, tile_rows), 1)
     col_iota = lax.broadcasted_iota(jnp.int32, (slot_total, tile_cols), 1)
-    left_pick = (row_iota == left_row).astype(jnp.float32)
-    right_pick = (row_iota == right_row).astype(jnp.float32)
-    left_mask = col_iota == left_col
-    right_mask = col_iota == right_col
-    edge_row = right_mask & (right_row == tile_rows)
-    edge_col = (row_iota == right_row) & (right_col == tile_cols)
+    left_pick = (col_iota == left_col).astype(jnp.float32)
+    right_pick = (col_iota == right_col).astype(jnp.float32)
+    left_mask = row_iota == left_row
+    right_mask = row_iota == right_row
+    edge_row = (col_iota == right_col) & (right_row == tile_rows)
+    edge_col = right_mask & (right_col == tile_cols)
     total = jnp.zeros((slot_total, lift_ref.shape[1]), jnp.float32)
     for channel in range(channels):
         block = macro_ref[channel]
         left = jnp.dot(left_pick, block, precision=HIGHEST, preferred_element_type=jnp.float32)
         left = jnp.sum(jnp.where(left_mask, left, 0.0), axis=1, keepdims=True)
         right = jnp.dot(right_pick, block, precision=HIGHEST, preferred_element_type=jnp.float32)
-        right = jnp.where(right_mask, right, 0.0) + jnp.where(edge_row, row_ref[channel : channel + 1, :], 0.0)
+        right = jnp.where(right_mask, right, 0.0) + jnp.where(edge_col, col_ref[channel : channel + 1, :], 0.0)
         right = jnp.sum(right, axis=1, keepdims=True)
-        beyond = jnp.where(edge_col, col_ref[channel : channel + 1, :], 0.0)
+        beyond = jnp.where(edge_row, row_ref[channel : channel + 1, :], 0.0)
         right = right + jnp.sum(beyond, axis=1, keepdims=True)
         total = total + left * lift_ref[channel : channel + 1, :]
         total = total + right * lift_ref[channels + channel : channels + channel + 1, :]
@@ -174,6 +210,22 @@
     copy = pltpu.make_async_copy(buffer, out_ref.at[source_ref[0]], out_sem)
     copy.start()
     copy.wait()
+
+
+def put_kernel(partners, me_ref, *rest):
+    got_refs, (_, out_ref, buffer, in_sem, out_sem) = rest[: len(partners)], rest[len(partners) :]
+    places = [jnp.bitwise_xor(me_ref[0], k) for k in partners]
+    fetches = [pltpu.make_async_copy(got_refs[i], buffer.at[i], in_sem.at[i]) for i in range(len(partners))]
+    sends = [
+        pltpu.make_async_copy(buffer.at[i], out_ref.at[place], out_sem.at[i]) for i, place in enumerate(places)
+    ]
+    for fetch in fetches:
+        fetch.start()
+    for fetch, send in zip(fetches, sends):
+        fetch.wait()
+        send.start()
+    for send in sends:
+        send.wait()
 
 
 def flux_kernel(members, sums_ref, readout_ref, place_ref, place_row_ref, flux_ref, hit_ref):
@@ -221,27 +273,46 @@
         return lax.ppermute(value, ("gx", "gy"), [(source, source ^ k) for source in range(devices)])
 
     slots_smem = jax.ShapeDtypeStruct((slot_total,), jnp.int32)
-    table, ids, *raw_sent = pl.pallas_call(
-        functools.partial(route_kernel, capacity, raw),
-        out_shape=[slots_smem, slots_smem] + [block] * len(raw),
-        in_specs=[SMEM, SMEM, SMEM, ANY],
-        out_specs=[SMEM, SMEM] + [ANY] * len(raw),
+
+    def gather_scratch(count):
+        return [
+            pltpu.VMEM((count, capacity, members, state_width), jnp.bfloat16),
+            pltpu.SemaphoreType.DMA((count, capacity)),
+            pltpu.SemaphoreType.DMA((count, capacity)),
+        ]
+
+    fields = jnp.transpose(macro_state, (0, 2, 1))
+    raw_first, first_row, first_col = pl.pallas_call(
+        functools.partial(first_kernel, capacity, raw[0]),
+        out_shape=[
+            block,
+            jax.ShapeDtypeStruct((channels, tile_cols), jnp.float32),
+            jax.ShapeDtypeStruct((channels, tile_rows), jnp.float32),
+        ],
+        in_specs=[SMEM, SMEM, ANY, ANY],
+        out_specs=[ANY, VMEM, VMEM],
         scratch_shapes=[
-            pltpu.SMEM((devices,), jnp.int32),
-            pltpu.VMEM((len(raw), capacity, members, state_width), jnp.bfloat16),
-            pltpu.SemaphoreType.DMA((len(raw), capacity)),
-            pltpu.SemaphoreType.DMA((len(raw), capacity)),
-        ],
-        name="route",
-    )(me_ref, owner.reshape(slot_total), faces, states)
-
-    raw_got = []
-    for turn, k in enumerate(raw):
-        raw_got.append(exchanged(raw_sent[turn], k))
-
-    first_row, first_col, table = lax.optimization_barrier((macro_state[:, 0, :], macro_state[:, :, 0], table))
+            pltpu.SMEM((slot_total,), jnp.int32),
+            pltpu.VMEM(fields.shape, jnp.float32),
+            pltpu.SemaphoreType.DMA,
+        ]
+        + gather_scratch(1),
+        name="first",
+    )(me_ref, owner.reshape(slot_total), fields, states)
+    owners, raw_first = lax.optimization_barrier((owner.reshape(slot_total), raw_first))
     next_row = passed_along(first_row, "gx", -1)
     next_col = passed_along(first_col, "gy", -1)
+    raw_got = [exchanged(raw_first, raw[0])]
+    table, ids, *raw_sent = pl.pallas_call(
+        functools.partial(route_kernel, capacity, raw[1:]),
+        out_shape=[slots_smem, slots_smem] + [block] * (RAW - 1),
+        in_specs=[SMEM, SMEM, SMEM, ANY],
+        out_specs=[SMEM, SMEM] + [ANY] * (RAW - 1),
+        scratch_shapes=[pltpu.SMEM((devices,), jnp.int32)] + gather_scratch(RAW - 1),
+        name="route",
+    )(me_ref, owners, faces, states)
+    for turn, k in enumerate(raw[1:]):
+        raw_got.append(exchanged(raw_sent[turn], k))
 
     live = ids >= 0
     safe = jnp.where(live, ids, 0)
@@ -260,7 +331,7 @@
         in_specs=[VMEM] * 5,
         out_specs=[VMEM] * (2 + len(raw)),
         name="forcing",
-    )(macro_state, next_row, next_col, place_cols, lift_weight)
+    )(fields, next_row, next_col, place_cols, lift_weight)
 
     force_got = []
     for turn, k in enumerate(raw):
@@ -310,13 +381,6 @@
     south_flux = jnp.where(hit[1] > 0.5, face_flux[1], diffusion * (macro_state - beyond_row))
     west_flux = passed_along(east_flux[:, :, -1], "gy", 1)
     north_flux = passed_along(south_flux[:, -1, :], "gx", 1)
-    macro_next = macro_state - time_step * (
-        east_flux
-        - jnp.concatenate([west_flux[:, :, None], east_flux[:, :, :-1]], axis=2)
-        + south_flux
-        - jnp.concatenate([north_flux[:, None, :], south_flux[:, :-1, :]], axis=1)
-    )
-
     out = relaxed[0]
     for turn, k in enumerate(raw):
         out = pl.pallas_call(
@@ -330,8 +394,33 @@
             ],
             input_output_aliases={4: 0},
         )(jnp.bitwise_xor(me_ref, k), raw_got[turn], force_got[turn], micro_weight, out)
-    for k in order[RAW:]:
-        out = lax.dynamic_update_slice(out, got[k][None], (jnp.bitwise_xor(me, k), 0, 0, 0))
+
+    def put(out, partners):
+        return pl.pallas_call(
+            functools.partial(put_kernel, partners),
+            out_shape=whole,
+            in_specs=[SMEM] + [ANY] * (len(partners) + 1),
+            out_specs=ANY,
+            scratch_shapes=[
+                pltpu.VMEM((len(partners), capacity, members, state_width), jnp.bfloat16),
+                pltpu.SemaphoreType.DMA((len(partners),)),
+                pltpu.SemaphoreType.DMA((len(partners),)),
+            ],
+            input_output_aliases={len(partners) + 1: 0},
+        )(me_ref, *[got[k] for k in partners], out)
+
+    landings = [order[i : i + GROUP] for i in range(RAW, devices - 1, GROUP)]
+    for partners in landings[:-1]:
+        out = put(out, partners)
+    out, west_flux, north_flux = lax.optimization_barrier((out, west_flux, north_flux))
+    macro_next = macro_state - time_step * (
+        east_flux
+        - jnp.concatenate([west_flux[:, :, None], east_flux[:, :, :-1]], axis=2)
+        + south_flux
+        - jnp.concatenate([north_flux[:, None, :], south_flux[:, :-1, :]], axis=1)
+    )
+    out, macro_next = lax.optimization_barrier((out, macro_next))
+    out = put(out, landings[-1])
     return macro_next, out.reshape(1, 1, devices, capacity, members, state_width)
 
 

time: 348 us -> 360 us (1.034)
  the two profiles are of different devices: /device:TPU:20 before, /device:TPU:7 now
where the time goes in v2:
time: 360 us; the launch traced here: 359 us
  starting transfers between devices  170 us (47%)
  Pallas kernels  91.4 us (25%)
  waiting for transfers between devices  83.2 us (23%)
  local copies, waits for them, and re-layouts  8.4 us (2%)
  other arithmetic  4.23 us (1%)
    ppermute x33, starting transfers between devices, exchanged(): lax.ppermute(value, ('gx', 'gy'), [(source, source ^ k) for source in ran...  163 us
    ppermute x33, waiting for transfers between devices, exchanged(): lax.ppermute(value, ('gx', 'gy'), [(source, source ^ k) for source in ran...  83.2 us
    pallas_call x9, Pallas kernels, per_device(): pl.pallas_call(functools.partial(relax_kernel, capacity, partners, kept,...  54.6 us
    pallas_call x8, Pallas kernels, put(): pl.pallas_call(functools.partial(put_kernel, partners), out_shape=whole,...  17.2 us
  transfers between devices with their start and end apart: 37, of which 9 were waited for; matrix products, arithmetic and copies ran while one was open for 3% of the time, Pallas kernels for 24%

profile of v2, /device:TPU:7, one launch (start us, length us, event | category | flops | bytes accessed | tf_op | source)
XLA Modules:
  0.0 358.8 jit_solution(12988805923825280587)
XLA Ops:
  0.7 3.8 %first.1 = (bf16[8,192,128]{2,1,0:T(8,128)(2,1)}, f32[4,64]{1,0:T(4,128)}, f32[4,128]{1,0:T(4,128)}) custom-call(s32[1]{0:T(128)} %bitcast.me_ref, s32[256]{0:T(256)} %bitcast.73, f32[4,64,128]{2,1,0:T(8,128)} %bitcast.53, bf16[256,192,128]{2,1,0:T(8,128)(2,1)} %bitcast.39), custom_call_target="tpu_custom_call" | custom-call | tf_op jit(solution)/shard_map/first/pallas_call | solution.py:285
  5.4 4.7 %route.1 = (s32[256]{0:T(256)}, s32[256]{0:T(256)}, bf16[8,192,128]{2,1,0:T(8,128)(2,1)}) custom-call(s32[1]{0:T(128)} %bitcast.me_ref, s32[256]{0:T(256)} %bitcast.74, s32[256]{0:T(256)} %bitcast.78, bf16[256,192,128]{2,1,0:T(8,128)(2,1)} %bitcast.40), custom_call_target="tpu_custom_call" | custom-call | tf_op jit(solution)/shard_map/route/pallas_call | solution.py:306
  17.8 2.9 forcing.1
  20.7 4.9 %shard_map.86 = (bf16[8,192,128]{2,1,0:T(8,128)(2,1)}, bf16[8,192,128]{2,1,0:T(8,128)(2,1)}, f32[16,128]{1,0:T(8,128)}) custom-call(s32[1]{0:T(128)} %bitcast.me_ref, s32[256]{0:T(256)} %get-tuple-element.132.table_ref, bf16[256,192,128]{2,1,0:T(8,128)(2,1)} %bitcast.41, f32[256,128]{1,0:T(8,128)} %get-tuple-element.83.force_ref, ...), custom_call_target="tpu_custom_call" | custom-call | tf_op jit(solution)/shard_map/pallas_call | solution.py:344
  25.7 6.4 %shard_map.87 = (bf16[8,192,128]{2,1,0:T(8,128)(2,1)}, bf16[8,192,128]{2,1,0:T(8,128)(2,1)}, bf16[8,192,128]{2,1,0:T(8,128)(2,1)}, bf16[8,192,128]{2,1,0:T(8,128)(2,1)}, f32[32,128]{1,0:T(8,128)}) custom-call(s32[1]{0:T(128)} %bitcast.me_ref, s32[256]{0:T(256)} %get-tuple-element.132.table_ref, bf16[256,192,128]{2,1,0:T(8,128)(2,1)} %bitcast.42, ...), custom_call_target="tpu_custom_call" | custom-call | tf_op jit(solution)/shard_map/pallas_call | solution.py:344
  32.1 6.5 %shard_map.88 = (bf16[8,192,128]{2,1,0:T(8,128)(2,1)}, bf16[8,192,128]{2,1,0:T(8,128)(2,1)}, bf16[8,192,128]{2,1,0:T(8,128)(2,1)}, bf16[8,192,128]{2,1,0:T(8,128)(2,1)}, f32[32,128]{1,0:T(8,128)}) custom-call(s32[1]{0:T(128)} %bitcast.me_ref, s32[256]{0:T(256)} %get-tuple-element.132.table_ref, bf16[256,192,128]{2,1,0:T(8,128)(2,1)} %bitcast.43, ...), custom_call_target="tpu_custom_call" | custom-call | tf_op jit(solution)/shard_map/pallas_call | solution.py:344
  38.6 6.7 %shard_map.89 = (bf16[8,192,128]{2,1,0:T(8,128)(2,1)}, bf16[8,192,128]{2,1,0:T(8,128)(2,1)}, bf16[8,192,128]{2,1,0:T(8,128)(2,1)}, bf16[8,192,128]{2,1,0:T(8,128)(2,1)}, f32[32,128]{1,0:T(8,128)}) custom-call(s32[1]{0:T(128)} %bitcast.me_ref, s32[256]{0:T(256)} %get-tuple-element.132.table_ref, bf16[256,192,128]{2,1,0:T(8,128)(2,1)} %bitcast.44, ...), custom_call_target="tpu_custom_call" | custom-call | tf_op jit(solution)/shard_map/pallas_call | solution.py:344
  45.3 6.5 %shard_map.90 = (bf16[8,192,128]{2,1,0:T(8,128)(2,1)}, bf16[8,192,128]{2,1,0:T(8,128)(2,1)}, bf16[8,192,128]{2,1,0:T(8,128)(2,1)}, bf16[8,192,128]{2,1,0:T(8,128)(2,1)}, f32[32,128]{1,0:T(8,128)}) custom-call(s32[1]{0:T(128)} %bitcast.me_ref, s32[256]{0:T(256)} %get-tuple-element.132.table_ref, bf16[256,192,128]{2,1,0:T(8,128)(2,1)} %bitcast.45, ...), custom_call_target="tpu_custom_call" | custom-call | tf_op jit(solution)/shard_map/pallas_call | solution.py:344
  51.8 6.5 %shard_map.91 = (bf16[8,192,128]{2,1,0:T(8,128)(2,1)}, bf16[8,192,128]{2,1,0:T(8,128)(2,1)}, bf16[8,192,128]{2,1,0:T(8,128)(2,1)}, bf16[8,192,128]{2,1,0:T(8,128)(2,1)}, f32[32,128]{1,0:T(8,128)}) custom-call(s32[1]{0:T(128)} %bitcast.me_ref, s32[256]{0:T(256)} %get-tuple-element.132.table_ref, bf16[256,192,128]{2,1,0:T(8,128)(2,1)} %bitcast.46, ...), custom_call_target="tpu_custom_call" | custom-call | tf_op jit(solution)/shard_map/pallas_call | solution.py:344
  58.3 6.4 %shard_map.92 = (bf16[8,192,128]{2,1,0:T(8,128)(2,1)}, bf16[8,192,128]{2,1,0:T(8,128)(2,1)}, bf16[8,192,128]{2,1,0:T(8,128)(2,1)}, bf16[8,192,128]{2,1,0:T(8,128)(2,1)}, f32[32,128]{1,0:T(8,128)}) custom-call(s32[1]{0:T(128)} %bitcast.me_ref, s32[256]{0:T(256)} %get-tuple-element.132.table_ref, bf16[256,192,128]{2,1,0:T(8,128)(2,1)} %bitcast.47, ...), custom_call_target="tpu_custom_call" | custom-call | tf_op jit(solution)/shard_map/pallas_call | solution.py:344
  66.2 5.8 %shard_map.93 = (bf16[8,192,128]{2,1,0:T(8,128)(2,1)}, bf16[8,192,128]{2,1,0:T(8,128)(2,1)}, bf16[8,192,128]{2,1,0:T(8,128)(2,1)}, f32[32,128]{1,0:T(8,128)}) custom-call(s32[1]{0:T(128)} %bitcast.me_ref, s32[256]{0:T(256)} %get-tuple-element.132.table_ref, bf16[256,192,128]{2,1,0:T(8,128)(2,1)} %bitcast.48, f32[256,128]{1,0:T(8,128)} %get-tuple-element.83.force_ref, ...), custom_call_target="tpu_custom_call" | custom-call | tf_op jit(solution)/shard_map/pallas_call | solution.py:344
  72.0 3.2 collective-permute-start.31
  75.3 4.9 %shard_map.94 = (bf16[32,8,192,128]{3,2,1,0:T(8,128)(2,1)}, f32[16,128]{1,0:T(8,128)}) custom-call(s32[1]{0:T(128)} %bitcast.me_ref, s32[256]{0:T(256)} %get-tuple-element.132.table_ref, bf16[256,192,128]{2,1,0:T(8,128)(2,1)} %bitcast.49, f32[256,128]{1,0:T(8,128)} %get-tuple-element.83.force_ref, f32[256,128]{1,0:T(8,128)} %get-tuple-element.84.live_ref, ...), custom_call_target="tpu_custom_call" | custom-call | tf_op jit(solution)/shard_map/pallas_call | solution.py:344
  81.8 4.8 %collective-permute-start.3 = (bf16[8,192,128]{2,1,0:T(8,128)(2,1)}, bf16[8,192,128]{2,1,0:T(8,128)(2,1)S(1)}, u32[]{:S(2)}, u32[]{:S(2)}) collective-permute-start(bf16[8,192,128]{2,1,0:T(8,128)(2,1)} %get-tuple-element.98), channel_id=1, source_target_pairs={{0,23},{1,22},{2,21},{3,20},{4,19},{5,18},{6,17},{7,16},{8,31},{9,... | collective-permute-start | bytes 1179656 | tf_op jit(solution)/shard_map/ppermute | solution.py:273
  88.7 4.0 %collective-permute-start.9 = (bf16[8,192,128]{2,1,0:T(8,128)(2,1)}, bf16[8,192,128]{2,1,0:T(8,128)(2,1)S(1)}, u32[]{:S(2)}, u32[]{:S(2)}) collective-permute-start(bf16[8,192,128]{2,1,0:T(8,128)(2,1)} %get-tuple-element.106), channel_id=1, source_target_pairs={{0,15},{1,14},{2,13},{3,12},{4,11},{5,10},{6,9},{7,8},{8,7},{9,6},... | collective-permute-start | bytes 1179656 | tf_op jit(solution)/shard_map/ppermute | solution.py:273
  92.6 3.3 collective-permute-done.3.rest_1_
  97.4 8.1 %collective-permute-done.6.rest_0_ = bf16[8,192,128]{2,1,0:T(8,128)(2,1)S(1)} collective-permute-done((bf16[8,192,128]{2,1,0:T(8,128)(2,1)}, bf16[8,192,128]{2,1,0:T(8,128)(2,1)S(1)}, u32[]{:S(2)}, u32[]{:S(2)}) %collective-permute-start.6) | collective-permute-done | bytes 393248 | tf_op jit(solution)/shard_map/ppermute | solution.py:273
  107.6 33.4 %collective-permute-start.12 = (bf16[8,192,128]{2,1,0:T(8,128)(2,1)}, bf16[8,192,128]{2,1,0:T(8,128)(2,1)}, u32[]{:S(2)}, u32[]{:S(2)}) collective-permute-start(bf16[8,192,128]{2,1,0:T(8,128)(2,1)} %get-tuple-element.109), channel_id=1, source_target_pairs={{0,18},{1,19},{2,16},{3,17},{4,22},{5,23},{6,20},{7,21},{8,26},{9,... | collective-permute-start | bytes 1179656 | tf_op jit(solution)/shard_map/ppermute | solution.py:273
  141.0 4.7 %collective-permute-start.13 = (bf16[8,192,128]{2,1,0:T(8,128)(2,1)}, bf16[8,192,128]{2,1,0:T(8,128)(2,1)}, u32[]{:S(2)}, u32[]{:S(2)}) collective-permute-start(bf16[8,192,128]{2,1,0:T(8,128)(2,1)} %get-tuple-element.110), channel_id=1, source_target_pairs={{0,30},{1,31},{2,28},{3,29},{4,26},{5,27},{6,24},{7,25},{8,22},{9,... | collective-permute-start | bytes 1179656 | tf_op jit(solution)/shard_map/ppermute | solution.py:273
  148.7 30.0 %collective-permute-start.16 = (bf16[8,192,128]{2,1,0:T(8,128)(2,1)}, bf16[8,192,128]{2,1,0:T(8,128)(2,1)}, u32[]{:S(2)}, u32[]{:S(2)}) collective-permute-start(bf16[8,192,128]{2,1,0:T(8,128)(2,1)} %get-tuple-element.113), channel_id=1, source_target_pairs={{0,11},{1,10},{2,9},{3,8},{4,15},{5,14},{6,13},{7,12},{8,3},{9,2},... | collective-permute-start | bytes 1179656 | tf_op jit(solution)/shard_map/ppermute | solution.py:273
  181.3 8.6 %collective-permute-start.19 = (bf16[8,192,128]{2,1,0:T(8,128)(2,1)}, bf16[8,192,128]{2,1,0:T(8,128)(2,1)}, u32[]{:S(2)}, u32[]{:S(2)}) collective-permute-start(bf16[8,192,128]{2,1,0:T(8,128)(2,1)} %get-tuple-element.116), channel_id=1, source_target_pairs={{0,21},{1,20},{2,23},{3,22},{4,17},{5,16},{6,19},{7,18},{8,29},{9,... | collective-permute-start | bytes 1179656 | tf_op jit(solution)/shard_map/ppermute | solution.py:273
  189.9 22.1 %collective-permute-start.20 = (bf16[8,192,128]{2,1,0:T(8,128)(2,1)}, bf16[8,192,128]{2,1,0:T(8,128)(2,1)}, u32[]{:S(2)}, u32[]{:S(2)}) collective-permute-start(bf16[8,192,128]{2,1,0:T(8,128)(2,1)} %get-tuple-element.117), channel_id=1, source_target_pairs={{0,3},{1,2},{2,1},{3,0},{4,7},{5,6},{6,5},{7,4},{8,11},{9,10},{10,... | collective-permute-start | bytes 1179656 | tf_op jit(solution)/shard_map/ppermute | solution.py:273
  215.3 7.7 %collective-permute-start.23 = (bf16[8,192,128]{2,1,0:T(8,128)(2,1)}, bf16[8,192,128]{2,1,0:T(8,128)(2,1)}, u32[]{:S(2)}, u32[]{:S(2)}) collective-permute-start(bf16[8,192,128]{2,1,0:T(8,128)(2,1)} %get-tuple-element.120), channel_id=1, source_target_pairs={{0,5},{1,4},{2,7},{3,6},{4,1},{5,0},{6,3},{7,2},{8,13},{9,12},{10,... | collective-permute-start | bytes 1179656 | tf_op jit(solution)/shard_map/ppermute | solution.py:273
  222.9 19.0 %collective-permute-done.19.rest_1_ = bf16[8,192,128]{2,1,0:T(8,128)(2,1)} collective-permute-done((bf16[8,192,128]{2,1,0:T(8,128)(2,1)}, bf16[8,192,128]{2,1,0:T(8,128)(2,1)}, u32[]{:S(2)}, u32[]{:S(2)}) %collective-permute-start.19) | collective-permute-done | bytes 393248 | tf_op jit(solution)/shard_map/ppermute | solution.py:273
  241.9 3.6 collective-permute-start.24
  245.5 5.4 %collective-permute-start.25 = (bf16[8,192,128]{2,1,0:T(8,128)(2,1)}, bf16[8,192,128]{2,1,0:T(8,128)(2,1)}, u32[]{:S(2)}, u32[]{:S(2)}) collective-permute-start(bf16[8,192,128]{2,1,0:T(8,128)(2,1)} %get-tuple-element.122), channel_id=1, source_target_pairs={{0,13},{1,12},{2,15},{3,14},{4,9},{5,8},{6,11},{7,10},{8,5},{9,4},... | collective-permute-start | bytes 1179656 | tf_op jit(solution)/shard_map/ppermute | solution.py:273
  256.9 3.3 flux.1
  260.2 12.3 %collective-permute-done.23.rest_1_ = bf16[8,192,128]{2,1,0:T(8,128)(2,1)} collective-permute-done((bf16[8,192,128]{2,1,0:T(8,128)(2,1)}, bf16[8,192,128]{2,1,0:T(8,128)(2,1)}, u32[]{:S(2)}, u32[]{:S(2)}) %collective-permute-start.23) | collective-permute-done | bytes 393248 | tf_op jit(solution)/shard_map/ppermute | solution.py:273
  275.0 10.4 %collective-permute-start.5 = (bf16[8,192,128]{2,1,0:T(8,128)(2,1)}, bf16[8,192,128]{2,1,0:T(8,128)(2,1)}, u32[]{:S(2)}, u32[]{:S(2)}) collective-permute-start(bf16[8,192,128]{2,1,0:T(8,128)(2,1)} %get-tuple-element.102), channel_id=1, source_target_pairs={{0,31},{1,30},{2,29},{3,28},{4,27},{5,26},{6,25},{7,24},{8,23},{9,... | collective-permute-start | bytes 1179656 | tf_op jit(solution)/shard_map/ppermute | solution.py:273
  286.6 22.5 %collective-permute-done.26.rest_0_ = bf16[8,192,128]{2,1,0:T(8,128)(2,1)} collective-permute-done((bf16[8,192,128]{2,1,0:T(8,128)(2,1)}, bf16[8,192,128]{2,1,0:T(8,128)(2,1)}, u32[]{:S(2)}, u32[]{:S(2)}) %collective-permute-start.26) | collective-permute-done | bytes 393248 | tf_op jit(solution)/shard_map/ppermute | solution.py:273
  314.0 4.3 %collective-permute-start.34 = (f32[4,128]{1,0:T(4,128)S(1)}, f32[4,128]{1,0:T(4,128)S(1)}, u32[]{:S(2)}, u32[]{:S(2)}) collective-permute-start(f32[4,128]{1,0:T(4,128)S(1)} %slice_reduce_fusion), channel_id=1, source_target_pairs={{0,1},{1,2},{2,3},{3,4},{4,5},{5,6},{6,7},{7,0},{8,9},{9,10},{10,1... | collective-permute-start | bytes 6152 | tf_op jit(solution)/shard_map/ppermute | solution.py:25
  318.3 15.1 %collective-permute-done.29.rest_3_ = bf16[8,192,128]{2,1,0:T(8,128)(2,1)} collective-permute-done((bf16[8,192,128]{2,1,0:T(8,128)(2,1)}, bf16[8,192,128]{2,1,0:T(8,128)(2,1)}, u32[]{:S(2)}, u32[]{:S(2)}) %collective-permute-start.29) | collective-permute-done | bytes 393248 | tf_op jit(solution)/shard_map/ppermute | solution.py:273
  (165 shorter events, 65.4 us)
Async XLA Ops:
  10.1 77.4 %collective-permute-start.30 = (bf16[8,192,128]{2,1,0:T(8,128)(2,1)}, bf16[8,192,128]{2,1,0:T(8,128)(2,1)S(1)}, u32[]{:S(2)}, u32[]{:S(2)}) collective-permute-start(bf16[8,192,128]{2,1,0:T(8,128)(2,1)} %get-tuple-element.127), channel_id=1, source_target_pairs={{0,12},{1,13},{2,14},{3,15},{4,8},{5,9},{6,10},{7,11},{8,4},{9,5},... | collective-permute-start | bytes 1179656 | tf_op jit(solution)/shard_map/ppermute | solution.py:273
  12.7 75.1 %collective-permute-start.32 = (bf16[8,192,128]{2,1,0:T(8,128)(2,1)}, bf16[8,192,128]{2,1,0:T(8,128)(2,1)S(1)}, u32[]{:S(2)}, u32[]{:S(2)}) collective-permute-start(bf16[8,192,128]{2,1,0:T(8,128)(2,1)} %get-tuple-element.129), channel_id=1, source_target_pairs={{0,4},{1,5},{2,6},{3,7},{4,0},{5,1},{6,2},{7,3},{8,12},{9,13},{10,... | collective-permute-start | bytes 1179656 | tf_op jit(solution)/shard_map/ppermute | solution.py:273
  64.8 23.9 %collective-permute-start.2 = (bf16[8,192,128]{2,1,0:T(8,128)(2,1)}, bf16[8,192,128]{2,1,0:T(8,128)(2,1)S(1)}, u32[]{:S(2)}, u32[]{:S(2)}) collective-permute-start(bf16[8,192,128]{2,1,0:T(8,128)(2,1)} %get-tuple-element.97), channel_id=1, source_target_pairs={{0,2},{1,3},{2,0},{3,1},{4,6},{5,7},{6,4},{7,5},{8,10},{9,11},{10,... | collective-permute-start | bytes 1179656 | tf_op jit(solution)/shard_map/ppermute | solution.py:273
  86.6 18.9 %collective-permute-start.6 = (bf16[8,192,128]{2,1,0:T(8,128)(2,1)}, bf16[8,192,128]{2,1,0:T(8,128)(2,1)S(1)}, u32[]{:S(2)}, u32[]{:S(2)}) collective-permute-start(bf16[8,192,128]{2,1,0:T(8,128)(2,1)} %get-tuple-element.103), channel_id=1, source_target_pairs={{0,24},{1,25},{2,26},{3,27},{4,28},{5,29},{6,30},{7,31},{8,16},{9,... | collective-permute-start | bytes 1179656 | tf_op jit(solution)/shard_map/ppermute | solution.py:273
  87.6 20.0 %collective-permute-start.7 = (bf16[8,192,128]{2,1,0:T(8,128)(2,1)}, bf16[8,192,128]{2,1,0:T(8,128)(2,1)S(1)}, u32[]{:S(2)}, u32[]{:S(2)}) collective-permute-start(bf16[8,192,128]{2,1,0:T(8,128)(2,1)} %get-tuple-element.104), channel_id=1, source_target_pairs={{0,7},{1,6},{2,5},{3,4},{4,3},{5,2},{6,1},{7,0},{8,15},{9,14},{10,... | collective-permute-start | bytes 1179656 | tf_op jit(solution)/shard_map/ppermute | solution.py:273
  88.6 52.4 %collective-permute-start.8 = (bf16[8,192,128]{2,1,0:T(8,128)(2,1)}, bf16[8,192,128]{2,1,0:T(8,128)(2,1)S(1)}, u32[]{:S(2)}, u32[]{:S(2)}) collective-permute-start(bf16[8,192,128]{2,1,0:T(8,128)(2,1)} %get-tuple-element.105), channel_id=1, source_target_pairs={{0,26},{1,27},{2,24},{3,25},{4,30},{5,31},{6,28},{7,29},{8,18},{9,... | collective-permute-start | bytes 1179656 | tf_op jit(solution)/shard_map/ppermute | solution.py:273
  88.7 57.1 %collective-permute-start.9 = (bf16[8,192,128]{2,1,0:T(8,128)(2,1)}, bf16[8,192,128]{2,1,0:T(8,128)(2,1)S(1)}, u32[]{:S(2)}, u32[]{:S(2)}) collective-permute-start(bf16[8,192,128]{2,1,0:T(8,128)(2,1)} %get-tuple-element.106), channel_id=1, source_target_pairs={{0,15},{1,14},{2,13},{3,12},{4,11},{5,10},{6,9},{7,8},{8,7},{9,6},... | collective-permute-start | bytes 1179656 | tf_op jit(solution)/shard_map/ppermute | solution.py:273
  95.9 51.8 %collective-permute-start.10 = (bf16[8,192,128]{2,1,0:T(8,128)(2,1)}, bf16[8,192,128]{2,1,0:T(8,128)(2,1)}, u32[]{:S(2)}, u32[]{:S(2)}) collective-permute-start(bf16[8,192,128]{2,1,0:T(8,128)(2,1)} %get-tuple-element.107), channel_id=1, source_target_pairs={{0,16},{1,17},{2,18},{3,19},{4,20},{5,21},{6,22},{7,23},{8,24},{9,... | collective-permute-start | bytes 1179656 | tf_op jit(solution)/shard_map/ppermute | solution.py:273
  105.4 43.3 %collective-permute-start.11 = (bf16[8,192,128]{2,1,0:T(8,128)(2,1)}, bf16[8,192,128]{2,1,0:T(8,128)(2,1)}, u32[]{:S(2)}, u32[]{:S(2)}) collective-permute-start(bf16[8,192,128]{2,1,0:T(8,128)(2,1)} %get-tuple-element.108), channel_id=1, source_target_pairs={{0,22},{1,23},{2,20},{3,21},{4,18},{5,19},{6,16},{7,17},{8,30},{9,... | collective-permute-start | bytes 1179656 | tf_op jit(solution)/shard_map/ppermute | solution.py:273
  107.6 71.2 %collective-permute-start.12 = (bf16[8,192,128]{2,1,0:T(8,128)(2,1)}, bf16[8,192,128]{2,1,0:T(8,128)(2,1)}, u32[]{:S(2)}, u32[]{:S(2)}) collective-permute-start(bf16[8,192,128]{2,1,0:T(8,128)(2,1)} %get-tuple-element.109), channel_id=1, source_target_pairs={{0,18},{1,19},{2,16},{3,17},{4,22},{5,23},{6,20},{7,21},{8,26},{9,... | collective-permute-start | bytes 1179656 | tf_op jit(solution)/shard_map/ppermute | solution.py:273
  141.0 38.6 %collective-permute-start.13 = (bf16[8,192,128]{2,1,0:T(8,128)(2,1)}, bf16[8,192,128]{2,1,0:T(8,128)(2,1)}, u32[]{:S(2)}, u32[]{:S(2)}) collective-permute-start(bf16[8,192,128]{2,1,0:T(8,128)(2,1)} %get-tuple-element.110), channel_id=1, source_target_pairs={{0,30},{1,31},{2,28},{3,29},{4,26},{5,27},{6,24},{7,25},{8,22},{9,... | collective-permute-start | bytes 1179656 | tf_op jit(solution)/shard_map/ppermute | solution.py:273
  145.7 35.6 %collective-permute-start.14 = (bf16[8,192,128]{2,1,0:T(8,128)(2,1)}, bf16[8,192,128]{2,1,0:T(8,128)(2,1)}, u32[]{:S(2)}, u32[]{:S(2)}) collective-permute-start(bf16[8,192,128]{2,1,0:T(8,128)(2,1)} %get-tuple-element.111), channel_id=1, source_target_pairs={{0,9},{1,8},{2,11},{3,10},{4,13},{5,12},{6,15},{7,14},{8,1},{9,0},... | collective-permute-start | bytes 1179656 | tf_op jit(solution)/shard_map/ppermute | solution.py:273
  147.8 42.1 %collective-permute-start.15 = (bf16[8,192,128]{2,1,0:T(8,128)(2,1)}, bf16[8,192,128]{2,1,0:T(8,128)(2,1)}, u32[]{:S(2)}, u32[]{:S(2)}) collective-permute-start(bf16[8,192,128]{2,1,0:T(8,128)(2,1)} %get-tuple-element.112), channel_id=1, source_target_pairs={{0,6},{1,7},{2,4},{3,5},{4,2},{5,3},{6,0},{7,1},{8,14},{9,15},{10,... | collective-permute-start | bytes 1179656 | tf_op jit(solution)/shard_map/ppermute | solution.py:273
  148.7 63.3 %collective-permute-start.16 = (bf16[8,192,128]{2,1,0:T(8,128)(2,1)}, bf16[8,192,128]{2,1,0:T(8,128)(2,1)}, u32[]{:S(2)}, u32[]{:S(2)}) collective-permute-start(bf16[8,192,128]{2,1,0:T(8,128)(2,1)} %get-tuple-element.113), channel_id=1, source_target_pairs={{0,11},{1,10},{2,9},{3,8},{4,15},{5,14},{6,13},{7,12},{8,3},{9,2},... | collective-permute-start | bytes 1179656 | tf_op jit(solution)/shard_map/ppermute | solution.py:273
  178.8 34.9 %collective-permute-start.17 = (bf16[8,192,128]{2,1,0:T(8,128)(2,1)}, bf16[8,192,128]{2,1,0:T(8,128)(2,1)}, u32[]{:S(2)}, u32[]{:S(2)}) collective-permute-start(bf16[8,192,128]{2,1,0:T(8,128)(2,1)} %get-tuple-element.114), channel_id=1, source_target_pairs={{0,14},{1,15},{2,12},{3,13},{4,10},{5,11},{6,8},{7,9},{8,6},{9,7},... | collective-permute-start | bytes 1179656 | tf_op jit(solution)/shard_map/ppermute | solution.py:273
  179.6 35.7 %collective-permute-start.18 = (bf16[8,192,128]{2,1,0:T(8,128)(2,1)}, bf16[8,192,128]{2,1,0:T(8,128)(2,1)}, u32[]{:S(2)}, u32[]{:S(2)}) collective-permute-start(bf16[8,192,128]{2,1,0:T(8,128)(2,1)} %get-tuple-element.115), channel_id=1, source_target_pairs={{0,1},{1,0},{2,3},{3,2},{4,5},{5,4},{6,7},{7,6},{8,9},{9,8},{10,11... | collective-permute-start | bytes 1179656 | tf_op jit(solution)/shard_map/ppermute | solution.py:273
  181.3 60.6 %collective-permute-start.19 = (bf16[8,192,128]{2,1,0:T(8,128)(2,1)}, bf16[8,192,128]{2,1,0:T(8,128)(2,1)}, u32[]{:S(2)}, u32[]{:S(2)}) collective-permute-start(bf16[8,192,128]{2,1,0:T(8,128)(2,1)} %get-tuple-element.116), channel_id=1, source_target_pairs={{0,21},{1,20},{2,23},{3,22},{4,17},{5,16},{6,19},{7,18},{8,29},{9,... | collective-permute-start | bytes 1179656 | tf_op jit(solution)/shard_map/ppermute | solution.py:273
  189.9 55.6 %collective-permute-start.20 = (bf16[8,192,128]{2,1,0:T(8,128)(2,1)}, bf16[8,192,128]{2,1,0:T(8,128)(2,1)}, u32[]{:S(2)}, u32[]{:S(2)}) collective-permute-start(bf16[8,192,128]{2,1,0:T(8,128)(2,1)} %get-tuple-element.117), channel_id=1, source_target_pairs={{0,3},{1,2},{2,1},{3,0},{4,7},{5,6},{6,5},{7,4},{8,11},{9,10},{10,... | collective-permute-start | bytes 1179656 | tf_op jit(solution)/shard_map/ppermute | solution.py:273
  212.0 40.0 %collective-permute-start.21 = (bf16[8,192,128]{2,1,0:T(8,128)(2,1)}, bf16[8,192,128]{2,1,0:T(8,128)(2,1)}, u32[]{:S(2)}, u32[]{:S(2)}) collective-permute-start(bf16[8,192,128]{2,1,0:T(8,128)(2,1)} %get-tuple-element.118), channel_id=1, source_target_pairs={{0,29},{1,28},{2,31},{3,30},{4,25},{5,24},{6,27},{7,26},{8,21},{9,... | collective-permute-start | bytes 1179656 | tf_op jit(solution)/shard_map/ppermute | solution.py:273
  213.7 40.0 %collective-permute-start.22 = (bf16[8,192,128]{2,1,0:T(8,128)(2,1)}, bf16[8,192,128]{2,1,0:T(8,128)(2,1)}, u32[]{:S(2)}, u32[]{:S(2)}) collective-permute-start(bf16[8,192,128]{2,1,0:T(8,128)(2,1)} %get-tuple-element.119), channel_id=1, source_target_pairs={{0,25},{1,24},{2,27},{3,26},{4,29},{5,28},{6,31},{7,30},{8,17},{9,... | collective-permute-start | bytes 1179656 | tf_op jit(solution)/shard_map/ppermute | solution.py:273
  215.3 57.2 %collective-permute-start.23 = (bf16[8,192,128]{2,1,0:T(8,128)(2,1)}, bf16[8,192,128]{2,1,0:T(8,128)(2,1)}, u32[]{:S(2)}, u32[]{:S(2)}) collective-permute-start(bf16[8,192,128]{2,1,0:T(8,128)(2,1)} %get-tuple-element.120), channel_id=1, source_target_pairs={{0,5},{1,4},{2,7},{3,6},{4,1},{5,0},{6,3},{7,2},{8,13},{9,12},{10,... | collective-permute-start | bytes 1179656 | tf_op jit(solution)/shard_map/ppermute | solution.py:273
  241.9 33.1 %collective-permute-start.24 = (bf16[8,192,128]{2,1,0:T(8,128)(2,1)}, bf16[8,192,128]{2,1,0:T(8,128)(2,1)}, u32[]{:S(2)}, u32[]{:S(2)}) collective-permute-start(bf16[8,192,128]{2,1,0:T(8,128)(2,1)} %get-tuple-element.121), channel_id=1, source_target_pairs={{0,27},{1,26},{2,25},{3,24},{4,31},{5,30},{6,29},{7,28},{8,19},{9,... | collective-permute-start | bytes 1179656 | tf_op jit(solution)/shard_map/ppermute | solution.py:273
  245.5 40.5 %collective-permute-start.25 = (bf16[8,192,128]{2,1,0:T(8,128)(2,1)}, bf16[8,192,128]{2,1,0:T(8,128)(2,1)}, u32[]{:S(2)}, u32[]{:S(2)}) collective-permute-start(bf16[8,192,128]{2,1,0:T(8,128)(2,1)} %get-tuple-element.122), channel_id=1, source_target_pairs={{0,13},{1,12},{2,15},{3,14},{4,9},{5,8},{6,11},{7,10},{8,5},{9,4},... | collective-permute-start | bytes 1179656 | tf_op jit(solution)/shard_map/ppermute | solution.py:273
  252.0 57.1 %collective-permute-start.26 = (bf16[8,192,128]{2,1,0:T(8,128)(2,1)}, bf16[8,192,128]{2,1,0:T(8,128)(2,1)}, u32[]{:S(2)}, u32[]{:S(2)}) collective-permute-start(bf16[8,192,128]{2,1,0:T(8,128)(2,1)} %get-tuple-element.123), channel_id=1, source_target_pairs={{0,20},{1,21},{2,22},{3,23},{4,16},{5,17},{6,18},{7,19},{8,28},{9,... | collective-permute-start | bytes 1179656 | tf_op jit(solution)/shard_map/ppermute | solution.py:273
  253.7 57.7 %collective-permute-start.27 = (bf16[8,192,128]{2,1,0:T(8,128)(2,1)}, bf16[8,192,128]{2,1,0:T(8,128)(2,1)}, u32[]{:S(2)}, u32[]{:S(2)}) collective-permute-start(bf16[8,192,128]{2,1,0:T(8,128)(2,1)} %get-tuple-element.124), channel_id=1, source_target_pairs={{0,17},{1,16},{2,19},{3,18},{4,21},{5,20},{6,23},{7,22},{8,25},{9,... | collective-permute-start | bytes 1179656 | tf_op jit(solution)/shard_map/ppermute | solution.py:273
  272.5 81.0 %collective-permute-start.4 = (bf16[8,192,128]{2,1,0:T(8,128)(2,1)}, bf16[8,192,128]{2,1,0:T(8,128)(2,1)}, u32[]{:S(2)}, u32[]{:S(2)}) collective-permute-start(bf16[8,192,128]{2,1,0:T(8,128)(2,1)} %get-tuple-element.101), channel_id=1, source_target_pairs={{0,8},{1,9},{2,10},{3,11},{4,12},{5,13},{6,14},{7,15},{8,0},{9,1},... | collective-permute-start | bytes 1179656 | tf_op jit(solution)/shard_map/ppermute | solution.py:273
  275.0 78.5 %collective-permute-start.5 = (bf16[8,192,128]{2,1,0:T(8,128)(2,1)}, bf16[8,192,128]{2,1,0:T(8,128)(2,1)}, u32[]{:S(2)}, u32[]{:S(2)}) collective-permute-start(bf16[8,192,128]{2,1,0:T(8,128)(2,1)} %get-tuple-element.102), channel_id=1, source_target_pairs={{0,31},{1,30},{2,29},{3,28},{4,27},{5,26},{6,25},{7,24},{8,23},{9,... | collective-permute-start | bytes 1179656 | tf_op jit(solution)/shard_map/ppermute | solution.py:273
  286.0 28.0 %collective-permute-start.28 = (bf16[8,192,128]{2,1,0:T(8,128)(2,1)}, bf16[8,192,128]{2,1,0:T(8,128)(2,1)}, u32[]{:S(2)}, u32[]{:S(2)}) collective-permute-start(bf16[8,192,128]{2,1,0:T(8,128)(2,1)} %get-tuple-element.125), channel_id=1, source_target_pairs={{0,19},{1,18},{2,17},{3,16},{4,23},{5,22},{6,21},{7,20},{8,27},{9,... | collective-permute-start | bytes 1179656 | tf_op jit(solution)/shard_map/ppermute | solution.py:273
  309.1 24.3 %collective-permute-start.29 = (bf16[8,192,128]{2,1,0:T(8,128)(2,1)}, bf16[8,192,128]{2,1,0:T(8,128)(2,1)}, u32[]{:S(2)}, u32[]{:S(2)}) collective-permute-start(bf16[8,192,128]{2,1,0:T(8,128)(2,1)} %get-tuple-element.126), channel_id=1, source_target_pairs={{0,28},{1,29},{2,30},{3,31},{4,24},{5,25},{6,26},{7,27},{8,20},{9,... | collective-permute-start | bytes 1179656 | tf_op jit(solution)/shard_map/ppermute | solution.py:273
  311.4 45.4 %collective-permute-start.36 = (bf16[8,192,128]{2,1,0:T(8,128)(2,1)}, bf16[8,192,128]{2,1,0:T(8,128)(2,1)}, u32[]{:S(2)}, u32[]{:S(2)}) collective-permute-start(bf16[8,192,128]{2,1,0:T(8,128)(2,1)} %get-tuple-element.150), channel_id=1, source_target_pairs={{0,10},{1,11},{2,8},{3,9},{4,14},{5,15},{6,12},{7,13},{8,2},{9,3},... | collective-permute-start | bytes 1179656 | tf_op jit(solution)/shard_map/ppermute | solution.py:273
  314.0 41.7 %collective-permute-start.34 = (f32[4,128]{1,0:T(4,128)S(1)}, f32[4,128]{1,0:T(4,128)S(1)}, u32[]{:S(2)}, u32[]{:S(2)}) collective-permute-start(f32[4,128]{1,0:T(4,128)S(1)} %slice_reduce_fusion), channel_id=1, source_target_pairs={{0,1},{1,2},{2,3},{3,4},{4,5},{5,6},{6,7},{7,0},{8,9},{9,10},{10,1... | collective-permute-start | bytes 6152 | tf_op jit(solution)/shard_map/ppermute | solution.py:25
  333.5 22.2 %collective-permute-start.35 = (f32[4,64]{1,0:T(4,128)S(1)}, f32[4,64]{1,0:T(4,128)S(1)}, u32[]{:S(2)}, u32[]{:S(2)}) collective-permute-start(f32[4,64]{1,0:T(4,128)S(1)} %bitcast.76), channel_id=1, source_target_pairs={{0,8},{8,16},{16,24},{24,0},{1,9},{9,17},{17,25},{25,1},{2,10},{10... | collective-permute-start | bytes 3080 | tf_op jit(solution)/shard_map/ppermute | solution.py:25
  (30 other events, 1557.1 us)

commit v3 on v2

--- a/solution.py
+++ b/solution.py
@@ -11,6 +11,7 @@
 STEPS = 3
 RAW = 2
 GROUP = 4
+LEAD = 4
 
 
 diffusion = 0.2
@@ -32,12 +33,12 @@
     far = sorted([k for k in range(1, devices) if k & far_bit], key=turns)
     near = [k for k in range(1, devices) if not k & far_bit]
     near.sort(key=lambda k: (not k & row_bit, not k & col_bit, k))
-    order, spare = far[:RAW], max(0, len(near) - len(far) + RAW)
-    for place, k in enumerate(far[RAW:]):
-        take = 2 if place < spare else 1
-        order += [k] + near[:take]
-        near = near[take:]
-    return order + near
+    far.append(far.pop(len(far) // 2))
+    order = far[:LEAD]
+    for k in far[LEAD:-1]:
+        order += near[:1] + [k]
+        near = near[1:]
+    return order + near + far[-1:]
 
 
 def partner_groups(order):
@@ -45,7 +46,7 @@
     return [todo[:2]] + [todo[i : i + GROUP] for i in range(2, len(todo), GROUP)]
 
 
-def block_copies(turns, capacity, slot_of, states_ref, out_refs, buffer, in_sem, out_sem, between=None):
+def block_copies(turns, capacity, slot_of, states_ref, out_refs, buffer, in_sem, out_sem):
     def fetch(turn, i):
         return pltpu.make_async_copy(states_ref.at[slot_of(turn, i)], buffer.at[turn, i], in_sem.at[turn, i])
 
@@ -55,8 +56,6 @@
     steps = [(turn, i) for turn in range(turns) for i in range(capacity)]
     for step in steps:
         fetch(*step).start()
-    if between is not None:
-        between()
     for step in steps:
         fetch(*step).wait()
         send(*step).start()
@@ -65,7 +64,7 @@
 
 
 def first_kernel(capacity, partner, me_ref, owner_ref, macro_ref, states_ref, out_ref, row_ref, col_ref, *scratch):
-    slot_ref, macro_buffer, macro_sem, *gather = scratch
+    slot_ref, macro_buffer, macro_sem, in_sem = scratch
     slot_total = owner_ref.shape[0]
     owner = jnp.bitwise_xor(me_ref[0], partner)
     fields = pltpu.make_async_copy(macro_ref, macro_buffer, macro_sem)
@@ -77,19 +76,23 @@
 
     lax.fori_loop(0, slot_total, look, jnp.int32(0), unroll=8)
 
-    def edges():
-        fields.wait()
-        channels, _, tile_rows = macro_buffer.shape
-        pick = (lax.broadcasted_iota(jnp.int32, (8, tile_rows), 1) == 0).astype(jnp.float32)
-        for channel in range(channels):
-            field = macro_buffer[channel]
-            col_ref[channel : channel + 1, :] = field[0:1, :]
-            rows = lax.dot_general(
-                pick, field, (((1,), (1,)), ((), ())), precision=HIGHEST, preferred_element_type=jnp.float32
-            )
-            row_ref[channel : channel + 1, :] = rows[0:1, :]
-
-    block_copies(1, capacity, lambda turn, i: slot_ref[i], states_ref, [out_ref], *gather, between=edges)
+    def fetch(i):
+        return pltpu.make_async_copy(states_ref.at[slot_ref[i]], out_ref.at[i], in_sem.at[i])
+
+    for i in range(capacity):
+        fetch(i).start()
+    fields.wait()
+    channels, _, tile_rows = macro_buffer.shape
+    pick = (lax.broadcasted_iota(jnp.int32, (8, tile_rows), 1) == 0).astype(jnp.float32)
+    for channel in range(channels):
+        field = macro_buffer[channel]
+        col_ref[channel : channel + 1, :] = field[0:1, :]
+        rows = lax.dot_general(
+            pick, field, (((1,), (1,)), ((), ())), precision=HIGHEST, preferred_element_type=jnp.float32
+        )
+        row_ref[channel : channel + 1, :] = rows[0:1, :]
+    for i in range(capacity):
+        fetch(i).wait()
 
 
 def route_kernel(capacity, partners, me_ref, owner_ref, face_ref, states_ref, table_ref, ids_ref, *rest):
@@ -285,18 +288,18 @@
     raw_first, first_row, first_col = pl.pallas_call(
         functools.partial(first_kernel, capacity, raw[0]),
         out_shape=[
-            block,
-            jax.ShapeDtypeStruct((channels, tile_cols), jnp.float32),
-            jax.ShapeDtypeStruct((channels, tile_rows), jnp.float32),
+            pltpu.VMEM(block.shape, block.dtype),
+            pltpu.VMEM((channels, tile_cols), jnp.float32),
+            pltpu.VMEM((channels, tile_rows), jnp.float32),
         ],
         in_specs=[SMEM, SMEM, ANY, ANY],
-        out_specs=[ANY, VMEM, VMEM],
+        out_specs=[VMEM, VMEM, VMEM],
         scratch_shapes=[
             pltpu.SMEM((slot_total,), jnp.int32),
             pltpu.VMEM(fields.shape, jnp.float32),
             pltpu.SemaphoreType.DMA,
-        ]
-        + gather_scratch(1),
+            pltpu.SemaphoreType.DMA((capacity,)),
+        ],
         name="first",
     )(me_ref, owner.reshape(slot_total), fields, states)
     owners, raw_first = lax.optimization_barrier((owner.reshape(slot_total), raw_first))
@@ -409,8 +412,11 @@
             input_output_aliases={len(partners) + 1: 0},
         )(me_ref, *[got[k] for k in partners], out)
 
-    landings = [order[i : i + GROUP] for i in range(RAW, devices - 1, GROUP)]
-    for partners in landings[:-1]:
+    waiting = order[RAW:-1]
+    head = len(waiting) % GROUP
+    landings = [waiting[:head]] if head else []
+    landings += [waiting[i : i + GROUP] for i in range(head, len(waiting), GROUP)]
+    for partners in landings:
         out = put(out, partners)
     out, west_flux, north_flux = lax.optimization_barrier((out, west_flux, north_flux))
     macro_next = macro_state - time_step * (
@@ -419,8 +425,10 @@
         + south_flux
         - jnp.concatenate([north_flux[:, None, :], south_flux[:, :-1, :]], axis=1)
     )
-    out, macro_next = lax.optimization_barrier((out, macro_next))
-    out = put(out, landings[-1])
+    out, macro_next = lax.optimization_barrier((out, jnp.transpose(macro_next, (0, 2, 1))))
+    macro_next = jnp.transpose(macro_next, (0, 2, 1))
+    last = order[-1]
+    out = lax.dynamic_update_slice(out, got[last][None], (jnp.bitwise_xor(me, last), 0, 0, 0))
     return macro_next, out.reshape(1, 1, devices, capacity, members, state_width)
 
 

time: 360 us -> 378 us (1.050)
  the two profiles are of different devices: /device:TPU:7 before, /device:TPU:0 now
where the time goes in v3:
time: 378 us; the launch traced here: 376 us
  starting transfers between devices  161 us (43%)
  waiting for transfers between devices  113 us (30%)
  Pallas kernels  88.3 us (23%)
  local copies, waits for them, and re-layouts  8.58 us (2%)
    ppermute x33, starting transfers between devices, exchanged(): lax.ppermute(value, ('gx', 'gy'), [(source, source ^ k) for source in ran...  154 us
    ppermute x33, waiting for transfers between devices, exchanged(): lax.ppermute(value, ('gx', 'gy'), [(source, source ^ k) for source in ran...  113 us
    pallas_call x9, Pallas kernels, per_device(): pl.pallas_call(functools.partial(relax_kernel, capacity, partners, kept,...  54.6 us
    pallas_call x7, Pallas kernels, put(): pl.pallas_call(functools.partial(put_kernel, partners), out_shape=whole,...  15.4 us
  transfers between devices with their start and end apart: 37, of which 13 were waited for; matrix products, arithmetic and copies ran while one was open for 2% of the time, Pallas kernels for 23%

profile of v3, /device:TPU:0, one launch (start us, length us, event | category | flops | bytes accessed | tf_op | source)
XLA Modules:
  0.0 376.1 jit_solution(4804106166411422790)
XLA Ops:
  5.6 4.5 %collective-permute-start.1 = (f32[4,128]{1,0:T(4,128)S(1)}, f32[4,128]{1,0:T(4,128)S(1)}, u32[]{:S(2)}, u32[]{:S(2)}) collective-permute-start(f32[4,128]{1,0:T(4,128)S(1)} %get-tuple-element.81), channel_id=1, source_target_pairs={{0,7},{1,0},{2,1},{3,2},{4,3},{5,4},{6,5},{7,6},{8,15},{9,8},{10,9... | collective-permute-start | bytes 6152 | tf_op jit(solution)/shard_map/ppermute | solution.py:26
  10.2 4.7 %route.1 = (s32[256]{0:T(256)}, s32[256]{0:T(256)}, bf16[8,192,128]{2,1,0:T(8,128)(2,1)}) custom-call(s32[1]{0:T(128)} %bitcast.me_ref, s32[256]{0:T(256)} %bitcast.80, s32[256]{0:T(256)} %bitcast.84, bf16[256,192,128]{2,1,0:T(8,128)(2,1)} %bitcast.45), custom_call_target="tpu_custom_call" | custom-call | tf_op jit(solution)/shard_map/route/pallas_call | solution.py:309
  24.7 4.9 %shard_map.86 = (bf16[8,192,128]{2,1,0:T(8,128)(2,1)}, bf16[8,192,128]{2,1,0:T(8,128)(2,1)}, f32[16,128]{1,0:T(8,128)}) custom-call(s32[1]{0:T(128)} %bitcast.me_ref, s32[256]{0:T(256)} %get-tuple-element.132.table_ref, bf16[256,192,128]{2,1,0:T(8,128)(2,1)} %bitcast.46, f32[256,128]{1,0:T(8,128)} %get-tuple-element.83.force_ref, ...), custom_call_target="tpu_custom_call" | custom-call | tf_op jit(solution)/shard_map/pallas_call | solution.py:347
  29.6 6.5 %shard_map.87 = (bf16[8,192,128]{2,1,0:T(8,128)(2,1)}, bf16[8,192,128]{2,1,0:T(8,128)(2,1)}, bf16[8,192,128]{2,1,0:T(8,128)(2,1)}, bf16[8,192,128]{2,1,0:T(8,128)(2,1)}, f32[32,128]{1,0:T(8,128)}) custom-call(s32[1]{0:T(128)} %bitcast.me_ref, s32[256]{0:T(256)} %get-tuple-element.132.table_ref, bf16[256,192,128]{2,1,0:T(8,128)(2,1)} %bitcast.47, ...), custom_call_target="tpu_custom_call" | custom-call | tf_op jit(solution)/shard_map/pallas_call | solution.py:347
  36.1 6.5 %shard_map.88 = (bf16[8,192,128]{2,1,0:T(8,128)(2,1)}, bf16[8,192,128]{2,1,0:T(8,128)(2,1)}, bf16[8,192,128]{2,1,0:T(8,128)(2,1)}, bf16[8,192,128]{2,1,0:T(8,128)(2,1)}, f32[32,128]{1,0:T(8,128)}) custom-call(s32[1]{0:T(128)} %bitcast.me_ref, s32[256]{0:T(256)} %get-tuple-element.132.table_ref, bf16[256,192,128]{2,1,0:T(8,128)(2,1)} %bitcast.48, ...), custom_call_target="tpu_custom_call" | custom-call | tf_op jit(solution)/shard_map/pallas_call | solution.py:347
  42.6 6.6 %shard_map.89 = (bf16[8,192,128]{2,1,0:T(8,128)(2,1)}, bf16[8,192,128]{2,1,0:T(8,128)(2,1)}, bf16[8,192,128]{2,1,0:T(8,128)(2,1)}, bf16[8,192,128]{2,1,0:T(8,128)(2,1)}, f32[32,128]{1,0:T(8,128)}) custom-call(s32[1]{0:T(128)} %bitcast.me_ref, s32[256]{0:T(256)} %get-tuple-element.132.table_ref, bf16[256,192,128]{2,1,0:T(8,128)(2,1)} %bitcast.49, ...), custom_call_target="tpu_custom_call" | custom-call | tf_op jit(solution)/shard_map/pallas_call | solution.py:347
  49.2 6.5 %shard_map.90 = (bf16[8,192,128]{2,1,0:T(8,128)(2,1)}, bf16[8,192,128]{2,1,0:T(8,128)(2,1)}, bf16[8,192,128]{2,1,0:T(8,128)(2,1)}, bf16[8,192,128]{2,1,0:T(8,128)(2,1)}, f32[32,128]{1,0:T(8,128)}) custom-call(s32[1]{0:T(128)} %bitcast.me_ref, s32[256]{0:T(256)} %get-tuple-element.132.table_ref, bf16[256,192,128]{2,1,0:T(8,128)(2,1)} %bitcast.50, ...), custom_call_target="tpu_custom_call" | custom-call | tf_op jit(solution)/shard_map/pallas_call | solution.py:347
  55.7 6.5 %shard_map.91 = (bf16[8,192,128]{2,1,0:T(8,128)(2,1)}, bf16[8,192,128]{2,1,0:T(8,128)(2,1)}, bf16[8,192,128]{2,1,0:T(8,128)(2,1)}, bf16[8,192,128]{2,1,0:T(8,128)(2,1)}, f32[32,128]{1,0:T(8,128)}) custom-call(s32[1]{0:T(128)} %bitcast.me_ref, s32[256]{0:T(256)} %get-tuple-element.132.table_ref, bf16[256,192,128]{2,1,0:T(8,128)(2,1)} %bitcast.51, ...), custom_call_target="tpu_custom_call" | custom-call | tf_op jit(solution)/shard_map/pallas_call | solution.py:347
  62.2 6.5 %shard_map.92 = (bf16[8,192,128]{2,1,0:T(8,128)(2,1)}, bf16[8,192,128]{2,1,0:T(8,128)(2,1)}, bf16[8,192,128]{2,1,0:T(8,128)(2,1)}, bf16[8,192,128]{2,1,0:T(8,128)(2,1)}, f32[32,128]{1,0:T(8,128)}) custom-call(s32[1]{0:T(128)} %bitcast.me_ref, s32[256]{0:T(256)} %get-tuple-element.132.table_ref, bf16[256,192,128]{2,1,0:T(8,128)(2,1)} %bitcast.52, ...), custom_call_target="tpu_custom_call" | custom-call | tf_op jit(solution)/shard_map/pallas_call | solution.py:347
  68.9 5.7 %shard_map.93 = (bf16[8,192,128]{2,1,0:T(8,128)(2,1)}, bf16[8,192,128]{2,1,0:T(8,128)(2,1)}, bf16[8,192,128]{2,1,0:T(8,128)(2,1)}, f32[32,128]{1,0:T(8,128)}) custom-call(s32[1]{0:T(128)} %bitcast.me_ref, s32[256]{0:T(256)} %get-tuple-element.132.table_ref, bf16[256,192,128]{2,1,0:T(8,128)(2,1)} %bitcast.53, f32[256,128]{1,0:T(8,128)} %get-tuple-element.83.force_ref, ...), custom_call_target="tpu_custom_call" | custom-call | tf_op jit(solution)/shard_map/pallas_call | solution.py:347
  78.4 4.9 %shard_map.94 = (bf16[32,8,192,128]{3,2,1,0:T(8,128)(2,1)}, f32[16,128]{1,0:T(8,128)}) custom-call(s32[1]{0:T(128)} %bitcast.me_ref, s32[256]{0:T(256)} %get-tuple-element.132.table_ref, bf16[256,192,128]{2,1,0:T(8,128)(2,1)} %bitcast.54, f32[256,128]{1,0:T(8,128)} %get-tuple-element.83.force_ref, f32[256,128]{1,0:T(8,128)} %get-tuple-element.84.live_ref, ...), custom_call_target="tpu_custom_call" | custom-call | tf_op jit(solution)/shard_map/pallas_call | solution.py:347
  89.8 5.1 %collective-permute-start.9 = (bf16[8,192,128]{2,1,0:T(8,128)(2,1)}, bf16[8,192,128]{2,1,0:T(8,128)(2,1)}, u32[]{:S(2)}, u32[]{:S(2)}) collective-permute-start(bf16[8,192,128]{2,1,0:T(8,128)(2,1)} %get-tuple-element.106), channel_id=1, source_target_pairs={{0,31},{1,30},{2,29},{3,28},{4,27},{5,26},{6,25},{7,24},{8,23},{9,... | collective-permute-start | bytes 1179656 | tf_op jit(solution)/shard_map/ppermute | solution.py:276
  97.5 15.3 %collective-permute-done.6.rest_0_ = bf16[8,192,128]{2,1,0:T(8,128)(2,1)S(1)} collective-permute-done((bf16[8,192,128]{2,1,0:T(8,128)(2,1)}, bf16[8,192,128]{2,1,0:T(8,128)(2,1)S(1)}, u32[]{:S(2)}, u32[]{:S(2)}) %collective-permute-start.6) | collective-permute-done | bytes 393248 | tf_op jit(solution)/shard_map/ppermute | solution.py:276
  113.3 10.2 %collective-permute-done.7.rest_1_ = bf16[8,192,128]{2,1,0:T(8,128)(2,1)S(1)} collective-permute-done((bf16[8,192,128]{2,1,0:T(8,128)(2,1)}, bf16[8,192,128]{2,1,0:T(8,128)(2,1)S(1)}, u32[]{:S(2)}, u32[]{:S(2)}) %collective-permute-start.7) | collective-permute-done | bytes 393248 | tf_op jit(solution)/shard_map/ppermute | solution.py:276
  126.9 4.7 %collective-permute-done.9.rest_3_ = bf16[8,192,128]{2,1,0:T(8,128)(2,1)} collective-permute-done((bf16[8,192,128]{2,1,0:T(8,128)(2,1)}, bf16[8,192,128]{2,1,0:T(8,128)(2,1)}, u32[]{:S(2)}, u32[]{:S(2)}) %collective-permute-start.9) | collective-permute-done | bytes 393248 | tf_op jit(solution)/shard_map/ppermute | solution.py:276
  134.1 9.5 %collective-permute-done.10.rest_0_ = bf16[8,192,128]{2,1,0:T(8,128)(2,1)} collective-permute-done((bf16[8,192,128]{2,1,0:T(8,128)(2,1)}, bf16[8,192,128]{2,1,0:T(8,128)(2,1)}, u32[]{:S(2)}, u32[]{:S(2)}) %collective-permute-start.10) | collective-permute-done | bytes 393248 | tf_op jit(solution)/shard_map/ppermute | solution.py:276
  144.6 8.4 %collective-permute-done.11.rest_1_ = bf16[8,192,128]{2,1,0:T(8,128)(2,1)} collective-permute-done((bf16[8,192,128]{2,1,0:T(8,128)(2,1)}, bf16[8,192,128]{2,1,0:T(8,128)(2,1)}, u32[]{:S(2)}, u32[]{:S(2)}) %collective-permute-start.11) | collective-permute-done | bytes 393248 | tf_op jit(solution)/shard_map/ppermute | solution.py:276
  153.0 7.0 %collective-permute-start.17 = (bf16[8,192,128]{2,1,0:T(8,128)(2,1)}, bf16[8,192,128]{2,1,0:T(8,128)(2,1)}, u32[]{:S(2)}, u32[]{:S(2)}) collective-permute-start(bf16[8,192,128]{2,1,0:T(8,128)(2,1)} %get-tuple-element.114), channel_id=1, source_target_pairs={{0,30},{1,31},{2,28},{3,29},{4,26},{5,27},{6,24},{7,25},{8,22},{9,... | collective-permute-start | bytes 1179656 | tf_op jit(solution)/shard_map/ppermute | solution.py:276
  160.5 32.3 %collective-permute-start.18 = (bf16[8,192,128]{2,1,0:T(8,128)(2,1)}, bf16[8,192,128]{2,1,0:T(8,128)(2,1)}, u32[]{:S(2)}, u32[]{:S(2)}) collective-permute-start(bf16[8,192,128]{2,1,0:T(8,128)(2,1)} %get-tuple-element.115), channel_id=1, source_target_pairs={{0,27},{1,26},{2,25},{3,24},{4,31},{5,30},{6,29},{7,28},{8,19},{9,... | collective-permute-start | bytes 1179656 | tf_op jit(solution)/shard_map/ppermute | solution.py:276
  192.8 4.3 %collective-permute-start.19 = (bf16[8,192,128]{2,1,0:T(8,128)(2,1)}, bf16[8,192,128]{2,1,0:T(8,128)(2,1)}, u32[]{:S(2)}, u32[]{:S(2)}) collective-permute-start(bf16[8,192,128]{2,1,0:T(8,128)(2,1)} %get-tuple-element.116), channel_id=1, source_target_pairs={{0,29},{1,28},{2,31},{3,30},{4,25},{5,24},{6,27},{7,26},{8,21},{9,... | collective-permute-start | bytes 1179656 | tf_op jit(solution)/shard_map/ppermute | solution.py:276
  197.2 37.8 %collective-permute-start.22 = (bf16[8,192,128]{2,1,0:T(8,128)(2,1)}, bf16[8,192,128]{2,1,0:T(8,128)(2,1)}, u32[]{:S(2)}, u32[]{:S(2)}) collective-permute-start(bf16[8,192,128]{2,1,0:T(8,128)(2,1)} %get-tuple-element.119), channel_id=1, source_target_pairs={{0,19},{1,18},{2,17},{3,16},{4,23},{5,22},{6,21},{7,20},{8,27},{9,... | collective-permute-start | bytes 1179656 | tf_op jit(solution)/shard_map/ppermute | solution.py:276
  235.0 5.3 %collective-permute-done.19.rest_1_ = bf16[8,192,128]{2,1,0:T(8,128)(2,1)} collective-permute-done((bf16[8,192,128]{2,1,0:T(8,128)(2,1)}, bf16[8,192,128]{2,1,0:T(8,128)(2,1)}, u32[]{:S(2)}, u32[]{:S(2)}) %collective-permute-start.19) | collective-permute-done | bytes 393248 | tf_op jit(solution)/shard_map/ppermute | solution.py:276
  241.5 26.9 %collective-permute-start.26 = (bf16[8,192,128]{2,1,0:T(8,128)(2,1)}, bf16[8,192,128]{2,1,0:T(8,128)(2,1)}, u32[]{:S(2)}, u32[]{:S(2)}) collective-permute-start(bf16[8,192,128]{2,1,0:T(8,128)(2,1)} %get-tuple-element.123), channel_id=1, source_target_pairs={{0,20},{1,21},{2,22},{3,23},{4,16},{5,17},{6,18},{7,19},{8,28},{9,... | collective-permute-start | bytes 1179656 | tf_op jit(solution)/shard_map/ppermute | solution.py:276
  270.4 3.3 flux.1
  273.7 18.7 %collective-permute-done.23.rest_1_ = bf16[8,192,128]{2,1,0:T(8,128)(2,1)S(1)} collective-permute-done((bf16[8,192,128]{2,1,0:T(8,128)(2,1)}, bf16[8,192,128]{2,1,0:T(8,128)(2,1)S(1)}, u32[]{:S(2)}, u32[]{:S(2)}) %collective-permute-start.23) | collective-permute-done | bytes 393248 | tf_op jit(solution)/shard_map/ppermute | solution.py:276
  292.5 3.7 collective-permute-start.4
  296.2 5.9 %collective-permute-done.25.rest_3_ = bf16[8,192,128]{2,1,0:T(8,128)(2,1)} collective-permute-done((bf16[8,192,128]{2,1,0:T(8,128)(2,1)}, bf16[8,192,128]{2,1,0:T(8,128)(2,1)}, u32[]{:S(2)}, u32[]{:S(2)}) %collective-permute-start.25) | collective-permute-done | bytes 393248 | tf_op jit(solution)/shard_map/ppermute | solution.py:276
  302.1 11.7 %collective-permute-done.26.rest_0_ = bf16[8,192,128]{2,1,0:T(8,128)(2,1)} collective-permute-done((bf16[8,192,128]{2,1,0:T(8,128)(2,1)}, bf16[8,192,128]{2,1,0:T(8,128)(2,1)}, u32[]{:S(2)}, u32[]{:S(2)}) %collective-permute-start.26) | collective-permute-done | bytes 393248 | tf_op jit(solution)/shard_map/ppermute | solution.py:276
  313.8 9.8 %collective-permute-start.29 = (bf16[8,192,128]{2,1,0:T(8,128)(2,1)}, bf16[8,192,128]{2,1,0:T(8,128)(2,1)}, u32[]{:S(2)}, u32[]{:S(2)}) collective-permute-start(bf16[8,192,128]{2,1,0:T(8,128)(2,1)} %get-tuple-element.126), channel_id=1, source_target_pairs={{0,5},{1,4},{2,7},{3,6},{4,1},{5,0},{6,3},{7,2},{8,13},{9,12},{10,... | collective-permute-start | bytes 1179656 | tf_op jit(solution)/shard_map/ppermute | solution.py:276
  324.7 3.3 collective-permute-done.27.rest_1_
  327.9 6.7 %collective-permute-start.36 = (bf16[8,192,128]{2,1,0:T(8,128)(2,1)}, bf16[8,192,128]{2,1,0:T(8,128)(2,1)S(1)}, u32[]{:S(2)}, u32[]{:S(2)}) collective-permute-start(bf16[8,192,128]{2,1,0:T(8,128)(2,1)} %get-tuple-element.151), channel_id=1, source_target_pairs={{0,6},{1,7},{2,4},{3,5},{4,2},{5,3},{6,0},{7,1},{8,14},{9,15},{10,... | collective-permute-start | bytes 1179656 | tf_op jit(solution)/shard_map/ppermute | solution.py:276
  336.1 17.6 %collective-permute-done.29.rest_3_ = bf16[8,192,128]{2,1,0:T(8,128)(2,1)} collective-permute-done((bf16[8,192,128]{2,1,0:T(8,128)(2,1)}, bf16[8,192,128]{2,1,0:T(8,128)(2,1)}, u32[]{:S(2)}, u32[]{:S(2)}) %collective-permute-start.29) | collective-permute-done | bytes 393248 | tf_op jit(solution)/shard_map/ppermute | solution.py:276
  (165 shorter events, 63.2 us)
Async XLA Ops:
  14.8 72.4 %collective-permute-start.30 = (bf16[8,192,128]{2,1,0:T(8,128)(2,1)}, bf16[8,192,128]{2,1,0:T(8,128)(2,1)S(1)}, u32[]{:S(2)}, u32[]{:S(2)}) collective-permute-start(bf16[8,192,128]{2,1,0:T(8,128)(2,1)} %get-tuple-element.127), channel_id=1, source_target_pairs={{0,12},{1,13},{2,14},{3,15},{4,8},{5,9},{6,10},{7,11},{8,4},{9,5},... | collective-permute-start | bytes 1179656 | tf_op jit(solution)/shard_map/ppermute | solution.py:276
  14.9 74.9 %collective-permute-start.32 = (bf16[8,192,128]{2,1,0:T(8,128)(2,1)S(1)}, bf16[8,192,128]{2,1,0:T(8,128)(2,1)}, u32[]{:S(2)}, u32[]{:S(2)}) collective-permute-start(bf16[8,192,128]{2,1,0:T(8,128)(2,1)S(1)} %get-tuple-element.129), channel_id=1, source_target_pairs={{0,4},{1,5},{2,6},{3,7},{4,0},{5,1},{6,2},{7,3},{8,12},{9,13},{10,... | collective-permute-start | bytes 1179656 | tf_op jit(solution)/shard_map/ppermute | solution.py:276
  68.7 21.1 %collective-permute-start.2 = (bf16[8,192,128]{2,1,0:T(8,128)(2,1)}, bf16[8,192,128]{2,1,0:T(8,128)(2,1)S(1)}, u32[]{:S(2)}, u32[]{:S(2)}) collective-permute-start(bf16[8,192,128]{2,1,0:T(8,128)(2,1)} %get-tuple-element.97), channel_id=1, source_target_pairs={{0,26},{1,27},{2,24},{3,25},{4,30},{5,31},{6,28},{7,29},{8,18},{9,... | collective-permute-start | bytes 1179656 | tf_op jit(solution)/shard_map/ppermute | solution.py:276
  87.2 25.6 %collective-permute-start.6 = (bf16[8,192,128]{2,1,0:T(8,128)(2,1)}, bf16[8,192,128]{2,1,0:T(8,128)(2,1)S(1)}, u32[]{:S(2)}, u32[]{:S(2)}) collective-permute-start(bf16[8,192,128]{2,1,0:T(8,128)(2,1)} %get-tuple-element.103), channel_id=1, source_target_pairs={{0,18},{1,19},{2,16},{3,17},{4,22},{5,23},{6,20},{7,21},{8,26},{9,... | collective-permute-start | bytes 1179656 | tf_op jit(solution)/shard_map/ppermute | solution.py:276
  88.0 35.6 %collective-permute-start.7 = (bf16[8,192,128]{2,1,0:T(8,128)(2,1)}, bf16[8,192,128]{2,1,0:T(8,128)(2,1)S(1)}, u32[]{:S(2)}, u32[]{:S(2)}) collective-permute-start(bf16[8,192,128]{2,1,0:T(8,128)(2,1)} %get-tuple-element.104), channel_id=1, source_target_pairs={{0,23},{1,22},{2,21},{3,20},{4,19},{5,18},{6,17},{7,16},{8,31},{9,... | collective-permute-start | bytes 1179656 | tf_op jit(solution)/shard_map/ppermute | solution.py:276
  89.8 33.9 %collective-permute-start.8 = (bf16[8,192,128]{2,1,0:T(8,128)(2,1)}, bf16[8,192,128]{2,1,0:T(8,128)(2,1)}, u32[]{:S(2)}, u32[]{:S(2)}) collective-permute-start(bf16[8,192,128]{2,1,0:T(8,128)(2,1)} %get-tuple-element.105), channel_id=1, source_target_pairs={{0,24},{1,25},{2,26},{3,27},{4,28},{5,29},{6,30},{7,31},{8,16},{9,... | collective-permute-start | bytes 1179656 | tf_op jit(solution)/shard_map/ppermute | solution.py:276
  89.8 41.8 %collective-permute-start.9 = (bf16[8,192,128]{2,1,0:T(8,128)(2,1)}, bf16[8,192,128]{2,1,0:T(8,128)(2,1)}, u32[]{:S(2)}, u32[]{:S(2)}) collective-permute-start(bf16[8,192,128]{2,1,0:T(8,128)(2,1)} %get-tuple-element.106), channel_id=1, source_target_pairs={{0,31},{1,30},{2,29},{3,28},{4,27},{5,26},{6,25},{7,24},{8,23},{9,... | collective-permute-start | bytes 1179656 | tf_op jit(solution)/shard_map/ppermute | solution.py:276
  97.3 46.2 %collective-permute-start.10 = (bf16[8,192,128]{2,1,0:T(8,128)(2,1)}, bf16[8,192,128]{2,1,0:T(8,128)(2,1)}, u32[]{:S(2)}, u32[]{:S(2)}) collective-permute-start(bf16[8,192,128]{2,1,0:T(8,128)(2,1)} %get-tuple-element.107), channel_id=1, source_target_pairs={{0,11},{1,10},{2,9},{3,8},{4,15},{5,14},{6,13},{7,12},{8,3},{9,2},... | collective-permute-start | bytes 1179656 | tf_op jit(solution)/shard_map/ppermute | solution.py:276
  112.8 40.3 %collective-permute-start.11 = (bf16[8,192,128]{2,1,0:T(8,128)(2,1)}, bf16[8,192,128]{2,1,0:T(8,128)(2,1)}, u32[]{:S(2)}, u32[]{:S(2)}) collective-permute-start(bf16[8,192,128]{2,1,0:T(8,128)(2,1)} %get-tuple-element.108), channel_id=1, source_target_pairs={{0,7},{1,6},{2,5},{3,4},{4,3},{5,2},{6,1},{7,0},{8,15},{9,14},{10,... | collective-permute-start | bytes 1179656 | tf_op jit(solution)/shard_map/ppermute | solution.py:276
  123.5 29.5 %collective-permute-start.12 = (bf16[8,192,128]{2,1,0:T(8,128)(2,1)}, bf16[8,192,128]{2,1,0:T(8,128)(2,1)}, u32[]{:S(2)}, u32[]{:S(2)}) collective-permute-start(bf16[8,192,128]{2,1,0:T(8,128)(2,1)} %get-tuple-element.109), channel_id=1, source_target_pairs={{0,16},{1,17},{2,18},{3,19},{4,20},{5,21},{6,22},{7,23},{8,24},{9,... | collective-permute-start | bytes 1179656 | tf_op jit(solution)/shard_map/ppermute | solution.py:276
  123.7 36.8 %collective-permute-start.13 = (bf16[8,192,128]{2,1,0:T(8,128)(2,1)}, bf16[8,192,128]{2,1,0:T(8,128)(2,1)}, u32[]{:S(2)}, u32[]{:S(2)}) collective-permute-start(bf16[8,192,128]{2,1,0:T(8,128)(2,1)} %get-tuple-element.110), channel_id=1, source_target_pairs={{0,15},{1,14},{2,13},{3,12},{4,11},{5,10},{6,9},{7,8},{8,7},{9,6},... | collective-permute-start | bytes 1179656 | tf_op jit(solution)/shard_map/ppermute | solution.py:276
  131.6 61.2 %collective-permute-start.14 = (bf16[8,192,128]{2,1,0:T(8,128)(2,1)}, bf16[8,192,128]{2,1,0:T(8,128)(2,1)}, u32[]{:S(2)}, u32[]{:S(2)}) collective-permute-start(bf16[8,192,128]{2,1,0:T(8,128)(2,1)} %get-tuple-element.111), channel_id=1, source_target_pairs={{0,3},{1,2},{2,1},{3,0},{4,7},{5,6},{6,5},{7,4},{8,11},{9,10},{10,... | collective-permute-start | bytes 1179656 | tf_op jit(solution)/shard_map/ppermute | solution.py:276
  143.6 53.5 %collective-permute-start.15 = (bf16[8,192,128]{2,1,0:T(8,128)(2,1)}, bf16[8,192,128]{2,1,0:T(8,128)(2,1)}, u32[]{:S(2)}, u32[]{:S(2)}) collective-permute-start(bf16[8,192,128]{2,1,0:T(8,128)(2,1)} %get-tuple-element.112), channel_id=1, source_target_pairs={{0,22},{1,23},{2,20},{3,21},{4,18},{5,19},{6,16},{7,17},{8,30},{9,... | collective-permute-start | bytes 1179656 | tf_op jit(solution)/shard_map/ppermute | solution.py:276
  153.0 44.0 %collective-permute-start.16 = (bf16[8,192,128]{2,1,0:T(8,128)(2,1)}, bf16[8,192,128]{2,1,0:T(8,128)(2,1)}, u32[]{:S(2)}, u32[]{:S(2)}) collective-permute-start(bf16[8,192,128]{2,1,0:T(8,128)(2,1)} %get-tuple-element.113), channel_id=1, source_target_pairs={{0,9},{1,8},{2,11},{3,10},{4,13},{5,12},{6,15},{7,14},{8,1},{9,0},... | collective-permute-start | bytes 1179656 | tf_op jit(solution)/shard_map/ppermute | solution.py:276
  153.0 44.1 %collective-permute-start.17 = (bf16[8,192,128]{2,1,0:T(8,128)(2,1)}, bf16[8,192,128]{2,1,0:T(8,128)(2,1)}, u32[]{:S(2)}, u32[]{:S(2)}) collective-permute-start(bf16[8,192,128]{2,1,0:T(8,128)(2,1)} %get-tuple-element.114), channel_id=1, source_target_pairs={{0,30},{1,31},{2,28},{3,29},{4,26},{5,27},{6,24},{7,25},{8,22},{9,... | collective-permute-start | bytes 1179656 | tf_op jit(solution)/shard_map/ppermute | solution.py:276
  160.5 74.5 %collective-permute-start.18 = (bf16[8,192,128]{2,1,0:T(8,128)(2,1)}, bf16[8,192,128]{2,1,0:T(8,128)(2,1)}, u32[]{:S(2)}, u32[]{:S(2)}) collective-permute-start(bf16[8,192,128]{2,1,0:T(8,128)(2,1)} %get-tuple-element.115), channel_id=1, source_target_pairs={{0,27},{1,26},{2,25},{3,24},{4,31},{5,30},{6,29},{7,28},{8,19},{9,... | collective-permute-start | bytes 1179656 | tf_op jit(solution)/shard_map/ppermute | solution.py:276
  192.8 47.5 %collective-permute-start.19 = (bf16[8,192,128]{2,1,0:T(8,128)(2,1)}, bf16[8,192,128]{2,1,0:T(8,128)(2,1)}, u32[]{:S(2)}, u32[]{:S(2)}) collective-permute-start(bf16[8,192,128]{2,1,0:T(8,128)(2,1)} %get-tuple-element.116), channel_id=1, source_target_pairs={{0,29},{1,28},{2,31},{3,30},{4,25},{5,24},{6,27},{7,26},{8,21},{9,... | collective-permute-start | bytes 1179656 | tf_op jit(solution)/shard_map/ppermute | solution.py:276
  197.1 44.5 %collective-permute-start.20 = (bf16[8,192,128]{2,1,0:T(8,128)(2,1)}, bf16[8,192,128]{2,1,0:T(8,128)(2,1)}, u32[]{:S(2)}, u32[]{:S(2)}) collective-permute-start(bf16[8,192,128]{2,1,0:T(8,128)(2,1)} %get-tuple-element.117), channel_id=1, source_target_pairs={{0,1},{1,0},{2,3},{3,2},{4,5},{5,4},{6,7},{7,6},{8,9},{9,8},{10,11... | collective-permute-start | bytes 1179656 | tf_op jit(solution)/shard_map/ppermute | solution.py:276
  197.1 44.5 %collective-permute-start.21 = (bf16[8,192,128]{2,1,0:T(8,128)(2,1)}, bf16[8,192,128]{2,1,0:T(8,128)(2,1)}, u32[]{:S(2)}, u32[]{:S(2)}) collective-permute-start(bf16[8,192,128]{2,1,0:T(8,128)(2,1)} %get-tuple-element.118), channel_id=1, source_target_pairs={{0,14},{1,15},{2,12},{3,13},{4,10},{5,11},{6,8},{7,9},{8,6},{9,7},... | collective-permute-start | bytes 1179656 | tf_op jit(solution)/shard_map/ppermute | solution.py:276
  197.2 71.3 %collective-permute-start.22 = (bf16[8,192,128]{2,1,0:T(8,128)(2,1)}, bf16[8,192,128]{2,1,0:T(8,128)(2,1)}, u32[]{:S(2)}, u32[]{:S(2)}) collective-permute-start(bf16[8,192,128]{2,1,0:T(8,128)(2,1)} %get-tuple-element.119), channel_id=1, source_target_pairs={{0,19},{1,18},{2,17},{3,16},{4,23},{5,22},{6,21},{7,20},{8,27},{9,... | collective-permute-start | bytes 1179656 | tf_op jit(solution)/shard_map/ppermute | solution.py:276
  235.0 57.5 %collective-permute-start.23 = (bf16[8,192,128]{2,1,0:T(8,128)(2,1)}, bf16[8,192,128]{2,1,0:T(8,128)(2,1)S(1)}, u32[]{:S(2)}, u32[]{:S(2)}) collective-permute-start(bf16[8,192,128]{2,1,0:T(8,128)(2,1)} %get-tuple-element.120), channel_id=1, source_target_pairs={{0,13},{1,12},{2,15},{3,14},{4,9},{5,8},{6,11},{7,10},{8,5},{9,4},... | collective-permute-start | bytes 1179656 | tf_op jit(solution)/shard_map/ppermute | solution.py:276
  240.3 55.9 %collective-permute-start.24 = (bf16[8,192,128]{2,1,0:T(8,128)(2,1)}, bf16[8,192,128]{2,1,0:T(8,128)(2,1)}, u32[]{:S(2)}, u32[]{:S(2)}) collective-permute-start(bf16[8,192,128]{2,1,0:T(8,128)(2,1)} %get-tuple-element.121), channel_id=1, source_target_pairs={{0,25},{1,24},{2,27},{3,26},{4,29},{5,28},{6,31},{7,30},{8,17},{9,... | collective-permute-start | bytes 1179656 | tf_op jit(solution)/shard_map/ppermute | solution.py:276
  241.5 60.5 %collective-permute-start.25 = (bf16[8,192,128]{2,1,0:T(8,128)(2,1)}, bf16[8,192,128]{2,1,0:T(8,128)(2,1)}, u32[]{:S(2)}, u32[]{:S(2)}) collective-permute-start(bf16[8,192,128]{2,1,0:T(8,128)(2,1)} %get-tuple-element.122), channel_id=1, source_target_pairs={{0,21},{1,20},{2,23},{3,22},{4,17},{5,16},{6,19},{7,18},{8,29},{9,... | collective-permute-start | bytes 1179656 | tf_op jit(solution)/shard_map/ppermute | solution.py:276
  241.5 72.2 %collective-permute-start.26 = (bf16[8,192,128]{2,1,0:T(8,128)(2,1)}, bf16[8,192,128]{2,1,0:T(8,128)(2,1)}, u32[]{:S(2)}, u32[]{:S(2)}) collective-permute-start(bf16[8,192,128]{2,1,0:T(8,128)(2,1)} %get-tuple-element.123), channel_id=1, source_target_pairs={{0,20},{1,21},{2,22},{3,23},{4,16},{5,17},{6,18},{7,19},{8,28},{9,... | collective-permute-start | bytes 1179656 | tf_op jit(solution)/shard_map/ppermute | solution.py:276
  268.4 59.5 %collective-permute-start.27 = (bf16[8,192,128]{2,1,0:T(8,128)(2,1)}, bf16[8,192,128]{2,1,0:T(8,128)(2,1)}, u32[]{:S(2)}, u32[]{:S(2)}) collective-permute-start(bf16[8,192,128]{2,1,0:T(8,128)(2,1)} %get-tuple-element.124), channel_id=1, source_target_pairs={{0,28},{1,29},{2,30},{3,31},{4,24},{5,25},{6,26},{7,27},{8,20},{9,... | collective-permute-start | bytes 1179656 | tf_op jit(solution)/shard_map/ppermute | solution.py:276
  292.5 79.5 %collective-permute-start.4 = (bf16[8,192,128]{2,1,0:T(8,128)(2,1)}, bf16[8,192,128]{2,1,0:T(8,128)(2,1)}, u32[]{:S(2)}, u32[]{:S(2)}) collective-permute-start(bf16[8,192,128]{2,1,0:T(8,128)(2,1)} %get-tuple-element.101), channel_id=1, source_target_pairs={{0,8},{1,9},{2,10},{3,11},{4,12},{5,13},{6,14},{7,15},{8,0},{9,1},... | collective-permute-start | bytes 1179656 | tf_op jit(solution)/shard_map/ppermute | solution.py:276
  296.2 75.8 %collective-permute-start.5 = (bf16[8,192,128]{2,1,0:T(8,128)(2,1)}, bf16[8,192,128]{2,1,0:T(8,128)(2,1)}, u32[]{:S(2)}, u32[]{:S(2)}) collective-permute-start(bf16[8,192,128]{2,1,0:T(8,128)(2,1)} %get-tuple-element.102), channel_id=1, source_target_pairs={{0,10},{1,11},{2,8},{3,9},{4,14},{5,15},{6,12},{7,13},{8,2},{9,3},... | collective-permute-start | bytes 1179656 | tf_op jit(solution)/shard_map/ppermute | solution.py:276
  302.1 33.9 %collective-permute-start.28 = (bf16[8,192,128]{2,1,0:T(8,128)(2,1)}, bf16[8,192,128]{2,1,0:T(8,128)(2,1)}, u32[]{:S(2)}, u32[]{:S(2)}) collective-permute-start(bf16[8,192,128]{2,1,0:T(8,128)(2,1)} %get-tuple-element.125), channel_id=1, source_target_pairs={{0,17},{1,16},{2,19},{3,18},{4,21},{5,20},{6,23},{7,22},{8,25},{9,... | collective-permute-start | bytes 1179656 | tf_op jit(solution)/shard_map/ppermute | solution.py:276
  313.8 40.0 %collective-permute-start.29 = (bf16[8,192,128]{2,1,0:T(8,128)(2,1)}, bf16[8,192,128]{2,1,0:T(8,128)(2,1)}, u32[]{:S(2)}, u32[]{:S(2)}) collective-permute-start(bf16[8,192,128]{2,1,0:T(8,128)(2,1)} %get-tuple-element.126), channel_id=1, source_target_pairs={{0,5},{1,4},{2,7},{3,6},{4,1},{5,0},{6,3},{7,2},{8,13},{9,12},{10,... | collective-permute-start | bytes 1179656 | tf_op jit(solution)/shard_map/ppermute | solution.py:276
  327.9 47.4 %collective-permute-start.36 = (bf16[8,192,128]{2,1,0:T(8,128)(2,1)}, bf16[8,192,128]{2,1,0:T(8,128)(2,1)S(1)}, u32[]{:S(2)}, u32[]{:S(2)}) collective-permute-start(bf16[8,192,128]{2,1,0:T(8,128)(2,1)} %get-tuple-element.151), channel_id=1, source_target_pairs={{0,6},{1,7},{2,4},{3,5},{4,2},{5,3},{6,0},{7,1},{8,14},{9,15},{10,... | collective-permute-start | bytes 1179656 | tf_op jit(solution)/shard_map/ppermute | solution.py:276
  336.0 38.2 %collective-permute-start.34 = (f32[4,128]{1,0:T(4,128)S(1)}, f32[4,128]{1,0:T(4,128)S(1)}, u32[]{:S(2)}, u32[]{:S(2)}) collective-permute-start(f32[4,128]{1,0:T(4,128)S(1)} %slice_reduce_fusion), channel_id=1, source_target_pairs={{0,1},{1,2},{2,3},{3,4},{4,5},{5,6},{6,7},{7,0},{8,9},{9,10},{10,1... | collective-permute-start | bytes 6152 | tf_op jit(solution)/shard_map/ppermute | solution.py:26
  353.7 20.4 %collective-permute-start.35 = (f32[4,64]{1,0:T(4,128)S(1)}, f32[4,64]{1,0:T(4,128)S(1)}, u32[]{:S(2)}, u32[]{:S(2)}) collective-permute-start(f32[4,64]{1,0:T(4,128)S(1)} %bitcast.82), channel_id=1, source_target_pairs={{0,8},{8,16},{16,24},{24,0},{1,9},{9,17},{17,25},{25,1},{2,10},{10... | collective-permute-start | bytes 3080 | tf_op jit(solution)/shard_map/ppermute | solution.py:26
  (30 other events, 2320.6 us)

commit v4 on v3

--- a/solution.py
+++ b/solution.py
@@ -11,7 +11,7 @@
 STEPS = 3
 RAW = 2
 GROUP = 4
-LEAD = 4
+LEAD = 6
 
 
 diffusion = 0.2
@@ -33,6 +33,8 @@
     far = sorted([k for k in range(1, devices) if k & far_bit], key=turns)
     near = [k for k in range(1, devices) if not k & far_bit]
     near.sort(key=lambda k: (not k & row_bit, not k & col_bit, k))
+    quarter = len(far) // 4
+    far[quarter : 2 * quarter] = far[quarter : 2 * quarter][::-1]
     far.append(far.pop(len(far) // 2))
     order = far[:LEAD]
     for k in far[LEAD:-1]:
@@ -63,10 +65,11 @@
         send(*step).wait()
 
 
-def first_kernel(capacity, partner, me_ref, owner_ref, macro_ref, states_ref, out_ref, row_ref, col_ref, *scratch):
+def first_kernel(capacity, partner, owner_ref, macro_ref, states_ref, out_ref, row_ref, col_ref, *scratch):
     slot_ref, macro_buffer, macro_sem, in_sem = scratch
     slot_total = owner_ref.shape[0]
-    owner = jnp.bitwise_xor(me_ref[0], partner)
+    me = lax.axis_index("gx") * lax.axis_size("gy") + lax.axis_index("gy")
+    owner = jnp.bitwise_xor(me.astype(jnp.int32), partner)
     fields = pltpu.make_async_copy(macro_ref, macro_buffer, macro_sem)
     fields.start()
 
@@ -292,7 +295,7 @@
             pltpu.VMEM((channels, tile_cols), jnp.float32),
             pltpu.VMEM((channels, tile_rows), jnp.float32),
         ],
-        in_specs=[SMEM, SMEM, ANY, ANY],
+        in_specs=[SMEM, ANY, ANY],
         out_specs=[VMEM, VMEM, VMEM],
         scratch_shapes=[
             pltpu.SMEM((slot_total,), jnp.int32),
@@ -301,7 +304,7 @@
             pltpu.SemaphoreType.DMA((capacity,)),
         ],
         name="first",
-    )(me_ref, owner.reshape(slot_total), fields, states)
+    )(owner.reshape(slot_total), fields, states)
     owners, raw_first = lax.optimization_barrier((owner.reshape(slot_total), raw_first))
     next_row = passed_along(first_row, "gx", -1)
     next_col = passed_along(first_col, "gy", -1)

time: 378 us -> 366 us (0.968)
  the two profiles are of different devices: /device:TPU:0 before, /device:TPU:29 now
where the time goes in v4:
time: 366 us; the launch traced here: 365 us
  starting transfers between devices  152 us (42%)
  waiting for transfers between devices  111 us (30%)
  Pallas kernels  88.4 us (24%)
  local copies, waits for them, and re-layouts  8.58 us (2%)
    ppermute x33, starting transfers between devices, exchanged(): lax.ppermute(value, ('gx', 'gy'), [(source, source ^ k) for source in ran...  127 us
    ppermute x33, waiting for transfers between devices, exchanged(): lax.ppermute(value, ('gx', 'gy'), [(source, source ^ k) for source in ran...  111 us
    pallas_call x9, Pallas kernels, per_device(): pl.pallas_call(functools.partial(relax_kernel, capacity, partners, kept,...  54.7 us
    ppermute x4, starting transfers between devices, passed_along(): return lax.ppermute(value, axis, pairs)  24.3 us
    pallas_call x7, Pallas kernels, put(): pl.pallas_call(functools.partial(put_kernel, partners), out_shape=whole,...  15.4 us
  transfers between devices with their start and end apart: 37, of which 13 were waited for; matrix products, arithmetic and copies ran while one was open for 2% of the time, Pallas kernels for 24%

profile of v4, /device:TPU:29, one launch (start us, length us, event | category | flops | bytes accessed | tf_op | source)
XLA Modules:
  0.0 365.0 jit_solution(8024569982051804752)
XLA Ops:
  5.0 4.7 %route.1 = (s32[256]{0:T(256)}, s32[256]{0:T(256)}, bf16[8,192,128]{2,1,0:T(8,128)(2,1)}) custom-call(s32[1]{0:T(128)} %bitcast.me_ref, s32[256]{0:T(256)} %bitcast.80, s32[256]{0:T(256)} %bitcast.84, bf16[256,192,128]{2,1,0:T(8,128)(2,1)} %bitcast.45), custom_call_target="tpu_custom_call" | custom-call | tf_op jit(solution)/shard_map/route/pallas_call | solution.py:312
  17.3 2.9 forcing.1
  20.3 4.9 %shard_map.86 = (bf16[8,192,128]{2,1,0:T(8,128)(2,1)}, bf16[8,192,128]{2,1,0:T(8,128)(2,1)}, f32[16,128]{1,0:T(8,128)}) custom-call(s32[1]{0:T(128)} %bitcast.me_ref, s32[256]{0:T(256)} %get-tuple-element.132.table_ref, bf16[256,192,128]{2,1,0:T(8,128)(2,1)} %bitcast.46, f32[256,128]{1,0:T(8,128)} %get-tuple-element.83.force_ref, ...), custom_call_target="tpu_custom_call" | custom-call | tf_op jit(solution)/shard_map/pallas_call | solution.py:350
  25.2 6.5 %shard_map.87 = (bf16[8,192,128]{2,1,0:T(8,128)(2,1)}, bf16[8,192,128]{2,1,0:T(8,128)(2,1)}, bf16[8,192,128]{2,1,0:T(8,128)(2,1)}, bf16[8,192,128]{2,1,0:T(8,128)(2,1)}, f32[32,128]{1,0:T(8,128)}) custom-call(s32[1]{0:T(128)} %bitcast.me_ref, s32[256]{0:T(256)} %get-tuple-element.132.table_ref, bf16[256,192,128]{2,1,0:T(8,128)(2,1)} %bitcast.47, ...), custom_call_target="tpu_custom_call" | custom-call | tf_op jit(solution)/shard_map/pallas_call | solution.py:350
  31.7 6.5 %shard_map.88 = (bf16[8,192,128]{2,1,0:T(8,128)(2,1)}, bf16[8,192,128]{2,1,0:T(8,128)(2,1)}, bf16[8,192,128]{2,1,0:T(8,128)(2,1)}, bf16[8,192,128]{2,1,0:T(8,128)(2,1)}, f32[32,128]{1,0:T(8,128)}) custom-call(s32[1]{0:T(128)} %bitcast.me_ref, s32[256]{0:T(256)} %get-tuple-element.132.table_ref, bf16[256,192,128]{2,1,0:T(8,128)(2,1)} %bitcast.48, ...), custom_call_target="tpu_custom_call" | custom-call | tf_op jit(solution)/shard_map/pallas_call | solution.py:350
  38.2 6.6 %shard_map.89 = (bf16[8,192,128]{2,1,0:T(8,128)(2,1)}, bf16[8,192,128]{2,1,0:T(8,128)(2,1)}, bf16[8,192,128]{2,1,0:T(8,128)(2,1)}, bf16[8,192,128]{2,1,0:T(8,128)(2,1)}, f32[32,128]{1,0:T(8,128)}) custom-call(s32[1]{0:T(128)} %bitcast.me_ref, s32[256]{0:T(256)} %get-tuple-element.132.table_ref, bf16[256,192,128]{2,1,0:T(8,128)(2,1)} %bitcast.49, ...), custom_call_target="tpu_custom_call" | custom-call | tf_op jit(solution)/shard_map/pallas_call | solution.py:350
  44.8 6.5 %shard_map.90 = (bf16[8,192,128]{2,1,0:T(8,128)(2,1)}, bf16[8,192,128]{2,1,0:T(8,128)(2,1)}, bf16[8,192,128]{2,1,0:T(8,128)(2,1)}, bf16[8,192,128]{2,1,0:T(8,128)(2,1)}, f32[32,128]{1,0:T(8,128)}) custom-call(s32[1]{0:T(128)} %bitcast.me_ref, s32[256]{0:T(256)} %get-tuple-element.132.table_ref, bf16[256,192,128]{2,1,0:T(8,128)(2,1)} %bitcast.50, ...), custom_call_target="tpu_custom_call" | custom-call | tf_op jit(solution)/shard_map/pallas_call | solution.py:350
  51.3 6.5 %shard_map.91 = (bf16[8,192,128]{2,1,0:T(8,128)(2,1)}, bf16[8,192,128]{2,1,0:T(8,128)(2,1)}, bf16[8,192,128]{2,1,0:T(8,128)(2,1)}, bf16[8,192,128]{2,1,0:T(8,128)(2,1)}, f32[32,128]{1,0:T(8,128)}) custom-call(s32[1]{0:T(128)} %bitcast.me_ref, s32[256]{0:T(256)} %get-tuple-element.132.table_ref, bf16[256,192,128]{2,1,0:T(8,128)(2,1)} %bitcast.51, ...), custom_call_target="tpu_custom_call" | custom-call | tf_op jit(solution)/shard_map/pallas_call | solution.py:350
  57.8 6.5 %shard_map.92 = (bf16[8,192,128]{2,1,0:T(8,128)(2,1)}, bf16[8,192,128]{2,1,0:T(8,128)(2,1)}, bf16[8,192,128]{2,1,0:T(8,128)(2,1)}, bf16[8,192,128]{2,1,0:T(8,128)(2,1)}, f32[32,128]{1,0:T(8,128)}) custom-call(s32[1]{0:T(128)} %bitcast.me_ref, s32[256]{0:T(256)} %get-tuple-element.132.table_ref, bf16[256,192,128]{2,1,0:T(8,128)(2,1)} %bitcast.52, ...), custom_call_target="tpu_custom_call" | custom-call | tf_op jit(solution)/shard_map/pallas_call | solution.py:350
  66.6 5.8 %shard_map.93 = (bf16[8,192,128]{2,1,0:T(8,128)(2,1)}, bf16[8,192,128]{2,1,0:T(8,128)(2,1)}, bf16[8,192,128]{2,1,0:T(8,128)(2,1)}, f32[32,128]{1,0:T(8,128)}) custom-call(s32[1]{0:T(128)} %bitcast.me_ref, s32[256]{0:T(256)} %get-tuple-element.132.table_ref, bf16[256,192,128]{2,1,0:T(8,128)(2,1)} %bitcast.53, f32[256,128]{1,0:T(8,128)} %get-tuple-element.83.force_ref, ...), custom_call_target="tpu_custom_call" | custom-call | tf_op jit(solution)/shard_map/pallas_call | solution.py:350
  75.0 4.9 %shard_map.94 = (bf16[32,8,192,128]{3,2,1,0:T(8,128)(2,1)}, f32[16,128]{1,0:T(8,128)}) custom-call(s32[1]{0:T(128)} %bitcast.me_ref, s32[256]{0:T(256)} %get-tuple-element.132.table_ref, bf16[256,192,128]{2,1,0:T(8,128)(2,1)} %bitcast.54, f32[256,128]{1,0:T(8,128)} %get-tuple-element.83.force_ref, f32[256,128]{1,0:T(8,128)} %get-tuple-element.84.live_ref, ...), custom_call_target="tpu_custom_call" | custom-call | tf_op jit(solution)/shard_map/pallas_call | solution.py:350
  83.2 5.8 %collective-permute-start.7 = (bf16[8,192,128]{2,1,0:T(8,128)(2,1)}, bf16[8,192,128]{2,1,0:T(8,128)(2,1)S(1)}, u32[]{:S(2)}, u32[]{:S(2)}) collective-permute-start(bf16[8,192,128]{2,1,0:T(8,128)(2,1)} %get-tuple-element.104), channel_id=1, source_target_pairs={{0,31},{1,30},{2,29},{3,28},{4,27},{5,26},{6,25},{7,24},{8,23},{9,... | collective-permute-start | bytes 1179656 | tf_op jit(solution)/shard_map/ppermute | solution.py:279
  91.8 4.1 %collective-permute-start.10 = (bf16[8,192,128]{2,1,0:T(8,128)(2,1)}, bf16[8,192,128]{2,1,0:T(8,128)(2,1)}, u32[]{:S(2)}, u32[]{:S(2)}) collective-permute-start(bf16[8,192,128]{2,1,0:T(8,128)(2,1)} %get-tuple-element.107), channel_id=1, source_target_pairs={{0,9},{1,8},{2,11},{3,10},{4,13},{5,12},{6,15},{7,14},{8,1},{9,0},... | collective-permute-start | bytes 1179656 | tf_op jit(solution)/shard_map/ppermute | solution.py:279
  95.9 8.6 %collective-permute-done.6.rest_0_ = bf16[8,192,128]{2,1,0:T(8,128)(2,1)S(1)} collective-permute-done((bf16[8,192,128]{2,1,0:T(8,128)(2,1)}, bf16[8,192,128]{2,1,0:T(8,128)(2,1)S(1)}, u32[]{:S(2)}, u32[]{:S(2)}) %collective-permute-start.6) | collective-permute-done | bytes 393248 | tf_op jit(solution)/shard_map/ppermute | solution.py:279
  104.5 7.1 %collective-permute-start.12 = (bf16[8,192,128]{2,1,0:T(8,128)(2,1)}, bf16[8,192,128]{2,1,0:T(8,128)(2,1)}, u32[]{:S(2)}, u32[]{:S(2)}) collective-permute-start(bf16[8,192,128]{2,1,0:T(8,128)(2,1)} %get-tuple-element.109), channel_id=1, source_target_pairs={{0,11},{1,10},{2,9},{3,8},{4,15},{5,14},{6,13},{7,12},{8,3},{9,2},... | collective-permute-start | bytes 1179656 | tf_op jit(solution)/shard_map/ppermute | solution.py:279
  123.9 4.0 %collective-permute-start.16 = (bf16[8,192,128]{2,1,0:T(8,128)(2,1)}, bf16[8,192,128]{2,1,0:T(8,128)(2,1)}, u32[]{:S(2)}, u32[]{:S(2)}) collective-permute-start(bf16[8,192,128]{2,1,0:T(8,128)(2,1)} %get-tuple-element.113), channel_id=1, source_target_pairs={{0,3},{1,2},{2,1},{3,0},{4,7},{5,6},{6,5},{7,4},{8,11},{9,10},{10,... | collective-permute-start | bytes 1179656 | tf_op jit(solution)/shard_map/ppermute | solution.py:279
  127.9 8.1 %collective-permute-done.12.rest_2_ = bf16[8,192,128]{2,1,0:T(8,128)(2,1)} collective-permute-done((bf16[8,192,128]{2,1,0:T(8,128)(2,1)}, bf16[8,192,128]{2,1,0:T(8,128)(2,1)}, u32[]{:S(2)}, u32[]{:S(2)}) %collective-permute-start.12) | collective-permute-done | bytes 393248 | tf_op jit(solution)/shard_map/ppermute | solution.py:279
  138.7 9.1 %collective-permute-done.13.rest_3_ = bf16[8,192,128]{2,1,0:T(8,128)(2,1)} collective-permute-done((bf16[8,192,128]{2,1,0:T(8,128)(2,1)}, bf16[8,192,128]{2,1,0:T(8,128)(2,1)}, u32[]{:S(2)}, u32[]{:S(2)}) %collective-permute-start.13) | collective-permute-done | bytes 393248 | tf_op jit(solution)/shard_map/ppermute | solution.py:279
  147.8 9.6 %collective-permute-start.18 = (bf16[8,192,128]{2,1,0:T(8,128)(2,1)}, bf16[8,192,128]{2,1,0:T(8,128)(2,1)}, u32[]{:S(2)}, u32[]{:S(2)}) collective-permute-start(bf16[8,192,128]{2,1,0:T(8,128)(2,1)} %get-tuple-element.115), channel_id=1, source_target_pairs={{0,25},{1,24},{2,27},{3,26},{4,29},{5,28},{6,31},{7,30},{8,17},{9,... | collective-permute-start | bytes 1179656 | tf_op jit(solution)/shard_map/ppermute | solution.py:279
  158.5 24.8 %collective-permute-start.20 = (bf16[8,192,128]{2,1,0:T(8,128)(2,1)}, bf16[8,192,128]{2,1,0:T(8,128)(2,1)}, u32[]{:S(2)}, u32[]{:S(2)}) collective-permute-start(bf16[8,192,128]{2,1,0:T(8,128)(2,1)} %get-tuple-element.117), channel_id=1, source_target_pairs={{0,27},{1,26},{2,25},{3,24},{4,31},{5,30},{6,29},{7,28},{8,19},{9,... | collective-permute-start | bytes 1179656 | tf_op jit(solution)/shard_map/ppermute | solution.py:279
  186.2 4.2 %collective-permute-start.22 = (bf16[8,192,128]{2,1,0:T(8,128)(2,1)}, bf16[8,192,128]{2,1,0:T(8,128)(2,1)}, u32[]{:S(2)}, u32[]{:S(2)}) collective-permute-start(bf16[8,192,128]{2,1,0:T(8,128)(2,1)} %get-tuple-element.119), channel_id=1, source_target_pairs={{0,17},{1,16},{2,19},{3,18},{4,21},{5,20},{6,23},{7,22},{8,25},{9,... | collective-permute-start | bytes 1179656 | tf_op jit(solution)/shard_map/ppermute | solution.py:279
  190.3 11.3 %collective-permute-start.23 = (bf16[8,192,128]{2,1,0:T(8,128)(2,1)}, bf16[8,192,128]{2,1,0:T(8,128)(2,1)S(1)}, u32[]{:S(2)}, u32[]{:S(2)}) collective-permute-start(bf16[8,192,128]{2,1,0:T(8,128)(2,1)} %get-tuple-element.120), channel_id=1, source_target_pairs={{0,13},{1,12},{2,15},{3,14},{4,9},{5,8},{6,11},{7,10},{8,5},{9,4},... | collective-permute-start | bytes 1179656 | tf_op jit(solution)/shard_map/ppermute | solution.py:279
  201.6 22.3 %collective-permute-start.24 = (bf16[8,192,128]{2,1,0:T(8,128)(2,1)}, bf16[8,192,128]{2,1,0:T(8,128)(2,1)}, u32[]{:S(2)}, u32[]{:S(2)}) collective-permute-start(bf16[8,192,128]{2,1,0:T(8,128)(2,1)} %get-tuple-element.121), channel_id=1, source_target_pairs={{0,19},{1,18},{2,17},{3,16},{4,23},{5,22},{6,21},{7,20},{8,27},{9,... | collective-permute-start | bytes 1179656 | tf_op jit(solution)/shard_map/ppermute | solution.py:279
  225.6 9.3 %collective-permute-start.26 = (bf16[8,192,128]{2,1,0:T(8,128)(2,1)}, bf16[8,192,128]{2,1,0:T(8,128)(2,1)}, u32[]{:S(2)}, u32[]{:S(2)}) collective-permute-start(bf16[8,192,128]{2,1,0:T(8,128)(2,1)} %get-tuple-element.123), channel_id=1, source_target_pairs={{0,20},{1,21},{2,22},{3,23},{4,16},{5,17},{6,18},{7,19},{8,28},{9,... | collective-permute-start | bytes 1179656 | tf_op jit(solution)/shard_map/ppermute | solution.py:279
  237.3 3.3 flux.1
  240.7 31.9 %collective-permute-done.23.rest_1_ = bf16[8,192,128]{2,1,0:T(8,128)(2,1)S(1)} collective-permute-done((bf16[8,192,128]{2,1,0:T(8,128)(2,1)}, bf16[8,192,128]{2,1,0:T(8,128)(2,1)S(1)}, u32[]{:S(2)}, u32[]{:S(2)}) %collective-permute-start.23) | collective-permute-done | bytes 393248 | tf_op jit(solution)/shard_map/ppermute | solution.py:279
  272.7 8.1 %collective-permute-done.25.rest_3_ = bf16[8,192,128]{2,1,0:T(8,128)(2,1)} collective-permute-done((bf16[8,192,128]{2,1,0:T(8,128)(2,1)}, bf16[8,192,128]{2,1,0:T(8,128)(2,1)}, u32[]{:S(2)}, u32[]{:S(2)}) %collective-permute-start.25) | collective-permute-done | bytes 393248 | tf_op jit(solution)/shard_map/ppermute | solution.py:279
  280.8 22.4 %collective-permute-done.26.rest_0_ = bf16[8,192,128]{2,1,0:T(8,128)(2,1)} collective-permute-done((bf16[8,192,128]{2,1,0:T(8,128)(2,1)}, bf16[8,192,128]{2,1,0:T(8,128)(2,1)}, u32[]{:S(2)}, u32[]{:S(2)}) %collective-permute-start.26) | collective-permute-done | bytes 393248 | tf_op jit(solution)/shard_map/ppermute | solution.py:279
  304.2 11.3 %collective-permute-done.27.rest_1_ = bf16[8,192,128]{2,1,0:T(8,128)(2,1)} collective-permute-done((bf16[8,192,128]{2,1,0:T(8,128)(2,1)}, bf16[8,192,128]{2,1,0:T(8,128)(2,1)}, u32[]{:S(2)}, u32[]{:S(2)}) %collective-permute-start.27) | collective-permute-done | bytes 393248 | tf_op jit(solution)/shard_map/ppermute | solution.py:279
  317.0 3.1 collective-permute-done.28.rest_2_
  320.1 12.3 %collective-permute-start.34 = (f32[4,128]{1,0:T(4,128)S(1)}, f32[4,128]{1,0:T(4,128)S(1)}, u32[]{:S(2)}, u32[]{:S(2)}) collective-permute-start(f32[4,128]{1,0:T(4,128)S(1)} %slice_reduce_fusion), channel_id=1, source_target_pairs={{0,1},{1,2},{2,3},{3,4},{4,5},{5,6},{6,7},{7,0},{8,9},{9,10},{10,1... | collective-permute-start | bytes 6152 | tf_op jit(solution)/shard_map/ppermute | solution.py:26
  332.5 10.2 %collective-permute-start.35 = (f32[4,64]{1,0:T(4,128)S(1)}, f32[4,64]{1,0:T(4,128)S(1)}, u32[]{:S(2)}, u32[]{:S(2)}) collective-permute-start(f32[4,64]{1,0:T(4,128)S(1)} %bitcast.82), channel_id=1, source_target_pairs={{0,8},{8,16},{16,24},{24,0},{1,9},{9,17},{17,25},{25,1},{2,10},{10... | collective-permute-start | bytes 3080 | tf_op jit(solution)/shard_map/ppermute | solution.py:26
  (165 shorter events, 70.4 us)
Async XLA Ops:
  9.7 72.8 %collective-permute-start.30 = (bf16[8,192,128]{2,1,0:T(8,128)(2,1)}, bf16[8,192,128]{2,1,0:T(8,128)(2,1)S(1)}, u32[]{:S(2)}, u32[]{:S(2)}) collective-permute-start(bf16[8,192,128]{2,1,0:T(8,128)(2,1)} %get-tuple-element.127), channel_id=1, source_target_pairs={{0,12},{1,13},{2,14},{3,15},{4,8},{5,9},{6,10},{7,11},{8,4},{9,5},... | collective-permute-start | bytes 1179656 | tf_op jit(solution)/shard_map/ppermute | solution.py:279
  10.0 79.0 %collective-permute-start.32 = (bf16[8,192,128]{2,1,0:T(8,128)(2,1)S(1)}, bf16[8,192,128]{2,1,0:T(8,128)(2,1)}, u32[]{:S(2)}, u32[]{:S(2)}) collective-permute-start(bf16[8,192,128]{2,1,0:T(8,128)(2,1)S(1)} %get-tuple-element.129), channel_id=1, source_target_pairs={{0,4},{1,5},{2,6},{3,7},{4,0},{5,1},{6,2},{7,3},{8,12},{9,13},{10,... | collective-permute-start | bytes 1179656 | tf_op jit(solution)/shard_map/ppermute | solution.py:279
  64.3 24.9 %collective-permute-start.2 = (bf16[8,192,128]{2,1,0:T(8,128)(2,1)}, bf16[8,192,128]{2,1,0:T(8,128)(2,1)S(1)}, u32[]{:S(2)}, u32[]{:S(2)}) collective-permute-start(bf16[8,192,128]{2,1,0:T(8,128)(2,1)} %get-tuple-element.97), channel_id=1, source_target_pairs={{0,26},{1,27},{2,24},{3,25},{4,30},{5,31},{6,28},{7,29},{8,18},{9,... | collective-permute-start | bytes 1179656 | tf_op jit(solution)/shard_map/ppermute | solution.py:279
  82.1 22.4 %collective-permute-start.6 = (bf16[8,192,128]{2,1,0:T(8,128)(2,1)}, bf16[8,192,128]{2,1,0:T(8,128)(2,1)S(1)}, u32[]{:S(2)}, u32[]{:S(2)}) collective-permute-start(bf16[8,192,128]{2,1,0:T(8,128)(2,1)} %get-tuple-element.103), channel_id=1, source_target_pairs={{0,16},{1,17},{2,18},{3,19},{4,20},{5,21},{6,22},{7,23},{8,24},{9,... | collective-permute-start | bytes 1179656 | tf_op jit(solution)/shard_map/ppermute | solution.py:279
  83.2 21.3 %collective-permute-start.7 = (bf16[8,192,128]{2,1,0:T(8,128)(2,1)}, bf16[8,192,128]{2,1,0:T(8,128)(2,1)S(1)}, u32[]{:S(2)}, u32[]{:S(2)}) collective-permute-start(bf16[8,192,128]{2,1,0:T(8,128)(2,1)} %get-tuple-element.104), channel_id=1, source_target_pairs={{0,31},{1,30},{2,29},{3,28},{4,27},{5,26},{6,25},{7,24},{8,23},{9,... | collective-permute-start | bytes 1179656 | tf_op jit(solution)/shard_map/ppermute | solution.py:279
  89.0 24.8 %collective-permute-start.8 = (bf16[8,192,128]{2,1,0:T(8,128)(2,1)}, bf16[8,192,128]{2,1,0:T(8,128)(2,1)}, u32[]{:S(2)}, u32[]{:S(2)}) collective-permute-start(bf16[8,192,128]{2,1,0:T(8,128)(2,1)} %get-tuple-element.105), channel_id=1, source_target_pairs={{0,18},{1,19},{2,16},{3,17},{4,22},{5,23},{6,20},{7,21},{8,26},{9,... | collective-permute-start | bytes 1179656 | tf_op jit(solution)/shard_map/ppermute | solution.py:279
  89.2 29.6 %collective-permute-start.9 = (bf16[8,192,128]{2,1,0:T(8,128)(2,1)}, bf16[8,192,128]{2,1,0:T(8,128)(2,1)}, u32[]{:S(2)}, u32[]{:S(2)}) collective-permute-start(bf16[8,192,128]{2,1,0:T(8,128)(2,1)} %get-tuple-element.106), channel_id=1, source_target_pairs={{0,24},{1,25},{2,26},{3,27},{4,28},{5,29},{6,30},{7,31},{8,16},{9,... | collective-permute-start | bytes 1179656 | tf_op jit(solution)/shard_map/ppermute | solution.py:279
  91.8 27.5 %collective-permute-start.10 = (bf16[8,192,128]{2,1,0:T(8,128)(2,1)}, bf16[8,192,128]{2,1,0:T(8,128)(2,1)}, u32[]{:S(2)}, u32[]{:S(2)}) collective-permute-start(bf16[8,192,128]{2,1,0:T(8,128)(2,1)} %get-tuple-element.107), channel_id=1, source_target_pairs={{0,9},{1,8},{2,11},{3,10},{4,13},{5,12},{6,15},{7,14},{8,1},{9,0},... | collective-permute-start | bytes 1179656 | tf_op jit(solution)/shard_map/ppermute | solution.py:279
  104.5 19.4 %collective-permute-start.11 = (bf16[8,192,128]{2,1,0:T(8,128)(2,1)}, bf16[8,192,128]{2,1,0:T(8,128)(2,1)}, u32[]{:S(2)}, u32[]{:S(2)}) collective-permute-start(bf16[8,192,128]{2,1,0:T(8,128)(2,1)} %get-tuple-element.108), channel_id=1, source_target_pairs={{0,15},{1,14},{2,13},{3,12},{4,11},{5,10},{6,9},{7,8},{8,7},{9,6},... | collective-permute-start | bytes 1179656 | tf_op jit(solution)/shard_map/ppermute | solution.py:279
  104.5 31.5 %collective-permute-start.12 = (bf16[8,192,128]{2,1,0:T(8,128)(2,1)}, bf16[8,192,128]{2,1,0:T(8,128)(2,1)}, u32[]{:S(2)}, u32[]{:S(2)}) collective-permute-start(bf16[8,192,128]{2,1,0:T(8,128)(2,1)} %get-tuple-element.109), channel_id=1, source_target_pairs={{0,11},{1,10},{2,9},{3,8},{4,15},{5,14},{6,13},{7,12},{8,3},{9,2},... | collective-permute-start | bytes 1179656 | tf_op jit(solution)/shard_map/ppermute | solution.py:279
  113.8 34.0 %collective-permute-start.13 = (bf16[8,192,128]{2,1,0:T(8,128)(2,1)}, bf16[8,192,128]{2,1,0:T(8,128)(2,1)}, u32[]{:S(2)}, u32[]{:S(2)}) collective-permute-start(bf16[8,192,128]{2,1,0:T(8,128)(2,1)} %get-tuple-element.110), channel_id=1, source_target_pairs={{0,23},{1,22},{2,21},{3,20},{4,19},{5,18},{6,17},{7,16},{8,31},{9,... | collective-permute-start | bytes 1179656 | tf_op jit(solution)/shard_map/ppermute | solution.py:279
  118.8 38.9 %collective-permute-start.14 = (bf16[8,192,128]{2,1,0:T(8,128)(2,1)}, bf16[8,192,128]{2,1,0:T(8,128)(2,1)}, u32[]{:S(2)}, u32[]{:S(2)}) collective-permute-start(bf16[8,192,128]{2,1,0:T(8,128)(2,1)} %get-tuple-element.111), channel_id=1, source_target_pairs={{0,1},{1,0},{2,3},{3,2},{4,5},{5,4},{6,7},{7,6},{8,9},{9,8},{10,11... | collective-permute-start | bytes 1179656 | tf_op jit(solution)/shard_map/ppermute | solution.py:279
  119.3 39.2 %collective-permute-start.15 = (bf16[8,192,128]{2,1,0:T(8,128)(2,1)}, bf16[8,192,128]{2,1,0:T(8,128)(2,1)}, u32[]{:S(2)}, u32[]{:S(2)}) collective-permute-start(bf16[8,192,128]{2,1,0:T(8,128)(2,1)} %get-tuple-element.112), channel_id=1, source_target_pairs={{0,30},{1,31},{2,28},{3,29},{4,26},{5,27},{6,24},{7,25},{8,22},{9,... | collective-permute-start | bytes 1179656 | tf_op jit(solution)/shard_map/ppermute | solution.py:279
  123.9 59.4 %collective-permute-start.16 = (bf16[8,192,128]{2,1,0:T(8,128)(2,1)}, bf16[8,192,128]{2,1,0:T(8,128)(2,1)}, u32[]{:S(2)}, u32[]{:S(2)}) collective-permute-start(bf16[8,192,128]{2,1,0:T(8,128)(2,1)} %get-tuple-element.113), channel_id=1, source_target_pairs={{0,3},{1,2},{2,1},{3,0},{4,7},{5,6},{6,5},{7,4},{8,11},{9,10},{10,... | collective-permute-start | bytes 1179656 | tf_op jit(solution)/shard_map/ppermute | solution.py:279
  136.0 50.2 %collective-permute-start.17 = (bf16[8,192,128]{2,1,0:T(8,128)(2,1)}, bf16[8,192,128]{2,1,0:T(8,128)(2,1)}, u32[]{:S(2)}, u32[]{:S(2)}) collective-permute-start(bf16[8,192,128]{2,1,0:T(8,128)(2,1)} %get-tuple-element.114), channel_id=1, source_target_pairs={{0,7},{1,6},{2,5},{3,4},{4,3},{5,2},{6,1},{7,0},{8,15},{9,14},{10,... | collective-permute-start | bytes 1179656 | tf_op jit(solution)/shard_map/ppermute | solution.py:279
  147.8 42.5 %collective-permute-start.18 = (bf16[8,192,128]{2,1,0:T(8,128)(2,1)}, bf16[8,192,128]{2,1,0:T(8,128)(2,1)}, u32[]{:S(2)}, u32[]{:S(2)}) collective-permute-start(bf16[8,192,128]{2,1,0:T(8,128)(2,1)} %get-tuple-element.115), channel_id=1, source_target_pairs={{0,25},{1,24},{2,27},{3,26},{4,29},{5,28},{6,31},{7,30},{8,17},{9,... | collective-permute-start | bytes 1179656 | tf_op jit(solution)/shard_map/ppermute | solution.py:279
  157.7 44.0 %collective-permute-start.19 = (bf16[8,192,128]{2,1,0:T(8,128)(2,1)}, bf16[8,192,128]{2,1,0:T(8,128)(2,1)}, u32[]{:S(2)}, u32[]{:S(2)}) collective-permute-start(bf16[8,192,128]{2,1,0:T(8,128)(2,1)} %get-tuple-element.116), channel_id=1, source_target_pairs={{0,14},{1,15},{2,12},{3,13},{4,10},{5,11},{6,8},{7,9},{8,6},{9,7},... | collective-permute-start | bytes 1179656 | tf_op jit(solution)/shard_map/ppermute | solution.py:279
  158.5 65.4 %collective-permute-start.20 = (bf16[8,192,128]{2,1,0:T(8,128)(2,1)}, bf16[8,192,128]{2,1,0:T(8,128)(2,1)}, u32[]{:S(2)}, u32[]{:S(2)}) collective-permute-start(bf16[8,192,128]{2,1,0:T(8,128)(2,1)} %get-tuple-element.117), channel_id=1, source_target_pairs={{0,27},{1,26},{2,25},{3,24},{4,31},{5,30},{6,29},{7,28},{8,19},{9,... | collective-permute-start | bytes 1179656 | tf_op jit(solution)/shard_map/ppermute | solution.py:279
  183.3 42.3 %collective-permute-start.21 = (bf16[8,192,128]{2,1,0:T(8,128)(2,1)}, bf16[8,192,128]{2,1,0:T(8,128)(2,1)}, u32[]{:S(2)}, u32[]{:S(2)}) collective-permute-start(bf16[8,192,128]{2,1,0:T(8,128)(2,1)} %get-tuple-element.118), channel_id=1, source_target_pairs={{0,22},{1,23},{2,20},{3,21},{4,18},{5,19},{6,16},{7,17},{8,30},{9,... | collective-permute-start | bytes 1179656 | tf_op jit(solution)/shard_map/ppermute | solution.py:279
  186.2 48.8 %collective-permute-start.22 = (bf16[8,192,128]{2,1,0:T(8,128)(2,1)}, bf16[8,192,128]{2,1,0:T(8,128)(2,1)}, u32[]{:S(2)}, u32[]{:S(2)}) collective-permute-start(bf16[8,192,128]{2,1,0:T(8,128)(2,1)} %get-tuple-element.119), channel_id=1, source_target_pairs={{0,17},{1,16},{2,19},{3,18},{4,21},{5,20},{6,23},{7,22},{8,25},{9,... | collective-permute-start | bytes 1179656 | tf_op jit(solution)/shard_map/ppermute | solution.py:279
  190.3 82.2 %collective-permute-start.23 = (bf16[8,192,128]{2,1,0:T(8,128)(2,1)}, bf16[8,192,128]{2,1,0:T(8,128)(2,1)S(1)}, u32[]{:S(2)}, u32[]{:S(2)}) collective-permute-start(bf16[8,192,128]{2,1,0:T(8,128)(2,1)} %get-tuple-element.120), channel_id=1, source_target_pairs={{0,13},{1,12},{2,15},{3,14},{4,9},{5,8},{6,11},{7,10},{8,5},{9,4},... | collective-permute-start | bytes 1179656 | tf_op jit(solution)/shard_map/ppermute | solution.py:279
  201.6 71.0 %collective-permute-start.24 = (bf16[8,192,128]{2,1,0:T(8,128)(2,1)}, bf16[8,192,128]{2,1,0:T(8,128)(2,1)}, u32[]{:S(2)}, u32[]{:S(2)}) collective-permute-start(bf16[8,192,128]{2,1,0:T(8,128)(2,1)} %get-tuple-element.121), channel_id=1, source_target_pairs={{0,19},{1,18},{2,17},{3,16},{4,23},{5,22},{6,21},{7,20},{8,27},{9,... | collective-permute-start | bytes 1179656 | tf_op jit(solution)/shard_map/ppermute | solution.py:279
  223.9 56.9 %collective-permute-start.25 = (bf16[8,192,128]{2,1,0:T(8,128)(2,1)}, bf16[8,192,128]{2,1,0:T(8,128)(2,1)}, u32[]{:S(2)}, u32[]{:S(2)}) collective-permute-start(bf16[8,192,128]{2,1,0:T(8,128)(2,1)} %get-tuple-element.122), channel_id=1, source_target_pairs={{0,5},{1,4},{2,7},{3,6},{4,1},{5,0},{6,3},{7,2},{8,13},{9,12},{10,... | collective-permute-start | bytes 1179656 | tf_op jit(solution)/shard_map/ppermute | solution.py:279
  225.6 77.5 %collective-permute-start.26 = (bf16[8,192,128]{2,1,0:T(8,128)(2,1)}, bf16[8,192,128]{2,1,0:T(8,128)(2,1)}, u32[]{:S(2)}, u32[]{:S(2)}) collective-permute-start(bf16[8,192,128]{2,1,0:T(8,128)(2,1)} %get-tuple-element.123), channel_id=1, source_target_pairs={{0,20},{1,21},{2,22},{3,23},{4,16},{5,17},{6,18},{7,19},{8,28},{9,... | collective-permute-start | bytes 1179656 | tf_op jit(solution)/shard_map/ppermute | solution.py:279
  235.0 80.6 %collective-permute-start.27 = (bf16[8,192,128]{2,1,0:T(8,128)(2,1)}, bf16[8,192,128]{2,1,0:T(8,128)(2,1)}, u32[]{:S(2)}, u32[]{:S(2)}) collective-permute-start(bf16[8,192,128]{2,1,0:T(8,128)(2,1)} %get-tuple-element.124), channel_id=1, source_target_pairs={{0,28},{1,29},{2,30},{3,31},{4,24},{5,25},{6,26},{7,27},{8,20},{9,... | collective-permute-start | bytes 1179656 | tf_op jit(solution)/shard_map/ppermute | solution.py:279
  272.6 88.2 %collective-permute-start.4 = (bf16[8,192,128]{2,1,0:T(8,128)(2,1)}, bf16[8,192,128]{2,1,0:T(8,128)(2,1)}, u32[]{:S(2)}, u32[]{:S(2)}) collective-permute-start(bf16[8,192,128]{2,1,0:T(8,128)(2,1)} %get-tuple-element.101), channel_id=1, source_target_pairs={{0,8},{1,9},{2,10},{3,11},{4,12},{5,13},{6,14},{7,15},{8,0},{9,1},... | collective-permute-start | bytes 1179656 | tf_op jit(solution)/shard_map/ppermute | solution.py:279
  272.6 88.2 %collective-permute-start.5 = (bf16[8,192,128]{2,1,0:T(8,128)(2,1)}, bf16[8,192,128]{2,1,0:T(8,128)(2,1)}, u32[]{:S(2)}, u32[]{:S(2)}) collective-permute-start(bf16[8,192,128]{2,1,0:T(8,128)(2,1)} %get-tuple-element.102), channel_id=1, source_target_pairs={{0,10},{1,11},{2,8},{3,9},{4,14},{5,15},{6,12},{7,13},{8,2},{9,3},... | collective-permute-start | bytes 1179656 | tf_op jit(solution)/shard_map/ppermute | solution.py:279
  280.8 39.3 %collective-permute-start.28 = (bf16[8,192,128]{2,1,0:T(8,128)(2,1)}, bf16[8,192,128]{2,1,0:T(8,128)(2,1)}, u32[]{:S(2)}, u32[]{:S(2)}) collective-permute-start(bf16[8,192,128]{2,1,0:T(8,128)(2,1)} %get-tuple-element.125), channel_id=1, source_target_pairs={{0,29},{1,28},{2,31},{3,30},{4,25},{5,24},{6,27},{7,26},{8,21},{9,... | collective-permute-start | bytes 1179656 | tf_op jit(solution)/shard_map/ppermute | solution.py:279
  303.2 29.3 %collective-permute-start.29 = (bf16[8,192,128]{2,1,0:T(8,128)(2,1)}, bf16[8,192,128]{2,1,0:T(8,128)(2,1)}, u32[]{:S(2)}, u32[]{:S(2)}) collective-permute-start(bf16[8,192,128]{2,1,0:T(8,128)(2,1)} %get-tuple-element.126), channel_id=1, source_target_pairs={{0,21},{1,20},{2,23},{3,22},{4,17},{5,16},{6,19},{7,18},{8,29},{9,... | collective-permute-start | bytes 1179656 | tf_op jit(solution)/shard_map/ppermute | solution.py:279
  315.6 48.6 %collective-permute-start.36 = (bf16[8,192,128]{2,1,0:T(8,128)(2,1)}, bf16[8,192,128]{2,1,0:T(8,128)(2,1)S(1)}, u32[]{:S(2)}, u32[]{:S(2)}) collective-permute-start(bf16[8,192,128]{2,1,0:T(8,128)(2,1)} %get-tuple-element.151), channel_id=1, source_target_pairs={{0,6},{1,7},{2,4},{3,5},{4,2},{5,3},{6,0},{7,1},{8,14},{9,15},{10,... | collective-permute-start | bytes 1179656 | tf_op jit(solution)/shard_map/ppermute | solution.py:279
  320.1 43.0 %collective-permute-start.34 = (f32[4,128]{1,0:T(4,128)S(1)}, f32[4,128]{1,0:T(4,128)S(1)}, u32[]{:S(2)}, u32[]{:S(2)}) collective-permute-start(f32[4,128]{1,0:T(4,128)S(1)} %slice_reduce_fusion), channel_id=1, source_target_pairs={{0,1},{1,2},{2,3},{3,4},{4,5},{5,6},{6,7},{7,0},{8,9},{9,10},{10,1... | collective-permute-start | bytes 6152 | tf_op jit(solution)/shard_map/ppermute | solution.py:26
  332.5 30.6 %collective-permute-start.35 = (f32[4,64]{1,0:T(4,128)S(1)}, f32[4,64]{1,0:T(4,128)S(1)}, u32[]{:S(2)}, u32[]{:S(2)}) collective-permute-start(f32[4,64]{1,0:T(4,128)S(1)} %bitcast.82), channel_id=1, source_target_pairs={{0,8},{8,16},{16,24},{24,0},{1,9},{9,17},{17,25},{25,1},{2,10},{10... | collective-permute-start | bytes 3080 | tf_op jit(solution)/shard_map/ppermute | solution.py:26
  (30 other events, 2224.7 us)
